TPU v7x, 32 devices: a whole 2x2x4 slice. The times are simulated.
32 devices in a mesh: lat: 4 (over y, x), lon: 8 (over z, core).
Axes of the slice: x: 2, y: 2, z: 4, core: 2. Of those that a mesh axis runs over, the one named last changes fastest.
Arguments:
- adjoint_in: float32 [4, 79, 32, 1024], P(None, None, 'lat', 'lon'), may hold values from -6 to 6
- fractions: bfloat16 [4, 4, 79, 32, 1024], P(None, None, None, 'lat', 'lon'), may hold values from 0 to 0.95, as said below
- profiles: bfloat16 [2, 79, 32, 1024], P(None, None, 'lat', 'lon'), may hold values from 0.099609375 to 1
- kernel: bfloat16 [79, 79], replicated, may hold values from -0.625 to 0.625
- obs_weights: bfloat16 [79, 32768], P(None, ('lat', 'lon')), may hold values from 0.099609375 to 1.5
- obs_resid: bfloat16 [4, 32768], P(None, ('lat', 'lon')), may hold values from -5 to 5
- obs_cols: int32 [32768], P(('lat', 'lon')), may hold values from 0 to 1023
- obs_owner: int32 [4096, 1], P(('lat', 'lon')), may hold values from 0 to 31; in each aligned block of 128 rows (0 to 127, 128 to 255, ...) at most 6 rows name the same one
- obs_count: int32 [4096], P(('lat', 'lon')), may hold values from 5 to 8
- lat_matrix: bfloat16 [32, 32], replicated, as said below
- lon_matrix: bfloat16 [1024, 1024], P('lon'), as said below
Outputs:
- adjoint_out: float32 [4, 79, 32, 1024], P(None, None, 'lat', 'lon')
- smoothed_gradient: float32 [4, 32, 1024], P(None, 'lat', 'lon')
Inputs may be any that keep to these rules, and one draw needn't show every extreme that they name: `fractions`: fractions are nonnegative and the four of one cell and step sum to at most 0.95. `obs_owner`: owners are numbered as lat index times 8 plus lon index. Among the blocks of one device at most 6 share an owner. `obs_cols`: A tile's columns are numbered row by row: row within the tile times 128 plus column within the tile. The first obs_count slots of a block are valid, the others are padding. `lat_matrix`: Symmetric. `lon_matrix`: Symmetric.
All inputs are finite; a program needn't handle non-finite values.
Results may differ from a plain program's by a relative error of at most 0.0041.
Values may be sent and summed in bfloat16 or wider, within the bound.
No kernel may reach another device: no remote copies, remote signals or barrier semaphores. Data moves between devices by JAX's collectives and lax.ppermute only.
A program may use at most 192 MiB of HBM per device.

v0:
```python
import jax
import jax.numpy as jnp
from jax import lax
from jax.sharding import PartitionSpec as P

STEPS = 4
CAPACITY = 6


def extended(cells, sides, width, closed):
    for axis, dim in sides:
        count = lax.axis_size(axis)
        ends = count if closed else count - 1
        head = lax.slice_in_dim(cells, 0, width, axis=dim)
        tail = lax.slice_in_dim(cells, cells.shape[dim] - width, cells.shape[dim], axis=dim)
        cells = jnp.concatenate(
            [
                lax.ppermute(tail, axis, [(i, (i + 1) % count) for i in range(ends)]),
                cells,
                lax.ppermute(head, axis, [((i + 1) % count, i) for i in range(ends)]),
            ],
            axis=dim,
        )
    return cells


def convect(adjoint, kernel, entrain, detrain):
    lowered = (detrain * adjoint).astype(jnp.bfloat16)
    mixing = jnp.einsum("kj,tkyx->tjyx", kernel, lowered, preferred_element_type=jnp.float32)
    return adjoint + entrain * mixing


def combine_sides(field_in, north_side, south_side, east_side, west_side, fraction):
    remain = 1.0 - fraction[0] - fraction[1] - fraction[2] - fraction[3]
    return (
        remain * field_in
        + fraction[0] * east_side
        + fraction[1] * west_side
        + fraction[2] * north_side
        + fraction[3] * south_side
    )


def transport_rim(field_in, fraction):
    lat_ext = extended(field_in, (("lat", 2),), 1, False)
    lon_ext = extended(field_in, (("lon", 3),), 1, True)
    return combine_sides(
        field_in,
        lat_ext[:, :, 2:],
        lat_ext[:, :, :-2],
        lon_ext[..., 2:],
        lon_ext[..., :-2],
        fraction,
    )


def route_forcing(
    obs_weights, obs_resid, obs_cols, obs_owner, obs_count, tracers, levels, lat_rows, lon_cols
):
    cell_count = lat_rows * lon_cols
    devices = lax.axis_size(("lat", "lon"))
    blocks = obs_count.shape[0]
    slot_count = obs_cols.shape[0] // blocks
    owner_device = obs_owner[:, 0]
    block_order = jnp.arange(blocks, dtype=jnp.int32)
    earlier = (owner_device[None, :] == owner_device[:, None]) & (
        block_order[None, :] < block_order[:, None]
    )
    block_rank = jnp.sum(earlier.astype(jnp.int32), axis=1)
    target = owner_device * CAPACITY + block_rank
    buffer_slots = devices * CAPACITY
    source = jnp.full((buffer_slots,), blocks, jnp.int32).at[target].set(block_order)
    filled = source < blocks
    picked = jnp.minimum(source, blocks - 1)
    live_count = jnp.where(filled, obs_count[picked], 0)
    weights = obs_weights.reshape(levels, blocks, slot_count)[:, picked, :].reshape(
        levels, buffer_slots * slot_count
    )
    residual = obs_resid.reshape(tracers, blocks, slot_count)[:, picked, :].reshape(
        tracers, buffer_slots * slot_count
    )
    slot_index = jnp.arange(slot_count, dtype=jnp.int32)[None, :]
    columns = obs_cols.reshape(blocks, slot_count)[picked]
    columns = jnp.where(slot_index < live_count[:, None], columns, cell_count).reshape(
        1, buffer_slots * slot_count
    )
    weights, residual, columns = (
        lax.all_to_all(weights, ("lat", "lon"), split_axis=1, concat_axis=1, tiled=True),
        lax.all_to_all(residual, ("lat", "lon"), split_axis=1, concat_axis=1, tiled=True),
        lax.all_to_all(columns, ("lat", "lon"), split_axis=1, concat_axis=1, tiled=True),
    )
    cell_iota = jnp.arange(cell_count, dtype=jnp.int32)[None, :]
    selector = (columns[0][:, None] == cell_iota).astype(jnp.bfloat16)
    per_tracer = []
    for tracer_index in range(tracers):
        scaled_sel = residual[tracer_index][:, None] * selector
        per_tracer.append(jnp.dot(weights, scaled_sel, preferred_element_type=jnp.float32))
    forcing = jnp.stack(per_tracer, axis=0)
    return forcing.reshape(tracers, levels, lat_rows, lon_cols)


def shards(
    adjoint_in,
    fractions,
    profiles,
    kernel,
    obs_weights,
    obs_resid,
    obs_cols,
    obs_owner,
    obs_count,
    lat_matrix,
    lon_matrix,
):
    tracers, levels, lat_rows, lon_cols = adjoint_in.shape
    forcing = route_forcing(
        obs_weights, obs_resid, obs_cols, obs_owner, obs_count, tracers, levels, lat_rows, lon_cols
    )
    surface = jnp.zeros((tracers, lat_rows, lon_cols), jnp.float32)
    entrain = profiles[0].astype(jnp.float32)
    detrain = profiles[1].astype(jnp.float32)
    adjoint = adjoint_in
    for step_index in range(STEPS - 1, -1, -1):
        fraction = fractions[step_index].astype(jnp.float32)
        adjoint = transport_rim(convect(adjoint, kernel, entrain, detrain), fraction)
        if step_index == 0:
            adjoint = adjoint + forcing
        surface = surface + adjoint[:, 0]
    lat_start = lax.axis_index("lat") * lat_rows
    flattened = surface.astype(jnp.bfloat16).reshape(tracers * lat_rows, lon_cols)
    submatrix = lon_matrix
    across = lax.dot_general(
        lax.all_gather(flattened, "lon", axis=1, tiled=True),
        submatrix,
        (((1,), (1,)), ((), ())),
        preferred_element_type=jnp.float32,
    )
    lat_major = (
        across.astype(jnp.bfloat16)
        .reshape(tracers, lat_rows, lon_cols)
        .transpose(1, 0, 2)
        .reshape(lat_rows, tracers * lon_cols)
    )
    own_rows = lax.dynamic_slice_in_dim(lat_matrix, lat_start, lat_rows, 0)
    submatrix = own_rows
    smoothed = jnp.dot(
        submatrix,
        lax.all_gather(lat_major, "lat", axis=0, tiled=True),
        preferred_element_type=jnp.float32,
    )
    smoothed_gradient = smoothed.reshape(lat_rows, tracers, lon_cols).transpose(1, 0, 2)
    return (adjoint, smoothed_gradient)


def solution(mesh):
    placed = (
        P(None, None, "lat", "lon"),
        P(None, None, None, "lat", "lon"),
        P(None, None, "lat", "lon"),
        P(),
        P(None, ("lat", "lon")),
        P(None, ("lat", "lon")),
        P(("lat", "lon")),
        P(("lat", "lon"), None),
        P(("lat", "lon")),
        P(),
        P("lon", None),
    )
    return jax.shard_map(
        shards,
        mesh=mesh,
        in_specs=placed,
        out_specs=(P(None, None, "lat", "lon"), P(None, "lat", "lon")),
        check_vma=False,
    )
```

profile of v0, /device:TPU:0, one launch (start us, length us, event | category | flops | bytes accessed | tf_op | source)
XLA Modules:
  0.0 185.8 jit_solution(6507654934706488901)
XLA Ops:
  0.7 1.1 bitcast_convert_fusion.1
  2.7 1.5 fusion.92
  4.3 2.4 %copy.202 = f32[4,79,8,1]{1,2,3,0:T(8,128)} copy(f32[4,79,8,1]{3,1,2,0:T(8,128)} %get-tuple-element.32) | data formatting | bytes 20224 | tf_op jit(solution)/shard_map/slice | solution.py:14
  6.7 4.5 %collective-permute-start = (f32[4,79,8,1]{1,2,3,0:T(8,128)}, f32[4,79,8,1]{1,2,3,0:T(8,128)}, u32[]{:S(2)}, u32[]{:S(2)}) collective-permute-start(f32[4,79,8,1]{1,2,3,0:T(8,128)} %copy.202), channel_id=1, source_target_pairs={{1,0},{2,1},{3,2},{4,3},{5,4},{6,5},{7,6},{0,7},{9,8},{10,9},{11,1... | collective-permute-start | bytes 30344 | tf_op jit(solution)/shard_map/ppermute | solution.py:20
  11.2 1.1 copy.205
  13.0 1.3 collective-permute-start.2
  14.3 5.2 %collective-permute-start.3 = (f32[4,79,1,128]{3,1,2,0:T(8,128)}, f32[4,79,1,128]{3,1,2,0:T(8,128)}, u32[]{:S(2)}, u32[]{:S(2)}) collective-permute-start(f32[4,79,1,128]{3,1,2,0:T(8,128)} %get-tuple-element.35), channel_id=1, source_target_pairs={{0,8},{8,16},{16,24},{1,9},{9,17},{17,25},{2,10},{10,18},{18,26},{... | collective-permute-start | bytes 485384 | tf_op jit(solution)/shard_map/ppermute | solution.py:18
  19.7 1.0 scatter_custom_fusion
  20.7 1.6 gather_fusion.1
  24.2 4.5 %all-to-all-start.1 = ((s32[1,32,48]{2,0,1:T(1,128)}), s32[1,32,48]{2,0,1:T(1,128)S(1)}, u32[]{:S(2)}, u32[]{:S(2)}) async-start(s32[1,32,48]{2,0,1:T(1,128)} %bitcast.39), calls=%async_computation.1 | async-start | bytes 32768 | tf_op jit(solution)/shard_map/all_to_all | solution.py:90
  28.7 2.0 %slice_convert_fusion.3 = (f32[1,4,79,8,128]{4,3,2,1,0:T(8,128)S(1)}, f32[1,4,79,8,128]{4,3,2,1,0:T(8,128)S(1)}, f32[1,4,79,8,128]{4,3,2,1,0:T(8,128)S(1)}, f32[1,4,79,8,128]{4,3,2,1,0:T(8,128)S(1)}) fusion(bf16[4,4,79,8,128]{4,3,2,1,0:T(8,128)(2,1)} %param.12), kind=kLoop, calls=%fused_computation.109 | loop fusion | flops 1294336 | bytes 7766016 | tf_op jit(solution)/shard_map/convert_element_type | solution.py:124
  31.0 1.0 subtract_bitcast_fusion.2
  34.9 0.8 copy.207
  44.7 1.5 gather_fusion.3
  46.3 1.0 copy.241
  48.0 1.1 copy.236
  49.1 1.5 gather_fusion
  50.6 1.8 copy.192
  52.3 1.8 copy.228
  54.1 0.8 copy.231
  56.5 1.3 copy.203
  57.8 2.4 %copy.206 = f32[4,79,8,1]{3,1,2,0:T(8,128)} copy(f32[4,79,8,1]{1,2,3,0:T(8,128)} %collective-permute-done.1) | data formatting | bytes 20224 | tf_op jit(solution)/shard_map/ppermute | solution.py:18
  60.2 6.0 %all-to-all-start.2 = ((bf16[4,32,48]{2,0,1:T(4,128)(2,1)}), bf16[4,32,48]{2,0,1:T(4,128)(2,1)}, u32[]{:S(2)}, u32[]{:S(2)}) async-start(bf16[4,32,48]{2,0,1:T(4,128)(2,1)} %copy.242), calls=%async_computation.2 | async-start | bytes 65536 | tf_op jit(solution)/shard_map/all_to_all | solution.py:89
  66.7 1.3 reduce.11
  67.9 1.4 eq.65
  69.3 3.0 %fusion.54 = f32[4,79,8,128]{3,1,2,0:T(8,128)S(1)} fusion(f32[4,79,8,128]{3,1,2,0:T(8,128)S(1)} %fusion.27, f32[4,79,1,128]{3,1,2,0:T(8,128)} %collective-permute-done.3, f32[4,79,1,128]{3,1,2,0:T(8,128)} %collective-permute-done.2, f32[4,79,8,1]{3,1,2,0:T(8,128)} %copy.206, f32[4,79,8,1]{3,1,2,0:T(8,128)S(1)} %copy.203, f32[79,8,128]{2,0,1:T(8,128)} %copy.208, ...), kind=kLoop, calls=%fused_computation.80 | loop fusion | flops 4206592 | bytes 4550400 | tf_op jit(solution)/shard_map/add | solution.py:36
  74.2 1.3 collective-permute-start.6
  75.5 5.2 %collective-permute-start.7 = (f32[4,79,1,128]{3,1,2,0:T(8,128)}, f32[4,79,1,128]{3,1,2,0:T(8,128)}, u32[]{:S(2)}, u32[]{:S(2)}) collective-permute-start(f32[4,79,1,128]{3,1,2,0:T(8,128)} %get-tuple-element.31), channel_id=1, source_target_pairs={{0,8},{8,16},{16,24},{1,9},{9,17},{17,25},{2,10},{10,18},{18,26},{... | collective-permute-start | bytes 485384 | tf_op jit(solution)/shard_map/ppermute | solution.py:18
  80.7 1.6 fusion.90
  82.2 1.8 copy.211
  84.0 2.7 %collective-permute-start.4 = (f32[4,79,8,1]{1,2,3,0:T(8,128)S(1)}, f32[4,79,8,1]{1,2,3,0:T(8,128)}, u32[]{:S(2)}, u32[]{:S(2)}) collective-permute-start(f32[4,79,8,1]{1,2,3,0:T(8,128)S(1)} %copy.211), channel_id=1, source_target_pairs={{1,0},{2,1},{3,2},{4,3},{5,4},{6,5},{7,6},{0,7},{9,8},{10,9},{11,1... | collective-permute-start | bytes 30344 | tf_op jit(solution)/shard_map/ppermute | solution.py:20
  86.7 1.1 copy.214
  87.8 5.4 %all-to-all-start = ((bf16[79,32,48]{0,2,1:T(8,128)(2,1)}), bf16[79,32,48]{0,2,1:T(8,128)(2,1)}, u32[]{:S(2)}, u32[]{:S(2)}) async-start(bf16[79,32,48]{0,2,1:T(8,128)(2,1)} %bitcast.35), calls=%async_computation | async-start | bytes 786432 | tf_op jit(solution)/shard_map/all_to_all | solution.py:88
  93.2 1.1 slice_reduce_fusion.3
  97.0 1.3 copy.212
  98.3 2.4 %copy.215 = f32[4,79,8,1]{3,1,2,0:T(8,128)} copy(f32[4,79,8,1]{1,2,3,0:T(8,128)} %collective-permute-done.5) | data formatting | bytes 20224 | tf_op jit(solution)/shard_map/ppermute | solution.py:18
  100.7 3.0 %fusion.46 = f32[4,79,8,128]{3,1,2,0:T(8,128)S(1)} fusion(f32[4,79,8,128]{3,1,2,0:T(8,128)S(1)} %fusion.25, f32[4,79,1,128]{3,1,2,0:T(8,128)} %collective-permute-done.7, f32[4,79,1,128]{3,1,2,0:T(8,128)} %collective-permute-done.6, f32[4,79,8,1]{3,1,2,0:T(8,128)} %copy.215, f32[4,79,8,1]{3,1,2,0:T(8,128)S(1)} %copy.212, f32[79,8,128]{2,0,1:T(8,128)} %copy.217, ...), kind=kLoop, calls=%fused_computation.68 | loop fusion | flops 4206592 | bytes 4550400 | tf_op jit(solution)/shard_map/add | solution.py:36
  104.8 1.6 fusion.88
  106.4 1.8 copy.220
  108.1 3.1 %collective-permute-start.8 = (f32[4,79,8,1]{1,2,3,0:T(8,128)S(1)}, f32[4,79,8,1]{1,2,3,0:T(8,128)}, u32[]{:S(2)}, u32[]{:S(2)}) collective-permute-start(f32[4,79,8,1]{1,2,3,0:T(8,128)S(1)} %copy.220), channel_id=1, source_target_pairs={{1,0},{2,1},{3,2},{4,3},{5,4},{6,5},{7,6},{0,7},{9,8},{10,9},{11,1... | collective-permute-start | bytes 30344 | tf_op jit(solution)/shard_map/ppermute | solution.py:20
  111.3 1.1 copy.223
  113.1 1.3 collective-permute-start.10
  114.4 5.2 %collective-permute-start.11 = (f32[4,79,1,128]{3,1,2,0:T(8,128)}, f32[4,79,1,128]{3,1,2,0:T(8,128)}, u32[]{:S(2)}, u32[]{:S(2)}) collective-permute-start(f32[4,79,1,128]{3,1,2,0:T(8,128)} %get-tuple-element.27), channel_id=1, source_target_pairs={{0,8},{8,16},{16,24},{1,9},{9,17},{17,25},{2,10},{10,18},{18,26},{... | collective-permute-start | bytes 485384 | tf_op jit(solution)/shard_map/ppermute | solution.py:18
  119.6 1.3 copy.221
  120.9 2.4 %copy.224 = f32[4,79,8,1]{3,1,2,0:T(8,128)} copy(f32[4,79,8,1]{1,2,3,0:T(8,128)} %collective-permute-done.9) | data formatting | bytes 20224 | tf_op jit(solution)/shard_map/ppermute | solution.py:18
  123.3 2.9 %fusion.62 = f32[1,79,8,128]{3,1,2,0:T(8,128)} fusion(bf16[79,1536,1]{0,1,2:T(8,128)(2,1)} %bitcast.37, s32[8,128]{1,0:T(8,128)} %multiply_add_fusion, s32[1536]{0:T(1024)} %eq.65, bf16[1536]{0:T(1024)(128)(2,1)} %mul.397), kind=kOutput, calls=%fused_computation.95 | convolution fusion | flops 251658240 | bytes 579584 | tf_op jit(solution)/shard_map/dot_general | solution.py:97
  126.2 2.9 %fusion.63 = f32[1,79,8,128]{3,1,2,0:T(8,128)} fusion(bf16[79,1536,1]{0,1,2:T(8,128)(2,1)} %bitcast.37, s32[8,128]{1,0:T(8,128)S(1)} %copy-done.25, s32[1536]{0:T(1024)S(1)} %copy-done.19, bf16[1536]{0:T(1024)(128)(2,1)S(1)} %copy-done.23), kind=kOutput, calls=%fused_computation.96 | convolution fusion | flops 251658240 | bytes 579584 | tf_op jit(solution)/shard_map/dot_general | solution.py:97
  129.2 3.0 %fusion.64 = f32[1,79,8,128]{3,1,2,0:T(8,128)} fusion(bf16[79,1536,1]{0,1,2:T(8,128)(2,1)} %bitcast.37, s32[8,128]{1,0:T(8,128)S(1)} %copy-done.25, s32[1536]{0:T(1024)S(1)} %copy-done.19, bf16[1536]{0:T(1024)(128)(2,1)S(1)} %copy-done.24), kind=kOutput, calls=%fused_computation.97 | convolution fusion | flops 251658240 | bytes 579584 | tf_op jit(solution)/shard_map/dot_general | solution.py:97
  132.3 2.1 %fusion.38 = f32[4,79,8,128]{3,1,2,0:T(8,128)S(1)} fusion(f32[4,79,8,128]{3,1,2,0:T(8,128)S(1)} %fusion.23, f32[4,79,1,128]{3,1,2,0:T(8,128)} %collective-permute-done.11, f32[4,79,1,128]{3,1,2,0:T(8,128)} %collective-permute-done.10, f32[4,79,8,1]{3,1,2,0:T(8,128)S(1)} %copy-done.5, f32[4,79,8,1]{3,1,2,0:T(8,128)S(1)} %copy.221, ...), kind=kLoop, calls=%fused_computation.56 | loop fusion | flops 4206592 | bytes 4550400 | tf_op jit(solution)/shard_map/add | solution.py:36
  135.5 1.6 fusion.86
  137.8 1.8 copy.229
  139.6 3.0 %collective-permute-start.12 = (f32[4,79,8,1]{1,2,3,0:T(8,128)S(1)}, f32[4,79,8,1]{1,2,3,0:T(8,128)}, u32[]{:S(2)}, u32[]{:S(2)}) collective-permute-start(f32[4,79,8,1]{1,2,3,0:T(8,128)S(1)} %copy.229), channel_id=1, source_target_pairs={{1,0},{2,1},{3,2},{4,3},{5,4},{6,5},{7,6},{0,7},{9,8},{10,9},{11,1... | collective-permute-start | bytes 30344 | tf_op jit(solution)/shard_map/ppermute | solution.py:20
  142.6 1.1 copy.232
  143.7 1.3 collective-permute-start.14
  145.0 5.2 %collective-permute-start.15 = (f32[4,79,1,128]{3,1,2,0:T(8,128)}, f32[4,79,1,128]{3,1,2,0:T(8,128)}, u32[]{:S(2)}, u32[]{:S(2)}) collective-permute-start(f32[4,79,1,128]{3,1,2,0:T(8,128)} %get-tuple-element.23), channel_id=1, source_target_pairs={{0,8},{8,16},{16,24},{1,9},{9,17},{17,25},{2,10},{10,18},{18,26},{... | collective-permute-start | bytes 485384 | tf_op jit(solution)/shard_map/ppermute | solution.py:18
  150.2 2.9 %fusion.65 = f32[1,79,8,128]{3,1,2,0:T(8,128)} fusion(bf16[79,1536,1]{0,1,2:T(8,128)(2,1)} %bitcast.37, s32[8,128]{1,0:T(8,128)S(1)} %copy-done.26, s32[1536]{0:T(1024)S(1)} %copy-done.20, bf16[1536]{0:T(1024)(128)(2,1)S(1)} %copy-done.22), kind=kOutput, calls=%fused_computation.98 | convolution fusion | flops 251658240 | bytes 579584 | tf_op jit(solution)/shard_map/dot_general | solution.py:97
  153.1 1.3 copy.230
  154.5 2.4 %copy.233 = f32[4,79,8,1]{3,1,2,0:T(8,128)} copy(f32[4,79,8,1]{1,2,3,0:T(8,128)} %collective-permute-done.13) | data formatting | bytes 20224 | tf_op jit(solution)/shard_map/ppermute | solution.py:18
  156.9 3.2 %fusion.30 = f32[4,79,8,128]{3,1,2,0:T(8,128)S(1)} fusion(f32[4,79,8,128]{3,1,2,0:T(8,128)S(1)} %fusion.21, f32[4,79,1,128]{3,1,2,0:T(8,128)} %collective-permute-done.15, f32[4,79,1,128]{3,1,2,0:T(8,128)} %collective-permute-done.14, f32[4,79,8,1]{3,1,2,0:T(8,128)} %copy.233, f32[4,79,8,1]{3,1,2,0:T(8,128)S(1)} %copy.230, f32[1,79,8,128]{3,1,2,0:T(8,128)} %fusion.62, ...), kind=kLoop, calls=%fused_computation.44 | loop fusion | flops 5500928 | bytes 5844736 | tf_op jit(solution)/shard_map/add | solution.py:127
  160.1 1.1 fusion.76
  161.2 1.4 copy.247
  162.6 12.7 %all_gather.6 = bf16[32,1024]{1,0:T(8,128)(2,1)S(1)} all-gather(bf16[32,128]{1,0:T(8,128)(2,1)S(1)} %bitcast.134), channel_id=1, replica_groups=mesh['lat'=4,'lon'=8] {'lon'}, dimensions={1}, use_global_device_ids=true | all-gather | bytes 73728 | tf_op jit(solution)/shard_map/all_gather | solution.py:133
  175.5 8.9 %all_gather.7 = bf16[32,512]{1,0:T(8,128)(2,1)S(1)} all-gather(bf16[8,512]{1,0:T(8,128)(2,1)S(1)} %fusion.66), channel_id=1, replica_groups=mesh['lat'=4,'lon'=8] {'lat'}, dimensions={0}, use_global_device_ids=true | all-gather | bytes 40960 | tf_op jit(solution)/shard_map/all_gather | solution.py:148
  184.4 1.4 convolution_bitcast_fusion.4
  (134 shorter events, 27.2 us)
Async XLA Ops:
  0.6 174.7 %copy-start = (bf16[128,1024]{1,0:T(8,128)(2,1)S(1)}, bf16[128,1024]{1,0:T(8,128)(2,1)}, u32[]{:S(2)}) copy-start(bf16[128,1024]{1,0:T(8,128)(2,1)} %param.21) | copy-start | bytes 786436
  0.6 1.5 copy-start.6
  0.7 1.5 copy-start.14
  6.7 12.9 %copy-start.27 = (s32[128,1]{0,1:T(1,128)S(1)}, s32[128,1]{0,1:T(1,128)}, u32[]{:S(2)}) copy-start(s32[128,1]{0,1:T(1,128)} %param.18) | copy-start | bytes 1540
  6.7 14.1 %copy-start.1 = (s32[128]{0:T(128)S(1)}, s32[128]{0:T(128)}, u32[]{:S(2)}) copy-start(s32[128]{0:T(128)} %param.19) | copy-start | bytes 1540
  6.7 49.9 %collective-permute-start = (f32[4,79,8,1]{1,2,3,0:T(8,128)}, f32[4,79,8,1]{1,2,3,0:T(8,128)}, u32[]{:S(2)}, u32[]{:S(2)}) collective-permute-start(f32[4,79,8,1]{1,2,3,0:T(8,128)} %copy.202), channel_id=1, source_target_pairs={{1,0},{2,1},{3,2},{4,3},{5,4},{6,5},{7,6},{0,7},{9,8},{10,9},{11,1... | collective-permute-start | bytes 30344 | tf_op jit(solution)/shard_map/ppermute | solution.py:20
  11.2 11.4 %copy-start.21 = (s32[1024]{0:T(1024)S(1)}, s32[1024]{0:T(1024)}, u32[]{:S(2)}) copy-start(s32[1024]{0:T(1024)} %param.17) | copy-start | bytes 12292
  12.3 45.5 %collective-permute-start.1 = (f32[4,79,8,1]{1,2,3,0:T(8,128)}, f32[4,79,8,1]{1,2,3,0:T(8,128)}, u32[]{:S(2)}, u32[]{:S(2)}) collective-permute-start(f32[4,79,8,1]{1,2,3,0:T(8,128)} %copy.205), channel_id=1, source_target_pairs={{0,1},{1,2},{2,3},{3,4},{4,5},{5,6},{6,7},{7,0},{8,9},{9,10},{10,1... | collective-permute-start | bytes 30344 | tf_op jit(solution)/shard_map/ppermute | solution.py:18
  13.0 56.3 %collective-permute-start.2 = (f32[4,79,1,128]{3,1,2,0:T(8,128)}, f32[4,79,1,128]{3,1,2,0:T(8,128)}, u32[]{:S(2)}, u32[]{:S(2)}) collective-permute-start(f32[4,79,1,128]{3,1,2,0:T(8,128)} %get-tuple-element.34), channel_id=1, source_target_pairs={{8,0},{16,8},{24,16},{9,1},{17,9},{25,17},{10,2},{18,10},{26,18},{... | collective-permute-start | bytes 485384 | tf_op jit(solution)/shard_map/ppermute | solution.py:20
  14.3 55.0 %collective-permute-start.3 = (f32[4,79,1,128]{3,1,2,0:T(8,128)}, f32[4,79,1,128]{3,1,2,0:T(8,128)}, u32[]{:S(2)}, u32[]{:S(2)}) collective-permute-start(f32[4,79,1,128]{3,1,2,0:T(8,128)} %get-tuple-element.35), channel_id=1, source_target_pairs={{0,8},{8,16},{16,24},{1,9},{9,17},{17,25},{2,10},{10,18},{18,26},{... | collective-permute-start | bytes 485384 | tf_op jit(solution)/shard_map/ppermute | solution.py:18
  24.2 36.0 %all-to-all-start.1 = ((s32[1,32,48]{2,0,1:T(1,128)}), s32[1,32,48]{2,0,1:T(1,128)S(1)}, u32[]{:S(2)}, u32[]{:S(2)}) async-start(s32[1,32,48]{2,0,1:T(1,128)} %bitcast.39), calls=%async_computation.1 | async-start | bytes 32768 | tf_op jit(solution)/shard_map/all_to_all | solution.py:90
  41.3 3.1 %copy-start.18 = (bf16[4,1024]{1,0:T(4,128)(2,1)S(1)}, bf16[4,1024]{1,0:T(4,128)(2,1)}, u32[]{:S(2)}) copy-start(bf16[4,1024]{1,0:T(4,128)(2,1)} %param.16) | copy-start | bytes 24580
  60.2 27.7 %all-to-all-start.2 = ((bf16[4,32,48]{2,0,1:T(4,128)(2,1)}), bf16[4,32,48]{2,0,1:T(4,128)(2,1)}, u32[]{:S(2)}, u32[]{:S(2)}) async-start(bf16[4,32,48]{2,0,1:T(4,128)(2,1)} %copy.242), calls=%async_computation.2 | async-start | bytes 65536 | tf_op jit(solution)/shard_map/all_to_all | solution.py:89
  69.3 3.0 %copy-start.15 = (bf16[79,79]{1,0:T(8,128)(2,1)S(1)}, bf16[79,79]{1,0:T(8,128)(2,1)}, u32[]{:S(2)}) copy-start(bf16[79,79]{1,0:T(8,128)(2,1)} %param.14) | copy-start | bytes 37450
  72.4 1.1 copy-start.2
  74.2 26.5 %collective-permute-start.6 = (f32[4,79,1,128]{3,1,2,0:T(8,128)}, f32[4,79,1,128]{3,1,2,0:T(8,128)}, u32[]{:S(2)}, u32[]{:S(2)}) collective-permute-start(f32[4,79,1,128]{3,1,2,0:T(8,128)} %get-tuple-element.30), channel_id=1, source_target_pairs={{8,0},{16,8},{24,16},{9,1},{17,9},{25,17},{10,2},{18,10},{26,18},{... | collective-permute-start | bytes 485384 | tf_op jit(solution)/shard_map/ppermute | solution.py:20
  75.5 25.2 %collective-permute-start.7 = (f32[4,79,1,128]{3,1,2,0:T(8,128)}, f32[4,79,1,128]{3,1,2,0:T(8,128)}, u32[]{:S(2)}, u32[]{:S(2)}) collective-permute-start(f32[4,79,1,128]{3,1,2,0:T(8,128)} %get-tuple-element.31), channel_id=1, source_target_pairs={{0,8},{8,16},{16,24},{1,9},{9,17},{17,25},{2,10},{10,18},{18,26},{... | collective-permute-start | bytes 485384 | tf_op jit(solution)/shard_map/ppermute | solution.py:18
  84.0 13.0 %collective-permute-start.4 = (f32[4,79,8,1]{1,2,3,0:T(8,128)S(1)}, f32[4,79,8,1]{1,2,3,0:T(8,128)}, u32[]{:S(2)}, u32[]{:S(2)}) collective-permute-start(f32[4,79,8,1]{1,2,3,0:T(8,128)S(1)} %copy.211), channel_id=1, source_target_pairs={{1,0},{2,1},{3,2},{4,3},{5,4},{6,5},{7,6},{0,7},{9,8},{10,9},{11,1... | collective-permute-start | bytes 30344 | tf_op jit(solution)/shard_map/ppermute | solution.py:20
  87.8 10.5 %collective-permute-start.5 = (f32[4,79,8,1]{1,2,3,0:T(8,128)}, f32[4,79,8,1]{1,2,3,0:T(8,128)}, u32[]{:S(2)}, u32[]{:S(2)}) collective-permute-start(f32[4,79,8,1]{1,2,3,0:T(8,128)} %copy.214), channel_id=1, source_target_pairs={{0,1},{1,2},{2,3},{3,4},{4,5},{5,6},{6,7},{7,0},{8,9},{9,10},{10,1... | collective-permute-start | bytes 30344 | tf_op jit(solution)/shard_map/ppermute | solution.py:18
  87.8 35.5 %all-to-all-start = ((bf16[79,32,48]{0,2,1:T(8,128)(2,1)}), bf16[79,32,48]{0,2,1:T(8,128)(2,1)}, u32[]{:S(2)}, u32[]{:S(2)}) async-start(bf16[79,32,48]{0,2,1:T(8,128)(2,1)} %bitcast.35), calls=%async_computation | async-start | bytes 786432 | tf_op jit(solution)/shard_map/all_to_all | solution.py:88
  100.7 3.0 %copy-start.16 = (bf16[79,79]{1,0:T(8,128)(2,1)S(1)}, bf16[79,79]{1,0:T(8,128)(2,1)}, u32[]{:S(2)}) copy-start(bf16[79,79]{1,0:T(8,128)(2,1)} %param.14) | copy-start | bytes 37450
  103.7 1.1 copy-start.3
  108.1 11.5 %collective-permute-start.8 = (f32[4,79,8,1]{1,2,3,0:T(8,128)S(1)}, f32[4,79,8,1]{1,2,3,0:T(8,128)}, u32[]{:S(2)}, u32[]{:S(2)}) collective-permute-start(f32[4,79,8,1]{1,2,3,0:T(8,128)S(1)} %copy.220), channel_id=1, source_target_pairs={{1,0},{2,1},{3,2},{4,3},{5,4},{6,5},{7,6},{0,7},{9,8},{10,9},{11,1... | collective-permute-start | bytes 30344 | tf_op jit(solution)/shard_map/ppermute | solution.py:20
  112.3 8.5 %collective-permute-start.9 = (f32[4,79,8,1]{1,2,3,0:T(8,128)}, f32[4,79,8,1]{1,2,3,0:T(8,128)}, u32[]{:S(2)}, u32[]{:S(2)}) collective-permute-start(f32[4,79,8,1]{1,2,3,0:T(8,128)} %copy.223), channel_id=1, source_target_pairs={{0,1},{1,2},{2,3},{3,4},{4,5},{5,6},{6,7},{7,0},{8,9},{9,10},{10,1... | collective-permute-start | bytes 30344 | tf_op jit(solution)/shard_map/ppermute | solution.py:18
  113.1 19.1 %collective-permute-start.10 = (f32[4,79,1,128]{3,1,2,0:T(8,128)}, f32[4,79,1,128]{3,1,2,0:T(8,128)}, u32[]{:S(2)}, u32[]{:S(2)}) collective-permute-start(f32[4,79,1,128]{3,1,2,0:T(8,128)} %get-tuple-element.26), channel_id=1, source_target_pairs={{8,0},{16,8},{24,16},{9,1},{17,9},{25,17},{10,2},{18,10},{26,18},{... | collective-permute-start | bytes 485384 | tf_op jit(solution)/shard_map/ppermute | solution.py:20
  114.4 17.8 %collective-permute-start.11 = (f32[4,79,1,128]{3,1,2,0:T(8,128)}, f32[4,79,1,128]{3,1,2,0:T(8,128)}, u32[]{:S(2)}, u32[]{:S(2)}) collective-permute-start(f32[4,79,1,128]{3,1,2,0:T(8,128)} %get-tuple-element.27), channel_id=1, source_target_pairs={{0,8},{8,16},{16,24},{1,9},{9,17},{17,25},{2,10},{10,18},{18,26},{... | collective-permute-start | bytes 485384 | tf_op jit(solution)/shard_map/ppermute | solution.py:18
  123.3 2.9 %copy-start.19 = (s32[1536]{0:T(1024)S(1)}, s32[1536]{0:T(1024)}, u32[]{:S(2)}) copy-start(s32[1536]{0:T(1024)} %eq.65) | copy-start | bytes 18436
  123.3 2.9 %copy-start.23 = (bf16[1536]{0:T(1024)(128)(2,1)S(1)}, bf16[1536]{0:T(1024)(128)(2,1)}, u32[]{:S(2)}) copy-start(bf16[1536]{0:T(1024)(128)(2,1)} %mul.394) | copy-start | bytes 9220
  123.3 2.9 %copy-start.25 = (s32[8,128]{1,0:T(8,128)S(1)}, s32[8,128]{1,0:T(8,128)}, u32[]{:S(2)}) copy-start(s32[8,128]{1,0:T(8,128)} %multiply_add_fusion) | copy-start | bytes 12292
  126.2 2.9 %copy-start.24 = (bf16[1536]{0:T(1024)(128)(2,1)S(1)}, bf16[1536]{0:T(1024)(128)(2,1)}, u32[]{:S(2)}) copy-start(bf16[1536]{0:T(1024)(128)(2,1)} %mul.391) | copy-start | bytes 9220
  129.1 3.1 %copy-start.5 = (f32[4,79,8,1]{3,1,2,0:T(8,128)S(1)}, f32[4,79,8,1]{3,1,2,0:T(8,128)}, u32[]{:S(2)}) copy-start(f32[4,79,8,1]{3,1,2,0:T(8,128)} %copy.224) | copy-start | bytes 30340
  129.1 3.1 %copy-start.7 = (f32[79,8,128]{2,0,1:T(8,128)S(1)}, f32[79,8,128]{2,0,1:T(8,128)}, u32[]{:S(2)}) copy-start(f32[79,8,128]{2,0,1:T(8,128)} %copy.193) | copy-start | bytes 970756
  129.1 3.1 %copy-start.8 = (f32[79,8,128]{2,0,1:T(8,128)S(1)}, f32[79,8,128]{2,0,1:T(8,128)}, u32[]{:S(2)}) copy-start(f32[79,8,128]{2,0,1:T(8,128)} %copy.219) | copy-start | bytes 970756
  129.1 3.1 %copy-start.9 = (f32[79,8,128]{2,0,1:T(8,128)S(1)}, f32[79,8,128]{2,0,1:T(8,128)}, u32[]{:S(2)}) copy-start(f32[79,8,128]{2,0,1:T(8,128)} %copy.222) | copy-start | bytes 970756
  129.1 3.1 %copy-start.10 = (f32[79,8,128]{2,0,1:T(8,128)S(1)}, f32[79,8,128]{2,0,1:T(8,128)}, u32[]{:S(2)}) copy-start(f32[79,8,128]{2,0,1:T(8,128)} %copy.225) | copy-start | bytes 970756
  129.2 3.1 %copy-start.11 = (f32[79,8,128]{2,0,1:T(8,128)S(1)}, f32[79,8,128]{2,0,1:T(8,128)}, u32[]{:S(2)}) copy-start(f32[79,8,128]{2,0,1:T(8,128)} %copy.226) | copy-start | bytes 970756
  132.2 2.2 %copy-start.17 = (bf16[79,79]{1,0:T(8,128)(2,1)S(1)}, bf16[79,79]{1,0:T(8,128)(2,1)}, u32[]{:S(2)}) copy-start(bf16[79,79]{1,0:T(8,128)(2,1)} %param.14) | copy-start | bytes 37450
  134.4 1.1 copy-start.4
  137.8 12.4 %copy-start.20 = (s32[1536]{0:T(1024)S(1)}, s32[1536]{0:T(1024)}, u32[]{:S(2)}) copy-start(s32[1536]{0:T(1024)} %eq.65) | copy-start | bytes 18436
  137.8 12.4 %copy-start.22 = (bf16[1536]{0:T(1024)(128)(2,1)S(1)}, bf16[1536]{0:T(1024)(128)(2,1)}, u32[]{:S(2)}) copy-start(bf16[1536]{0:T(1024)(128)(2,1)} %mul.388) | copy-start | bytes 9220
  137.8 12.4 %copy-start.26 = (s32[8,128]{1,0:T(8,128)S(1)}, s32[8,128]{1,0:T(8,128)}, u32[]{:S(2)}) copy-start(s32[8,128]{1,0:T(8,128)} %multiply_add_fusion) | copy-start | bytes 12292
  139.6 13.5 %collective-permute-start.12 = (f32[4,79,8,1]{1,2,3,0:T(8,128)S(1)}, f32[4,79,8,1]{1,2,3,0:T(8,128)}, u32[]{:S(2)}, u32[]{:S(2)}) collective-permute-start(f32[4,79,8,1]{1,2,3,0:T(8,128)S(1)} %copy.229), channel_id=1, source_target_pairs={{1,0},{2,1},{3,2},{4,3},{5,4},{6,5},{7,6},{0,7},{9,8},{10,9},{11,1... | collective-permute-start | bytes 30344 | tf_op jit(solution)/shard_map/ppermute | solution.py:20
  143.7 10.8 %collective-permute-start.13 = (f32[4,79,8,1]{1,2,3,0:T(8,128)}, f32[4,79,8,1]{1,2,3,0:T(8,128)}, u32[]{:S(2)}, u32[]{:S(2)}) collective-permute-start(f32[4,79,8,1]{1,2,3,0:T(8,128)} %copy.232), channel_id=1, source_target_pairs={{0,1},{1,2},{2,3},{3,4},{4,5},{5,6},{6,7},{7,0},{8,9},{9,10},{10,1... | collective-permute-start | bytes 30344 | tf_op jit(solution)/shard_map/ppermute | solution.py:18
  143.7 13.2 %collective-permute-start.14 = (f32[4,79,1,128]{3,1,2,0:T(8,128)}, f32[4,79,1,128]{3,1,2,0:T(8,128)}, u32[]{:S(2)}, u32[]{:S(2)}) collective-permute-start(f32[4,79,1,128]{3,1,2,0:T(8,128)} %get-tuple-element.22), channel_id=1, source_target_pairs={{8,0},{16,8},{24,16},{9,1},{17,9},{25,17},{10,2},{18,10},{26,18},{... | collective-permute-start | bytes 485384 | tf_op jit(solution)/shard_map/ppermute | solution.py:20
  145.0 11.9 %collective-permute-start.15 = (f32[4,79,1,128]{3,1,2,0:T(8,128)}, f32[4,79,1,128]{3,1,2,0:T(8,128)}, u32[]{:S(2)}, u32[]{:S(2)}) collective-permute-start(f32[4,79,1,128]{3,1,2,0:T(8,128)} %get-tuple-element.23), channel_id=1, source_target_pairs={{0,8},{8,16},{16,24},{1,9},{9,17},{17,25},{2,10},{10,18},{18,26},{... | collective-permute-start | bytes 485384 | tf_op jit(solution)/shard_map/ppermute | solution.py:18
  153.1 3.7 %copy-start.12 = (f32[79,8,128]{2,0,1:T(8,128)S(1)}, f32[79,8,128]{2,0,1:T(8,128)}, u32[]{:S(2)}) copy-start(f32[79,8,128]{2,0,1:T(8,128)} %copy.192) | copy-start | bytes 970756
  153.1 3.8 %copy-start.13 = (f32[79,8,128]{2,0,1:T(8,128)S(1)}, f32[79,8,128]{2,0,1:T(8,128)}, u32[]{:S(2)}) copy-start(f32[79,8,128]{2,0,1:T(8,128)} %copy.228) | copy-start | bytes 970756
where the time goes:
time: 187 us; the launch traced here: 186 us
  local copies, waits for them, and re-layouts  73 us (39%)
  starting transfers between devices  55.3 us (30%)
  blocking collectives  21.6 us (12%)
  other arithmetic  19.5 us (10%)
  matrix products  15.2 us (8%)
    ppermute x8, starting transfers between devices, extended(): lax.ppermute(tail, axis, [(i, (i + 1) % count) for i in range(ends)])  20.9 us
    ppermute x8, starting transfers between devices, extended(): lax.ppermute(head, axis, [((i + 1) % count, i) for i in range(ends)])  18.5 us
    slice x12, local copies, waits for them, and re-layouts, extended(): head = lax.slice_in_dim(cells, 0, width, axis=dim)  17 us
    all_gather x1, blocking collectives, shards(): lax.all_gather(flattened, 'lon', axis=1, tiled=True)  12.7 us
    dot_general x4, matrix products, route_forcing(): jnp.dot(weights, scaled_sel, preferred_element_type=jnp.float32)  11.7 us
    ppermute x4, local copies, waits for them, and re-layouts, extended(): lax.ppermute(tail, axis, [(i, (i + 1) % count) for i in range(ends)])  9.52 us
    all_gather x1, blocking collectives, shards(): lax.all_gather(lat_major, 'lat', axis=0, tiled=True)  8.91 us
    add x3, other arithmetic, combine_sides(): remain * field_in + fraction[0] * east_side + fraction[1] * west_side  8.15 us
  transfers between devices with their start and end apart: 19, of which 0 were waited for; matrix products, arithmetic and copies ran while one was open for 46% of the time, Pallas kernels for 0%

commit v1 on v0

v1 whole, which is shorter than its diff:
```python
import functools

import jax
import jax.numpy as jnp
from jax import lax
from jax.experimental import pallas as pl
from jax.experimental.pallas import tpu as pltpu
from jax.sharding import PartitionSpec as P

STEPS = 4
CAPACITY = 6
F32 = jnp.float32
BF16 = jnp.bfloat16
BOTH = ("lat", "lon")
LANES = 128


def iota(shape, dim):
    return lax.broadcasted_iota(jnp.int32, shape, dim)


def dot_nt(a, b):
    return lax.dot_general(a, b, (((1,), (1,)), ((), ())), preferred_element_type=F32)


def dot_tn(a, b):
    return lax.dot_general(a, b, (((0,), (0,)), ((), ())), preferred_element_type=F32)


def full(shape):
    return pl.BlockSpec(shape, lambda i: (0,) * len(shape))


def params(limit=48 << 20):
    return pltpu.CompilerParams(vmem_limit_bytes=limit)


def expand_kernel(kernel, levels, padded, rows):
    size = padded * rows
    spread = (iota((size, levels), 0) // rows == iota((size, levels), 1)).astype(BF16)
    half = dot_nt(spread, kernel).astype(BF16)
    whole = dot_nt(half, spread)
    same = iota((size, size), 0) % rows == iota((size, size), 1) % rows
    return jnp.where(same, whole, 0.0).astype(BF16)


def convect(dims, adj, low, mix, kron, profiles, mixed):
    tracers, levels, rows = dims
    mix[...] = jnp.dot(kron[...], low[...], preferred_element_type=F32)

    def body(k, carry):
        entrain = profiles[0, k].astype(F32)
        start = pl.multiple_of(k * rows, rows)
        for t in range(tracers):
            at = pl.multiple_of((t * levels + k) * rows, rows)
            mixed[pl.ds(at, rows), :] = adj[pl.ds(at, rows), :] + entrain * mix[
                pl.ds(start, rows), t * LANES : (t + 1) * LANES
            ]
        return carry

    lax.fori_loop(0, levels, body, 0)


def send_edges(dims, mixed, up, down, west, east):
    tracers, levels, rows = dims
    count = tracers * levels
    lat = lax.axis_index("lat")
    last = lax.axis_size("lat") - 1
    first_row = mixed[pl.ds(0, count, stride=rows), :]
    last_row = mixed[pl.ds(rows - 1, count, stride=rows), :]
    up[...] = jnp.where(lat < last, last_row, 0.0).astype(BF16)
    down[...] = jnp.where(lat > 0, first_row, 0.0).astype(BF16)
    lane = iota((rows, LANES), 1)
    sub = iota((rows, LANES), 0)
    pick = ((sub == 0) & (lane == 0)) | ((sub == 1) & (lane == LANES - 1))
    sides = dot_nt(pick.astype(BF16), mixed[...].astype(BF16))
    west[...] = sides[0:1]
    east[...] = sides[1:2]


def store_low(low, k2, rows, t, parts):
    low[pl.ds(pl.multiple_of(k2 * 2 * rows, 2 * rows), 2 * rows), t * LANES : (t + 1) * LANES] = jnp.concatenate(
        parts, axis=0
    ).astype(BF16)


def over_levels(levels, body):
    def pair(k2, carry):
        body(k2, (2 * k2, 2 * k2 + 1))
        return carry

    lax.fori_loop(0, levels // 2, pair, 0)
    if levels % 2:
        body(levels // 2, (levels - 1,))


def first_body(dims, kernel, profiles, adjoint, mixed, kron, up, down, west, east, low, mix):
    tracers, levels, rows = dims
    kron[...] = expand_kernel(kernel[...], levels, low.shape[0] // rows, rows)

    def body(k2, ks):
        detrains = [profiles[1, k].astype(F32) for k in ks]
        for t in range(tracers):
            parts = [
                d * adjoint[pl.ds(pl.multiple_of((t * levels + k) * rows, rows), rows), :] for d, k in zip(detrains, ks)
            ]
            store_low(low, k2, rows, t, parts if len(parts) == 2 else parts + [jnp.zeros_like(parts[0])])

    over_levels(levels, body)
    convect(dims, adjoint, low, mix, kron, profiles, mixed)
    send_edges(dims, mixed, up, down, west, east)


def unpack_halo(dims, north, south, east, west, north_scr, south_scr, sides):
    tracers, levels, rows = dims
    count = tracers * levels
    north_scr[0:count, :] = north[...].astype(F32)
    south_scr[0:count, :] = south[...].astype(F32)
    sub = iota((rows, count * rows), 0)
    got = jnp.where(sub == 0, east[...], jnp.where(sub == 1, west[...], 0.0)).astype(BF16)
    lane = iota((rows, LANES), 1)
    sub = iota((rows, LANES), 0)
    place = (((sub == 0) & (lane == LANES - 1)) | ((sub == 1) & (lane == 0))).astype(BF16)
    sides[...] = dot_tn(got, place)


def transport(dims, k, fraction, mixed, north_scr, south_scr, sides):
    tracers, levels, rows = dims
    f = [fraction[0, d, k].astype(F32) for d in range(4)]
    remain = 1.0 - f[0] - f[1] - f[2] - f[3]
    lane = iota((rows, LANES), 1)
    sub = iota((rows, LANES), 0)
    out = []
    for t in range(tracers):
        index = t * levels + k
        at = pl.ds(pl.multiple_of(index * rows, rows), rows)
        m = mixed[at, :]
        side = sides[at, :]
        east = jnp.where(lane == LANES - 1, side, pltpu.roll(m, LANES - 1, 1))
        west = jnp.where(lane == 0, side, pltpu.roll(m, 1, 1))
        north = jnp.where(
            sub == rows - 1,
            jnp.broadcast_to(north_scr[pl.ds(index, 1), :], (rows, LANES)),
            pltpu.roll(m, rows - 1, 0),
        )
        south = jnp.where(
            sub == 0, jnp.broadcast_to(south_scr[pl.ds(index, 1), :], (rows, LANES)), pltpu.roll(m, 1, 0)
        )
        out.append((at, remain * m + f[0] * east + f[1] * west + f[2] * north + f[3] * south))
    return out


def step_body(dims, mixed, north, south, east, west, fraction, profiles, kron, surface, *rest):
    new_mixed, up, down, to_west, to_east, new_surface, north_scr, south_scr, sides, adj, low, mix = rest
    tracers, levels, rows = dims
    unpack_halo(dims, north, south, east, west, north_scr, south_scr, sides)

    def body(k2, ks):
        parts = [[] for _ in range(tracers)]
        for k in ks:
            detrain = profiles[1, k].astype(F32)
            for t, (at, value) in enumerate(transport(dims, k, fraction, mixed, north_scr, south_scr, sides)):
                adj[at, :] = value
                parts[t].append(detrain * value)
        for t in range(tracers):
            two = parts[t] if len(ks) == 2 else parts[t] + [jnp.zeros_like(parts[t][0])]
            store_low(low, k2, rows, t, two)

    over_levels(levels, body)
    convect(dims, adj, low, mix, kron, profiles, new_mixed)
    send_edges(dims, new_mixed, up, down, to_west, to_east)
    for t in range(tracers):
        at = t * levels * rows
        new_surface[t * rows : (t + 1) * rows, :] = surface[t * rows : (t + 1) * rows, :] + adj[at : at + rows, :]


def last_body(dims, mixed, north, south, east, west, fraction, forcing, surface, *rest):
    adjoint, surface_low, north_scr, south_scr, sides = rest
    tracers, levels, rows = dims
    unpack_halo(dims, north, south, east, west, north_scr, south_scr, sides)

    def body(k, carry):
        start = pl.multiple_of(k * rows, rows)
        for t, (at, value) in enumerate(transport(dims, k, fraction, mixed, north_scr, south_scr, sides)):
            adjoint[at, :] = value + forcing[pl.ds(start, rows), t * LANES : (t + 1) * LANES]
        return carry

    lax.fori_loop(0, levels, body, 0)
    for t in range(tracers):
        at = t * levels * rows
        total = surface[t * rows : (t + 1) * rows, :] + adjoint[at : at + rows, :]
        surface_low[t * rows : (t + 1) * rows, :] = total.astype(BF16)


def pack_body(sizes, owner, count, cols, weights, resid, out):
    devices, blocks, slots, levels, tracers, chunk = sizes
    own = owner[...].astype(F32)
    wide = jnp.broadcast_to(own, (blocks, blocks))
    below = iota((blocks, blocks), 0)
    along = iota((blocks, blocks), 1)
    own_col = jnp.sum(jnp.where(below == along, wide, 0.0), axis=1, keepdims=True)
    earlier = jnp.where((own_col == wide) & (below < along), 1.0, 0.0)
    rank = jnp.sum(earlier, axis=0, keepdims=True)
    table = jnp.concatenate(
        [own, rank, count[...].astype(F32), jnp.zeros((5, blocks), F32)], axis=0
    ).astype(BF16)
    total = blocks * slots
    spread = (iota((blocks, total), 1) // slots == iota((blocks, total), 0)).astype(BF16)
    each = jnp.dot(table, spread, preferred_element_type=F32)
    slot = iota((1, total), 1) % slots
    target = (each[0:1].astype(jnp.int32) * CAPACITY + each[1:2].astype(jnp.int32)) * slots + slot
    valid = slot < each[2:3].astype(jnp.int32)
    held = jnp.where(valid, resid[...].astype(F32), 0.0)
    place = cols[...]
    high = (place // LANES).astype(F32)
    lower = (place % LANES).astype(F32)
    fill = LANES - levels - tracers - 2
    data = jnp.concatenate(
        [weights[...].astype(F32), held, high, lower, jnp.zeros((fill, total), F32)], axis=0
    ).astype(BF16)

    def body(c, carry):
        at = pl.multiple_of(c * chunk, chunk)
        pick = jnp.where(iota((chunk, total), 0) + at == target, 1.0, 0.0).astype(BF16)
        out[pl.ds(at, chunk), :] = dot_nt(pick, data).astype(BF16)
        return carry

    lax.fori_loop(0, out.shape[0] // chunk, body, 0)


def forcing_body(dims, chunk, got, forcing, left, right):
    tracers, levels, rows = dims
    padded = left.shape[0] // rows

    def body(c, carry):
        at = pl.multiple_of(c * chunk, chunk)
        part = got[pl.ds(at, chunk), :].astype(F32)
        lane = iota((chunk, LANES), 1).astype(F32)
        hit = part[:, levels + tracers + 1 : levels + tracers + 2] == lane
        for t in range(tracers):
            right[:, t * LANES : (t + 1) * LANES] = jnp.where(
                hit, part[:, levels + t : levels + t + 1], 0.0
            ).astype(BF16)
        turned = part.T
        high = turned[levels + tracers : levels + tracers + 1, :]
        sub = iota((rows, chunk), 0).astype(F32)
        mine = sub == high
        for k2 in range(padded // 2):
            two = []
            for k in (2 * k2, 2 * k2 + 1):
                two.append(jnp.where(mine, turned[k : k + 1, :], 0.0) if k < levels else jnp.zeros((rows, chunk), F32))
            left[2 * k2 * rows : (2 * k2 + 2) * rows, :] = jnp.concatenate(two, axis=0).astype(BF16)
        value = jnp.dot(left[...], right[...], preferred_element_type=F32)

        @pl.when(c == 0)
        def _():
            forcing[...] = value

        @pl.when(c > 0)
        def _():
            forcing[...] += value

        return carry

    lax.fori_loop(0, got.shape[0] // chunk, body, 0)


def lon_body(got, matrix, out):
    count = got.shape[0]
    total = jnp.zeros(out.shape, F32)
    for z in range(count):
        total = total + dot_nt(got[z], matrix[:, z * LANES : (z + 1) * LANES])
    out[...] = total.astype(BF16)


def lat_body(tracers, rows, got, matrix, out):
    bands = got.shape[0]
    size = tracers * rows
    lat = lax.axis_index("lat")
    own = matrix[pl.ds(pl.multiple_of(lat * rows, rows), rows), :]
    own = jnp.concatenate([own] * tracers, axis=0)
    total = jnp.zeros(out.shape, F32)
    for b in range(bands):
        block = own[:, b * rows : (b + 1) * rows]
        block = jnp.concatenate([block] * tracers, axis=1)
        same = iota((size, size), 0) // rows == iota((size, size), 1) // rows
        total = total + jnp.dot(
            jnp.where(same, block, 0.0).astype(BF16), got[b], preferred_element_type=F32
        )
    out[...] = total


def ring(axis, step):
    count = lax.axis_size(axis)
    return [(i, (i + step) % count) for i in range(count)]


def exchange(up, down, to_west, to_east):
    south = lax.ppermute(up, "lat", ring("lat", 1))
    north = lax.ppermute(down, "lat", ring("lat", -1))
    east = lax.ppermute(to_west, "lon", ring("lon", -1))
    west = lax.ppermute(to_east, "lon", ring("lon", 1))
    return north, south, east, west


def shards(
    adjoint_in,
    fractions,
    profiles,
    kernel,
    obs_weights,
    obs_resid,
    obs_cols,
    obs_owner,
    obs_count,
    lat_matrix,
    lon_matrix,
):
    dims = tracers, levels, rows = adjoint_in.shape[:3]
    assert adjoint_in.shape[3] == LANES
    padded = (levels + 1) // 2 * 2
    count = tracers * levels
    cells = count * rows
    wide = tracers * LANES
    devices = lax.axis_size(BOTH)
    state = jax.ShapeDtypeStruct((cells, LANES), F32)
    row_edge = jax.ShapeDtypeStruct((count, LANES), BF16)
    side_edge = jax.ShapeDtypeStruct((1, cells), F32)
    edges = [row_edge, row_edge, side_edge, side_edge]
    kron_type = jax.ShapeDtypeStruct((padded * rows, padded * rows), BF16)
    surface_type = jax.ShapeDtypeStruct((tracers * rows, LANES), F32)
    low_scr = pltpu.VMEM((padded * rows, wide), BF16)
    mix_scr = pltpu.VMEM((padded * rows, wide), F32)
    halo_scr = [
        pltpu.VMEM(((count + 7) // 8 * 8, LANES), F32),
        pltpu.VMEM(((count + 7) // 8 * 8, LANES), F32),
        pltpu.VMEM((cells, LANES), F32),
    ]

    def spec(leaf):
        return full(leaf.shape)

    mixed, kron, *out = pl.pallas_call(
        functools.partial(first_body, dims),
        grid=(1,),
        out_shape=[state, kron_type] + edges,
        in_specs=[full(kernel.shape), full(profiles.shape), spec(state)],
        out_specs=[spec(s) for s in [state, kron_type] + edges],
        scratch_shapes=[low_scr, mix_scr],
        compiler_params=params(),
        name="first",
    )(kernel, profiles, adjoint_in.reshape(cells, LANES))
    halo = exchange(*out)

    blocks = obs_count.shape[0]
    slots = obs_cols.shape[0] // blocks
    rows_out = devices * CAPACITY * slots
    packed = pl.pallas_call(
        functools.partial(pack_body, (devices, blocks, slots, levels, tracers, 8 * CAPACITY * slots)),
        out_shape=jax.ShapeDtypeStruct((rows_out, LANES), BF16),
        compiler_params=params(),
        name="pack",
    )(
        obs_owner.reshape(1, blocks),
        obs_count.reshape(1, blocks),
        obs_cols.reshape(1, blocks * slots),
        obs_weights,
        obs_resid,
    )
    got = lax.all_to_all(
        packed.reshape(devices, CAPACITY * slots, LANES), BOTH, split_axis=0, concat_axis=0, tiled=True
    )
    chunk = min(rows_out, 1536)
    forcing = pl.pallas_call(
        functools.partial(forcing_body, dims, chunk),
        out_shape=jax.ShapeDtypeStruct((padded * rows, wide), F32),
        scratch_shapes=[pltpu.VMEM((padded * rows, chunk), BF16), pltpu.VMEM((chunk, wide), BF16)],
        compiler_params=params(),
        name="forcing",
    )(got.reshape(rows_out, LANES))

    surface = jnp.zeros(surface_type.shape, F32)
    for step_index in range(STEPS - 1, 0, -1):
        frac_spec = pl.BlockSpec((1,) + fractions.shape[1:], lambda i, n=step_index: (n, 0, 0, 0, 0))
        mixed, *out, surface = pl.pallas_call(
            functools.partial(step_body, dims),
            grid=(1,),
            out_shape=[state] + edges + [surface_type],
            in_specs=[spec(state), spec(row_edge), spec(row_edge), spec(side_edge), spec(side_edge)]
            + [frac_spec, full(profiles.shape), spec(kron_type), spec(surface_type)],
            out_specs=[spec(s) for s in [state] + edges + [surface_type]],
            scratch_shapes=halo_scr + [pltpu.VMEM((cells, LANES), F32), low_scr, mix_scr],
            compiler_params=params(),
            name="step",
        )(mixed, *halo, fractions, profiles, kron, surface)
        halo = exchange(*out)

    frac_spec = pl.BlockSpec((1,) + fractions.shape[1:], lambda i: (0, 0, 0, 0, 0))
    low_type = jax.ShapeDtypeStruct(surface_type.shape, BF16)
    adjoint, surface_low = pl.pallas_call(
        functools.partial(last_body, dims),
        grid=(1,),
        out_shape=[state, low_type],
        in_specs=[spec(state), spec(row_edge), spec(row_edge), spec(side_edge), spec(side_edge)]
        + [frac_spec, full(forcing.shape), spec(surface_type)],
        out_specs=[spec(state), spec(low_type)],
        scratch_shapes=halo_scr,
        compiler_params=params(),
        name="last",
    )(mixed, *halo, fractions, forcing, surface)

    lon_count = lax.axis_size("lon")
    spread = jnp.broadcast_to(surface_low[None], (lon_count,) + surface_low.shape)
    band = lax.all_to_all(spread, "lon", split_axis=0, concat_axis=0, tiled=True)
    across = pl.pallas_call(
        lon_body,
        out_shape=low_type,
        compiler_params=params(),
        name="lon_smooth",
    )(band, lon_matrix)
    column = lax.all_gather(across, "lat", axis=0)
    smoothed = pl.pallas_call(
        functools.partial(lat_body, tracers, rows),
        out_shape=surface_type,
        compiler_params=params(),
        name="lat_smooth",
    )(column, lat_matrix)
    return adjoint.reshape(adjoint_in.shape), smoothed.reshape(tracers, rows, LANES)


def solution(mesh):
    placed = (
        P(None, None, "lat", "lon"),
        P(None, None, None, "lat", "lon"),
        P(None, None, "lat", "lon"),
        P(),
        P(None, BOTH),
        P(None, BOTH),
        P(BOTH),
        P(BOTH, None),
        P(BOTH),
        P(),
        P("lon", None),
    )
    return jax.shard_map(
        shards,
        mesh=mesh,
        in_specs=placed,
        out_specs=(P(None, None, "lat", "lon"), P(None, "lat", "lon")),
        check_vma=False,
    )
```

time: 187 us -> 100 us (0.53)
  local copies, waits for them, and re-layouts: 73 us -> 6.06 us
  Pallas kernels: 0 us -> 36.6 us
  starting transfers between devices: 55.3 us -> 22.1 us
  other arithmetic: 19.5 us -> 0 us
  waiting for transfers between devices: 0.05 us -> 17.7 us
  matrix products: 15.2 us -> 0 us
  blocking collectives: 21.6 us -> 16.6 us
    pallas_call x0 -> x9, Pallas kernels: none -> 36.6 us  [the longest x3 21.1 us: shards(): pl.pallas_call(functools.partial(step_body, dims), grid=(1,), out_shape=[...]
    ppermute x16, starting transfers between devices: 39.4 us -> 14.8 us  [the longest x4 10.5 us: exchange(): north = lax.ppermute(down, 'lat', ring('lat', -1))]
    slice x17 -> x0, local copies, waits for them, and re-layouts: 22.4 us -> none  [the longest x12 17 us: extended(): head = lax.slice_in_dim(cells, 0, width, axis=dim)]
    mul x26 -> x0, local copies, waits for them, and re-layouts: 20.6 us -> none  [the longest x4 4.15 us: combine_sides(): remain * field_in + fraction[0] * east_side + fraction[1] * west_side]
    ppermute x16, waiting for transfers between devices: 0.04 us -> 17.7 us  [the longest x4 13.2 us: exchange(): west = lax.ppermute(to_east, 'lon', ring('lon', 1))]
    dot_general x10 -> x0, matrix products: 15.2 us -> none  [the longest x4 11.7 us: route_forcing(): jnp.dot(weights, scaled_sel, preferred_element_type=jnp.float32)]
    ppermute x8 -> x0, local copies, waits for them, and re-layouts: 14.7 us -> none  [the longest x4 9.52 us: extended(): lax.ppermute(tail, axis, [(i, (i + 1) % count) for i in range(ends)])]
    all_gather x2 -> x1, blocking collectives: 21.6 us -> 8.28 us  [shards(): column = lax.all_gather(across, 'lat', axis=0)]
  transfers between devices with their start and end apart: 19 -> 17, of which waited for: 0 -> 10; matrix products, arithmetic and copies ran while one was open for 46% -> 0% of each run, Pallas kernels for 0% -> 25%
where the time goes in v1:
time: 100 us; the launch traced here: 99.8 us
  Pallas kernels  36.6 us (37%)
  starting transfers between devices  22.1 us (22%)
  waiting for transfers between devices  17.7 us (18%)
  blocking collectives  16.6 us (17%)
  local copies, waits for them, and re-layouts  6.06 us (6%)
    pallas_call x3, Pallas kernels, shards(): pl.pallas_call(functools.partial(step_body, dims), grid=(1,), out_shape=[...  21.1 us
    ppermute x4, waiting for transfers between devices, exchange(): west = lax.ppermute(to_east, 'lon', ring('lon', 1))  13.2 us
    ppermute x4, starting transfers between devices, exchange(): north = lax.ppermute(down, 'lat', ring('lat', -1))  10.5 us
    all_to_all x1, blocking collectives, shards(): lax.all_to_all(spread, 'lon', split_axis=0, concat_axis=0, tiled=True)  8.3 us
    all_gather x1, blocking collectives, shards(): column = lax.all_gather(across, 'lat', axis=0)  8.28 us
    pallas_call x1, Pallas kernels, shards(): pl.pallas_call(functools.partial(last_body, dims), grid=(1,), out_shape=[...  7.85 us
    all_to_all x1, starting transfers between devices, shards(): lax.all_to_all(packed.reshape(devices, CAPACITY * slots, LANES), BOTH, sp...  7.33 us
    unnamed x26, local copies, waits for them, and re-layouts  6.05 us
  transfers between devices with their start and end apart: 17, of which 10 were waited for; matrix products, arithmetic and copies ran while one was open for 0% of the time, Pallas kernels for 25%

profile of v1, /device:TPU:0, one launch (start us, length us, event | category | flops | bytes accessed | tf_op | source)
XLA Modules:
  0.0 99.8 jit_solution(18054460348115242197)
XLA Ops:
  0.6 0.0 copy-start.1
  0.6 0.0 copy-start.6
  0.7 1.0 copy-done.6
  1.6 0.0 copy-start.8
  1.6 0.7 copy-done.8
  2.3 0.0 copy-start.10
  2.3 0.7 copy-done.10
  3.0 0.0 copy-start.11
  3.0 0.7 copy-done.11
  3.6 0.7 copy-done.12
  4.3 2.5 %pack.1 = bf16[1536,128]{1,0:T(8,128)(2,1)} custom-call(s32[1,128]{1,0:T(1,128)S(1)} %bitcast.13, s32[1,128]{1,0:T(1,128)S(1)} %bitcast.14, s32[1,1024]{1,0:T(1,128)S(1)} %bitcast.12, bf16[79,1024]{1,0:T(8,128)(2,1)S(1)} %copy-done.6, bf16[4,1024]{1,0:T(4,128)(2,1)S(1)} %copy-done.8), custom_call_target="tpu_custom_call" | custom-call | tf_op jit(solution)/shard_map/pack/pallas_call | solution.py:358
  6.8 7.3 %all-to-all-start = ((bf16[32,48,128]{2,1,0:T(8,128)(2,1)}), bf16[32,48,128]{2,1,0:T(8,128)(2,1)S(1)}, u32[]{:S(2)}, u32[]{:S(2)}) async-start(bf16[32,48,128]{2,1,0:T(8,128)(2,1)} %bitcast.4), calls=%async_computation | async-start | bytes 786432 | tf_op jit(solution)/shard_map/all_to_all | solution.py:370
  14.1 0.0 copy-done.1
  14.1 0.0 copy-done.7
  14.1 0.0 copy-start.2
  14.1 1.3 %copy-done.2 = f32[4,79,8,128]{3,2,1,0:T(8,128)S(1)} copy-done((f32[4,79,8,128]{3,2,1,0:T(8,128)S(1)}, f32[4,79,8,128]{3,2,1,0:T(8,128)}, u32[]{:S(2)}) %copy-start.2) | copy-done | bytes 1294360
  15.4 2.4 %first.1 = (f32[2528,128]{1,0:T(8,128)S(1)}, bf16[640,640]{1,0:T(8,128)(2,1)S(1)}, bf16[316,128]{1,0:T(8,128)(2,1)S(1)}, bf16[316,128]{1,0:T(8,128)(2,1)S(1)}, f...) custom-call(bf16[79,79]{1,0:T(8,128)(2,1)S(1)} %copy-done.7, bf16[2,79,8,128]{3,2,1,0:T(8,128)(2,1)S(1)} %copy-done.1, ...), custom_call_target="tpu_custom_call" | custom-call | tf_op jit(solution)/shard_map/first/pallas_call | solution.py:343
  17.9 2.7 %collective-permute-start = (bf16[316,128]{1,0:T(8,128)(2,1)S(1)}, bf16[316,128]{1,0:T(8,128)(2,1)S(1)}, u32[]{:S(2)}, u32[]{:S(2)}) collective-permute-start(bf16[316,128]{1,0:T(8,128)(2,1)S(1)} %get-tuple-element.29), channel_id=1, source_target_pairs={{0,24},{8,0},{16,8},{24,16},{1,25},{9,1},{17,9},{25,17},{2,26},{10... | collective-permute-start | bytes 242696 | tf_op jit(solution)/shard_map/ppermute | solution.py:300
  20.6 0.0 collective-permute-start.1
  20.6 2.8 %collective-permute-start.2 = (f32[1,2528]{1,0:T(1,128)S(1)}, f32[1,2528]{1,0:T(1,128)S(1)}, u32[]{:S(2)}, u32[]{:S(2)}) collective-permute-start(f32[1,2528]{1,0:T(1,128)S(1)} %get-tuple-element.31), channel_id=1, source_target_pairs={{0,7},{1,0},{2,1},{3,2},{4,3},{5,4},{6,5},{7,6},{8,15},{9,8},{10,9... | collective-permute-start | bytes 30344 | tf_op jit(solution)/shard_map/ppermute | solution.py:301
  23.4 0.0 collective-permute-start.3
  23.4 1.4 %collective-permute-done.2.east = f32[1,2528]{1,0:T(1,128)S(1)} collective-permute-done((f32[1,2528]{1,0:T(1,128)S(1)}, f32[1,2528]{1,0:T(1,128)S(1)}, u32[]{:S(2)}, u32[]{:S(2)}) %collective-permute-start.2) | collective-permute-done | bytes 10144 | tf_op jit(solution)/shard_map/ppermute | solution.py:301
  24.8 3.5 %collective-permute-done.3.west = f32[1,2528]{1,0:T(1,128)S(1)} collective-permute-done((f32[1,2528]{1,0:T(1,128)S(1)}, f32[1,2528]{1,0:T(1,128)S(1)}, u32[]{:S(2)}, u32[]{:S(2)}) %collective-permute-start.3) | collective-permute-done | bytes 10144 | tf_op jit(solution)/shard_map/ppermute | solution.py:302
  28.3 0.0 collective-permute-done.north
  28.3 0.0 collective-permute-done.1.south
  28.3 7.0 %step.3 = (f32[2528,128]{1,0:T(8,128)S(1)}, bf16[316,128]{1,0:T(8,128)(2,1)S(1)}, bf16[316,128]{1,0:T(8,128)(2,1)S(1)}, f32[1,2528]{1,0:T(1,128)S(1)}, f32[1,2528]{1,0:T(1,128)S(1)}, /*index=5*/f32[32,128]{1,0:T(8,128)S(1)}) custom-call(f32[2528,128]{1,0:T(8,128)S(1)} %get-tuple-element.28.mixed, bf16[316,128]{1,0:T(8,128)(2,1)S(1)} %collective-permute-done.north, ...), custom_call_target="tpu_custom_call" | custom-call | tf_op jit(solution)/shard_map/step/pallas_call | solution.py:385
  35.3 2.7 %collective-permute-start.4 = (bf16[316,128]{1,0:T(8,128)(2,1)S(1)}, bf16[316,128]{1,0:T(8,128)(2,1)S(1)}, u32[]{:S(2)}, u32[]{:S(2)}) collective-permute-start(bf16[316,128]{1,0:T(8,128)(2,1)S(1)} %get-tuple-element.35), channel_id=1, source_target_pairs={{0,24},{8,0},{16,8},{24,16},{1,25},{9,1},{17,9},{25,17},{2,26},{10... | collective-permute-start | bytes 242696 | tf_op jit(solution)/shard_map/ppermute | solution.py:300
  38.0 0.0 collective-permute-start.5
  38.0 0.0 collective-permute-start.6
  38.0 0.5 collective-permute-start.7
  38.5 0.9 collective-permute-done.6.east
  39.4 3.5 %collective-permute-done.7.west = f32[1,2528]{1,0:T(1,128)S(1)} collective-permute-done((f32[1,2528]{1,0:T(1,128)S(1)}, f32[1,2528]{1,0:T(1,128)S(1)}, u32[]{:S(2)}, u32[]{:S(2)}) %collective-permute-start.7) | collective-permute-done | bytes 10144 | tf_op jit(solution)/shard_map/ppermute | solution.py:302
  42.9 0.0 collective-permute-done.4.north
  42.9 0.4 collective-permute-done.5.south
  43.3 7.0 %step.4 = (f32[2528,128]{1,0:T(8,128)S(1)}, bf16[316,128]{1,0:T(8,128)(2,1)S(1)}, bf16[316,128]{1,0:T(8,128)(2,1)S(1)}, f32[1,2528]{1,0:T(1,128)S(1)}, f32[1,2528]{1,0:T(1,128)S(1)}, /*index=5*/f32[32,128]{1,0:T(8,128)S(1)}) custom-call(f32[2528,128]{1,0:T(8,128)S(1)} %get-tuple-element.34.mixed, bf16[316,128]{1,0:T(8,128)(2,1)S(1)} %collective-permute-done.4.north, ...), custom_call_target="tpu_custom_call" | custom-call | tf_op jit(solution)/shard_map/step/pallas_call | solution.py:385
  50.3 2.5 %collective-permute-start.8 = (bf16[316,128]{1,0:T(8,128)(2,1)S(1)}, bf16[316,128]{1,0:T(8,128)(2,1)S(1)}, u32[]{:S(2)}, u32[]{:S(2)}) collective-permute-start(bf16[316,128]{1,0:T(8,128)(2,1)S(1)} %get-tuple-element.41), channel_id=1, source_target_pairs={{0,24},{8,0},{16,8},{24,16},{1,25},{9,1},{17,9},{25,17},{2,26},{10... | collective-permute-start | bytes 242696 | tf_op jit(solution)/shard_map/ppermute | solution.py:300
  52.9 0.0 collective-permute-start.9
  52.9 0.0 collective-permute-start.10
  52.9 0.5 collective-permute-start.11
  53.4 0.9 collective-permute-done.10.east
  54.3 3.5 %collective-permute-done.11.west = f32[1,2528]{1,0:T(1,128)S(1)} collective-permute-done((f32[1,2528]{1,0:T(1,128)S(1)}, f32[1,2528]{1,0:T(1,128)S(1)}, u32[]{:S(2)}, u32[]{:S(2)}) %collective-permute-start.11) | collective-permute-done | bytes 10144 | tf_op jit(solution)/shard_map/ppermute | solution.py:302
  57.8 0.0 collective-permute-done.8.north
  57.8 0.4 collective-permute-done.9.south
  58.2 7.1 %step.5 = (f32[2528,128]{1,0:T(8,128)S(1)}, bf16[316,128]{1,0:T(8,128)(2,1)S(1)}, bf16[316,128]{1,0:T(8,128)(2,1)S(1)}, f32[1,2528]{1,0:T(1,128)S(1)}, f32[1,2528]{1,0:T(1,128)S(1)}, /*index=5*/f32[32,128]{1,0:T(8,128)S(1)}) custom-call(f32[2528,128]{1,0:T(8,128)S(1)} %get-tuple-element.40.mixed, bf16[316,128]{1,0:T(8,128)(2,1)S(1)} %collective-permute-done.8.north, ...), custom_call_target="tpu_custom_call" | custom-call | tf_op jit(solution)/shard_map/step/pallas_call | solution.py:385
  65.3 1.1 %copy-done.3 = f32[2528,128]{1,0:T(8,128)} copy-done((f32[2528,128]{1,0:T(8,128)}, f32[2528,128]{1,0:T(8,128)S(1)}, u32[]{:S(2)}) %copy-start.3) | copy-done | bytes 1294360
  66.4 2.5 %collective-permute-start.12 = (bf16[316,128]{1,0:T(8,128)(2,1)S(1)}, bf16[316,128]{1,0:T(8,128)(2,1)S(1)}, u32[]{:S(2)}, u32[]{:S(2)}) collective-permute-start(bf16[316,128]{1,0:T(8,128)(2,1)S(1)} %get-tuple-element.47), channel_id=1, source_target_pairs={{0,24},{8,0},{16,8},{24,16},{1,25},{9,1},{17,9},{25,17},{2,26},{10... | collective-permute-start | bytes 242696 | tf_op jit(solution)/shard_map/ppermute | solution.py:300
  68.9 0.0 collective-permute-start.13
  68.9 0.0 collective-permute-start.14
  68.9 0.5 collective-permute-start.15
  69.4 0.0 all-to-all-done
  69.4 1.7 %forcing.1 = f32[640,512]{1,0:T(8,128)S(1)} custom-call(bf16[1536,128]{1,0:T(8,128)(2,1)S(1)} %bitcast.9), custom_call_target="tpu_custom_call" | custom-call | tf_op jit(solution)/shard_map/forcing/pallas_call | solution.py:374
  71.1 0.0 collective-permute-done.14.east
  71.1 2.7 %collective-permute-done.15.west = f32[1,2528]{1,0:T(1,128)S(1)} collective-permute-done((f32[1,2528]{1,0:T(1,128)S(1)}, f32[1,2528]{1,0:T(1,128)S(1)}, u32[]{:S(2)}, u32[]{:S(2)}) %collective-permute-start.15) | collective-permute-done | bytes 10144 | tf_op jit(solution)/shard_map/ppermute | solution.py:302
  73.8 0.0 collective-permute-done.12.north
  73.8 0.4 collective-permute-done.13.south
  74.2 0.0 copy-done
  74.3 0.0 copy-done.4
  74.3 7.8 %last.1 = (f32[2528,128]{1,0:T(8,128)}, bf16[32,128]{1,0:T(8,128)(2,1)S(1)}) custom-call(f32[2528,128]{1,0:T(8,128)S(1)} %copy-done.4, bf16[316,128]{1,0:T(8,128)(2,1)S(1)} %collective-permute-done.12.north, bf16[316,128]{1,0:T(8,128)(2,1)S(1)} %collective-permute-done.13.south, f32[1,2528]{1,0:T(1,128)S(1)} %collective-permute-done.14.east, ...), custom_call_target="tpu_custom_call" | custom-call | tf_op jit(solution)/shard_map/last/pallas_call | solution.py:400
  82.1 8.3 %all_to_all.10.got = bf16[8,32,128]{2,1,0:T(8,128)(2,1)S(1)} all-to-all(bf16[8,32,128]{2,1,0:T(8,128)(2,1)S(1)} %broadcast_in_dim.10), channel_id=1, replica_groups=mesh['lat'=4,'lon'=8] {'lon'}, dimensions={0} | all-to-all | bytes 131072 | tf_op jit(solution)/shard_map/all_to_all | solution.py:414
  90.4 0.0 copy-done.5
  90.4 0.2 lon_smooth.1
  90.6 8.3 %all-gather = bf16[128,128]{1,0:T(8,128)(2,1)S(1)} all-gather(bf16[32,128]{1,0:T(8,128)(2,1)S(1)} %lon_smooth.1), channel_id=2, replica_groups=mesh['lat'=4,'lon'=8] {'lat'}, dimensions={0}, use_global_device_ids=true | all-gather | bytes 40960 | tf_op jit(solution)/shard_map/all_gather | solution.py:421
  98.9 0.0 copy-done.9
  98.9 0.8 lat_smooth.1
  (9 shorter events, 0.0 us)
Async XLA Ops:
  0.6 13.5 %copy-start.1 = (bf16[2,79,8,128]{3,2,1,0:T(8,128)(2,1)S(1)}, bf16[2,79,8,128]{3,2,1,0:T(8,128)(2,1)}, u32[]{:S(2)}) copy-start(bf16[2,79,8,128]{3,2,1,0:T(8,128)(2,1)} %profiles.7) | copy-start | bytes 970756
  0.6 1.0 copy-start.6
  1.6 0.7 copy-start.8
  2.3 0.7 copy-start.10
  3.0 0.7 copy-start.11
  3.6 0.7 copy-start.12
  4.3 9.8 %copy-start.7 = (bf16[79,79]{1,0:T(8,128)(2,1)S(1)}, bf16[79,79]{1,0:T(8,128)(2,1)}, u32[]{:S(2)}) copy-start(bf16[79,79]{1,0:T(8,128)(2,1)} %kernel.1) | copy-start | bytes 37450
  6.8 62.6 %all-to-all-start = ((bf16[32,48,128]{2,1,0:T(8,128)(2,1)}), bf16[32,48,128]{2,1,0:T(8,128)(2,1)S(1)}, u32[]{:S(2)}, u32[]{:S(2)}) async-start(bf16[32,48,128]{2,1,0:T(8,128)(2,1)} %bitcast.4), calls=%async_computation | async-start | bytes 786432 | tf_op jit(solution)/shard_map/all_to_all | solution.py:370
  14.1 1.3 %copy-start.2 = (f32[4,79,8,128]{3,2,1,0:T(8,128)S(1)}, f32[4,79,8,128]{3,2,1,0:T(8,128)}, u32[]{:S(2)}) copy-start(f32[4,79,8,128]{3,2,1,0:T(8,128)} %param.11) | copy-start | bytes 3883012
  17.9 10.4 %collective-permute-start = (bf16[316,128]{1,0:T(8,128)(2,1)S(1)}, bf16[316,128]{1,0:T(8,128)(2,1)S(1)}, u32[]{:S(2)}, u32[]{:S(2)}) collective-permute-start(bf16[316,128]{1,0:T(8,128)(2,1)S(1)} %get-tuple-element.29), channel_id=1, source_target_pairs={{0,24},{8,0},{16,8},{24,16},{1,25},{9,1},{17,9},{25,17},{2,26},{10... | collective-permute-start | bytes 242696 | tf_op jit(solution)/shard_map/ppermute | solution.py:300
  20.6 7.7 %collective-permute-start.1 = (bf16[316,128]{1,0:T(8,128)(2,1)S(1)}, bf16[316,128]{1,0:T(8,128)(2,1)S(1)}, u32[]{:S(2)}, u32[]{:S(2)}) collective-permute-start(bf16[316,128]{1,0:T(8,128)(2,1)S(1)} %get-tuple-element.30), channel_id=1, source_target_pairs={{0,8},{8,16},{16,24},{24,0},{1,9},{9,17},{17,25},{25,1},{2,10},{10... | collective-permute-start | bytes 242696 | tf_op jit(solution)/shard_map/ppermute | solution.py:299
  20.6 4.2 %collective-permute-start.2 = (f32[1,2528]{1,0:T(1,128)S(1)}, f32[1,2528]{1,0:T(1,128)S(1)}, u32[]{:S(2)}, u32[]{:S(2)}) collective-permute-start(f32[1,2528]{1,0:T(1,128)S(1)} %get-tuple-element.31), channel_id=1, source_target_pairs={{0,7},{1,0},{2,1},{3,2},{4,3},{5,4},{6,5},{7,6},{8,15},{9,8},{10,9... | collective-permute-start | bytes 30344 | tf_op jit(solution)/shard_map/ppermute | solution.py:301
  23.4 4.9 %collective-permute-start.3 = (f32[1,2528]{1,0:T(1,128)S(1)}, f32[1,2528]{1,0:T(1,128)S(1)}, u32[]{:S(2)}, u32[]{:S(2)}) collective-permute-start(f32[1,2528]{1,0:T(1,128)S(1)} %get-tuple-element.32), channel_id=1, source_target_pairs={{0,1},{1,2},{2,3},{3,4},{4,5},{5,6},{6,7},{7,0},{8,9},{9,10},{10,1... | collective-permute-start | bytes 30344 | tf_op jit(solution)/shard_map/ppermute | solution.py:302
  35.3 7.6 %collective-permute-start.4 = (bf16[316,128]{1,0:T(8,128)(2,1)S(1)}, bf16[316,128]{1,0:T(8,128)(2,1)S(1)}, u32[]{:S(2)}, u32[]{:S(2)}) collective-permute-start(bf16[316,128]{1,0:T(8,128)(2,1)S(1)} %get-tuple-element.35), channel_id=1, source_target_pairs={{0,24},{8,0},{16,8},{24,16},{1,25},{9,1},{17,9},{25,17},{2,26},{10... | collective-permute-start | bytes 242696 | tf_op jit(solution)/shard_map/ppermute | solution.py:300
  38.0 5.3 %collective-permute-start.5 = (bf16[316,128]{1,0:T(8,128)(2,1)S(1)}, bf16[316,128]{1,0:T(8,128)(2,1)S(1)}, u32[]{:S(2)}, u32[]{:S(2)}) collective-permute-start(bf16[316,128]{1,0:T(8,128)(2,1)S(1)} %get-tuple-element.36), channel_id=1, source_target_pairs={{0,8},{8,16},{16,24},{24,0},{1,9},{9,17},{17,25},{25,1},{2,10},{10... | collective-permute-start | bytes 242696 | tf_op jit(solution)/shard_map/ppermute | solution.py:299
  38.0 1.4 %collective-permute-start.6 = (f32[1,2528]{1,0:T(1,128)S(1)}, f32[1,2528]{1,0:T(1,128)S(1)}, u32[]{:S(2)}, u32[]{:S(2)}) collective-permute-start(f32[1,2528]{1,0:T(1,128)S(1)} %get-tuple-element.37), channel_id=1, source_target_pairs={{0,7},{1,0},{2,1},{3,2},{4,3},{5,4},{6,5},{7,6},{8,15},{9,8},{10,9... | collective-permute-start | bytes 30344 | tf_op jit(solution)/shard_map/ppermute | solution.py:301
  38.0 4.9 %collective-permute-start.7 = (f32[1,2528]{1,0:T(1,128)S(1)}, f32[1,2528]{1,0:T(1,128)S(1)}, u32[]{:S(2)}, u32[]{:S(2)}) collective-permute-start(f32[1,2528]{1,0:T(1,128)S(1)} %get-tuple-element.38), channel_id=1, source_target_pairs={{0,1},{1,2},{2,3},{3,4},{4,5},{5,6},{6,7},{7,0},{8,9},{9,10},{10,1... | collective-permute-start | bytes 30344 | tf_op jit(solution)/shard_map/ppermute | solution.py:302
  50.3 7.4 %collective-permute-start.8 = (bf16[316,128]{1,0:T(8,128)(2,1)S(1)}, bf16[316,128]{1,0:T(8,128)(2,1)S(1)}, u32[]{:S(2)}, u32[]{:S(2)}) collective-permute-start(bf16[316,128]{1,0:T(8,128)(2,1)S(1)} %get-tuple-element.41), channel_id=1, source_target_pairs={{0,24},{8,0},{16,8},{24,16},{1,25},{9,1},{17,9},{25,17},{2,26},{10... | collective-permute-start | bytes 242696 | tf_op jit(solution)/shard_map/ppermute | solution.py:300
  52.9 5.3 %collective-permute-start.9 = (bf16[316,128]{1,0:T(8,128)(2,1)S(1)}, bf16[316,128]{1,0:T(8,128)(2,1)S(1)}, u32[]{:S(2)}, u32[]{:S(2)}) collective-permute-start(bf16[316,128]{1,0:T(8,128)(2,1)S(1)} %get-tuple-element.42), channel_id=1, source_target_pairs={{0,8},{8,16},{16,24},{24,0},{1,9},{9,17},{17,25},{25,1},{2,10},{10... | collective-permute-start | bytes 242696 | tf_op jit(solution)/shard_map/ppermute | solution.py:299
  52.9 1.4 %collective-permute-start.10 = (f32[1,2528]{1,0:T(1,128)S(1)}, f32[1,2528]{1,0:T(1,128)S(1)}, u32[]{:S(2)}, u32[]{:S(2)}) collective-permute-start(f32[1,2528]{1,0:T(1,128)S(1)} %get-tuple-element.43), channel_id=1, source_target_pairs={{0,7},{1,0},{2,1},{3,2},{4,3},{5,4},{6,5},{7,6},{8,15},{9,8},{10,9... | collective-permute-start | bytes 30344 | tf_op jit(solution)/shard_map/ppermute | solution.py:301
  52.9 4.9 %collective-permute-start.11 = (f32[1,2528]{1,0:T(1,128)S(1)}, f32[1,2528]{1,0:T(1,128)S(1)}, u32[]{:S(2)}, u32[]{:S(2)}) collective-permute-start(f32[1,2528]{1,0:T(1,128)S(1)} %get-tuple-element.44), channel_id=1, source_target_pairs={{0,1},{1,2},{2,3},{3,4},{4,5},{5,6},{6,7},{7,0},{8,9},{9,10},{10,1... | collective-permute-start | bytes 30344 | tf_op jit(solution)/shard_map/ppermute | solution.py:302
  58.2 16.1 %copy-start = (bf16[4,4,79,8,128]{4,3,2,1,0:T(8,128)(2,1)S(1)}, bf16[4,4,79,8,128]{4,3,2,1,0:T(8,128)(2,1)}, u32[]{:S(2)}) copy-start(bf16[4,4,79,8,128]{4,3,2,1,0:T(8,128)(2,1)} %fraction.7) | copy-start | bytes 7766020
  65.3 1.1 %copy-start.3 = (f32[2528,128]{1,0:T(8,128)}, f32[2528,128]{1,0:T(8,128)S(1)}, u32[]{:S(2)}) copy-start(f32[2528,128]{1,0:T(8,128)S(1)} %get-tuple-element.46.mixed) | copy-start | bytes 3883012
  66.4 7.4 %collective-permute-start.12 = (bf16[316,128]{1,0:T(8,128)(2,1)S(1)}, bf16[316,128]{1,0:T(8,128)(2,1)S(1)}, u32[]{:S(2)}, u32[]{:S(2)}) collective-permute-start(bf16[316,128]{1,0:T(8,128)(2,1)S(1)} %get-tuple-element.47), channel_id=1, source_target_pairs={{0,24},{8,0},{16,8},{24,16},{1,25},{9,1},{17,9},{25,17},{2,26},{10... | collective-permute-start | bytes 242696 | tf_op jit(solution)/shard_map/ppermute | solution.py:300
  68.9 5.3 %collective-permute-start.13 = (bf16[316,128]{1,0:T(8,128)(2,1)S(1)}, bf16[316,128]{1,0:T(8,128)(2,1)S(1)}, u32[]{:S(2)}, u32[]{:S(2)}) collective-permute-start(bf16[316,128]{1,0:T(8,128)(2,1)S(1)} %get-tuple-element.48), channel_id=1, source_target_pairs={{0,8},{8,16},{16,24},{24,0},{1,9},{9,17},{17,25},{25,1},{2,10},{10... | collective-permute-start | bytes 242696 | tf_op jit(solution)/shard_map/ppermute | solution.py:299
  68.9 2.2 %collective-permute-start.14 = (f32[1,2528]{1,0:T(1,128)S(1)}, f32[1,2528]{1,0:T(1,128)S(1)}, u32[]{:S(2)}, u32[]{:S(2)}) collective-permute-start(f32[1,2528]{1,0:T(1,128)S(1)} %get-tuple-element.49), channel_id=1, source_target_pairs={{0,7},{1,0},{2,1},{3,2},{4,3},{5,4},{6,5},{7,6},{8,15},{9,8},{10,9... | collective-permute-start | bytes 30344 | tf_op jit(solution)/shard_map/ppermute | solution.py:301
  68.9 4.9 %collective-permute-start.15 = (f32[1,2528]{1,0:T(1,128)S(1)}, f32[1,2528]{1,0:T(1,128)S(1)}, u32[]{:S(2)}, u32[]{:S(2)}) collective-permute-start(f32[1,2528]{1,0:T(1,128)S(1)} %get-tuple-element.50), channel_id=1, source_target_pairs={{0,1},{1,2},{2,3},{3,4},{4,5},{5,6},{6,7},{7,0},{8,9},{9,10},{10,1... | collective-permute-start | bytes 30344 | tf_op jit(solution)/shard_map/ppermute | solution.py:302
  69.4 4.8 %copy-start.4 = (f32[2528,128]{1,0:T(8,128)S(1)}, f32[2528,128]{1,0:T(8,128)}, u32[]{:S(2)}) copy-start(f32[2528,128]{1,0:T(8,128)} %copy-done.3) | copy-start | bytes 3883012
  74.3 16.2 %copy-start.5 = (bf16[128,1024]{1,0:T(8,128)(2,1)S(1)}, bf16[128,1024]{1,0:T(8,128)(2,1)}, u32[]{:S(2)}) copy-start(bf16[128,1024]{1,0:T(8,128)(2,1)} %matrix.2) | copy-start | bytes 786436
  74.3 24.7 %copy-start.9 = (bf16[32,32]{1,0:T(8,128)(2,1)S(1)}, bf16[32,32]{1,0:T(8,128)(2,1)}, u32[]{:S(2)}) copy-start(bf16[32,32]{1,0:T(8,128)(2,1)} %matrix.3) | copy-start | bytes 6148

commit v2 on v1

--- a/solution.py
+++ b/solution.py
@@ -13,6 +13,10 @@
 BF16 = jnp.bfloat16
 BOTH = ("lat", "lon")
 LANES = 128
+
+
+def aligned(value, by):
+    return value if isinstance(value, int) else pl.multiple_of(value, by)
 
 
 def iota(shape, dim):
@@ -48,17 +52,17 @@
     tracers, levels, rows = dims
     mix[...] = jnp.dot(kron[...], low[...], preferred_element_type=F32)
 
-    def body(k, carry):
-        entrain = profiles[0, k].astype(F32)
-        start = pl.multiple_of(k * rows, rows)
-        for t in range(tracers):
-            at = pl.multiple_of((t * levels + k) * rows, rows)
-            mixed[pl.ds(at, rows), :] = adj[pl.ds(at, rows), :] + entrain * mix[
-                pl.ds(start, rows), t * LANES : (t + 1) * LANES
-            ]
-        return carry
-
-    lax.fori_loop(0, levels, body, 0)
+    def body(k2, ks):
+        for k in ks:
+            entrain = profiles[0, k].astype(F32)
+            start = aligned(k * rows, rows)
+            for t in range(tracers):
+                at = aligned((t * levels + k) * rows, rows)
+                mixed[pl.ds(at, rows), :] = adj[pl.ds(at, rows), :] + entrain * mix[
+                    pl.ds(start, rows), t * LANES : (t + 1) * LANES
+                ]
+
+    over_levels(levels, body)
 
 
 def send_edges(dims, mixed, up, down, west, east):
@@ -79,17 +83,14 @@
 
 
 def store_low(low, k2, rows, t, parts):
-    low[pl.ds(pl.multiple_of(k2 * 2 * rows, 2 * rows), 2 * rows), t * LANES : (t + 1) * LANES] = jnp.concatenate(
+    low[pl.ds(aligned(k2 * 2 * rows, 2 * rows), 2 * rows), t * LANES : (t + 1) * LANES] = jnp.concatenate(
         parts, axis=0
     ).astype(BF16)
 
 
 def over_levels(levels, body):
-    def pair(k2, carry):
+    for k2 in range(levels // 2):
         body(k2, (2 * k2, 2 * k2 + 1))
-        return carry
-
-    lax.fori_loop(0, levels // 2, pair, 0)
     if levels % 2:
         body(levels // 2, (levels - 1,))
 
@@ -102,7 +103,7 @@
         detrains = [profiles[1, k].astype(F32) for k in ks]
         for t in range(tracers):
             parts = [
-                d * adjoint[pl.ds(pl.multiple_of((t * levels + k) * rows, rows), rows), :] for d, k in zip(detrains, ks)
+                d * adjoint[pl.ds(aligned((t * levels + k) * rows, rows), rows), :] for d, k in zip(detrains, ks)
             ]
             store_low(low, k2, rows, t, parts if len(parts) == 2 else parts + [jnp.zeros_like(parts[0])])
 
@@ -133,7 +134,7 @@
     out = []
     for t in range(tracers):
         index = t * levels + k
-        at = pl.ds(pl.multiple_of(index * rows, rows), rows)
+        at = pl.ds(aligned(index * rows, rows), rows)
         m = mixed[at, :]
         side = sides[at, :]
         east = jnp.where(lane == LANES - 1, side, pltpu.roll(m, LANES - 1, 1))
@@ -179,13 +180,13 @@
     tracers, levels, rows = dims
     unpack_halo(dims, north, south, east, west, north_scr, south_scr, sides)
 
-    def body(k, carry):
-        start = pl.multiple_of(k * rows, rows)
-        for t, (at, value) in enumerate(transport(dims, k, fraction, mixed, north_scr, south_scr, sides)):
-            adjoint[at, :] = value + forcing[pl.ds(start, rows), t * LANES : (t + 1) * LANES]
-        return carry
-
-    lax.fori_loop(0, levels, body, 0)
+    def body(k2, ks):
+        for k in ks:
+            start = aligned(k * rows, rows)
+            for t, (at, value) in enumerate(transport(dims, k, fraction, mixed, north_scr, south_scr, sides)):
+                adjoint[at, :] = value + forcing[pl.ds(start, rows), t * LANES : (t + 1) * LANES]
+
+    over_levels(levels, body)
     for t in range(tracers):
         at = t * levels * rows
         total = surface[t * rows : (t + 1) * rows, :] + adjoint[at : at + rows, :]
@@ -220,7 +221,7 @@
     ).astype(BF16)
 
     def body(c, carry):
-        at = pl.multiple_of(c * chunk, chunk)
+        at = aligned(c * chunk, chunk)
         pick = jnp.where(iota((chunk, total), 0) + at == target, 1.0, 0.0).astype(BF16)
         out[pl.ds(at, chunk), :] = dot_nt(pick, data).astype(BF16)
         return carry
@@ -233,7 +234,7 @@
     padded = left.shape[0] // rows
 
     def body(c, carry):
-        at = pl.multiple_of(c * chunk, chunk)
+        at = aligned(c * chunk, chunk)
         part = got[pl.ds(at, chunk), :].astype(F32)
         lane = iota((chunk, LANES), 1).astype(F32)
         hit = part[:, levels + tracers + 1 : levels + tracers + 2] == lane
@@ -277,7 +278,7 @@
     bands = got.shape[0]
     size = tracers * rows
     lat = lax.axis_index("lat")
-    own = matrix[pl.ds(pl.multiple_of(lat * rows, rows), rows), :]
+    own = matrix[pl.ds(aligned(lat * rows, rows), rows), :]
     own = jnp.concatenate([own] * tracers, axis=0)
     total = jnp.zeros(out.shape, F32)
     for b in range(bands):

time: 100 us -> 81.7 us (0.82)
  Pallas kernels: 36.6 us -> 18 us
    pallas_call x3, Pallas kernels: 21.1 us -> 9.28 us  [shards(): pl.pallas_call(functools.partial(step_body, dims), grid=(1,), out_shape=[...]
    pallas_call x1, Pallas kernels: 7.85 us -> 2.22 us  [shards(): pl.pallas_call(functools.partial(last_body, dims), grid=(1,), out_shape=[...]
    pallas_call x1, Pallas kernels: 2.43 us -> 1.35 us  [shards(): pl.pallas_call(functools.partial(first_body, dims), grid=(1,), out_shape=...]
  transfers between devices with their start and end apart: 17 -> 17, of which waited for: 10 -> 10; matrix products, arithmetic and copies ran while one was open for 0% -> 0% of each run, Pallas kernels for 25% -> 15%
where the time goes in v2:
time: 81.7 us; the launch traced here: 81.2 us
  starting transfers between devices  22.1 us (27%)
  Pallas kernels  18 us (22%)
  waiting for transfers between devices  17.7 us (22%)
  blocking collectives  16.6 us (20%)
  local copies, waits for them, and re-layouts  6.06 us (7%)
    ppermute x4, waiting for transfers between devices, exchange(): west = lax.ppermute(to_east, 'lon', ring('lon', 1))  13.2 us
    ppermute x4, starting transfers between devices, exchange(): north = lax.ppermute(down, 'lat', ring('lat', -1))  10.4 us
    pallas_call x3, Pallas kernels, shards(): pl.pallas_call(functools.partial(step_body, dims), grid=(1,), out_shape=[...  9.28 us
    all_to_all x1, blocking collectives, shards(): lax.all_to_all(spread, 'lon', split_axis=0, concat_axis=0, tiled=True)  8.3 us
    all_gather x1, blocking collectives, shards(): column = lax.all_gather(across, 'lat', axis=0)  8.28 us
    all_to_all x1, starting transfers between devices, shards(): lax.all_to_all(packed.reshape(devices, CAPACITY * slots, LANES), BOTH, sp...  7.33 us
    unnamed x26, local copies, waits for them, and re-layouts  6.05 us
    ppermute x4, waiting for transfers between devices, exchange(): east = lax.ppermute(to_west, 'lon', ring('lon', -1))  3.14 us
  transfers between devices with their start and end apart: 17, of which 10 were waited for; matrix products, arithmetic and copies ran while one was open for 0% of the time, Pallas kernels for 15%

profile of v2, /device:TPU:0, one launch (start us, length us, event | category | flops | bytes accessed | tf_op | source)
XLA Modules:
  0.0 81.2 jit_solution(16708009646835404181)
XLA Ops:
  0.6 0.0 copy-start.1
  0.6 0.0 copy-start.6
  0.7 1.0 %copy-done.6 = bf16[79,1024]{1,0:T(8,128)(2,1)S(1)} copy-done((bf16[79,1024]{1,0:T(8,128)(2,1)S(1)}, bf16[79,1024]{1,0:T(8,128)(2,1)}, u32[]{:S(2)}) %copy-start.6) | copy-done | bytes 161816
  1.6 0.0 copy-start.8
  1.6 0.7 copy-done.8
  2.3 0.0 copy-start.10
  2.3 0.7 copy-done.10
  3.0 0.0 copy-start.11
  3.0 0.7 copy-done.11
  3.6 0.7 copy-done.12
  4.3 2.5 %pack.1 = bf16[1536,128]{1,0:T(8,128)(2,1)} custom-call(s32[1,128]{1,0:T(1,128)S(1)} %bitcast.13, s32[1,128]{1,0:T(1,128)S(1)} %bitcast.14, s32[1,1024]{1,0:T(1,128)S(1)} %bitcast.12, bf16[79,1024]{1,0:T(8,128)(2,1)S(1)} %copy-done.6, bf16[4,1024]{1,0:T(4,128)(2,1)S(1)} %copy-done.8), custom_call_target="tpu_custom_call" | custom-call | tf_op jit(solution)/shard_map/pack/pallas_call | solution.py:359
  6.8 7.3 %all-to-all-start = ((bf16[32,48,128]{2,1,0:T(8,128)(2,1)}), bf16[32,48,128]{2,1,0:T(8,128)(2,1)S(1)}, u32[]{:S(2)}, u32[]{:S(2)}) async-start(bf16[32,48,128]{2,1,0:T(8,128)(2,1)} %bitcast.4), calls=%async_computation | async-start | bytes 786432 | tf_op jit(solution)/shard_map/all_to_all | solution.py:371
  14.1 0.0 copy-done.1
  14.1 0.0 copy-done.7
  14.1 0.0 copy-start.2
  14.1 1.3 %copy-done.2 = f32[4,79,8,128]{3,2,1,0:T(8,128)S(1)} copy-done((f32[4,79,8,128]{3,2,1,0:T(8,128)S(1)}, f32[4,79,8,128]{3,2,1,0:T(8,128)}, u32[]{:S(2)}) %copy-start.2) | copy-done | bytes 1294360
  15.4 1.4 %first.1 = (f32[2528,128]{1,0:T(8,128)S(1)}, bf16[640,640]{1,0:T(8,128)(2,1)S(1)}, bf16[316,128]{1,0:T(8,128)(2,1)S(1)}, bf16[316,128]{1,0:T(8,128)(2,1)S(1)}, f...) custom-call(bf16[79,79]{1,0:T(8,128)(2,1)S(1)} %copy-done.7, bf16[2,79,8,128]{3,2,1,0:T(8,128)(2,1)S(1)} %copy-done.1, ...), custom_call_target="tpu_custom_call" | custom-call | tf_op jit(solution)/shard_map/first/pallas_call | solution.py:344
  16.8 2.7 %collective-permute-start = (bf16[316,128]{1,0:T(8,128)(2,1)S(1)}, bf16[316,128]{1,0:T(8,128)(2,1)S(1)}, u32[]{:S(2)}, u32[]{:S(2)}) collective-permute-start(bf16[316,128]{1,0:T(8,128)(2,1)S(1)} %get-tuple-element.29), channel_id=1, source_target_pairs={{0,24},{8,0},{16,8},{24,16},{1,25},{9,1},{17,9},{25,17},{2,26},{10... | collective-permute-start | bytes 242696 | tf_op jit(solution)/shard_map/ppermute | solution.py:301
  19.5 0.0 collective-permute-start.1
  19.5 2.8 %collective-permute-start.2 = (f32[1,2528]{1,0:T(1,128)S(1)}, f32[1,2528]{1,0:T(1,128)S(1)}, u32[]{:S(2)}, u32[]{:S(2)}) collective-permute-start(f32[1,2528]{1,0:T(1,128)S(1)} %get-tuple-element.31), channel_id=1, source_target_pairs={{0,7},{1,0},{2,1},{3,2},{4,3},{5,4},{6,5},{7,6},{8,15},{9,8},{10,9... | collective-permute-start | bytes 30344 | tf_op jit(solution)/shard_map/ppermute | solution.py:302
  22.3 0.0 collective-permute-start.3
  22.3 1.4 %collective-permute-done.2.east = f32[1,2528]{1,0:T(1,128)S(1)} collective-permute-done((f32[1,2528]{1,0:T(1,128)S(1)}, f32[1,2528]{1,0:T(1,128)S(1)}, u32[]{:S(2)}, u32[]{:S(2)}) %collective-permute-start.2) | collective-permute-done | bytes 10144 | tf_op jit(solution)/shard_map/ppermute | solution.py:302
  23.7 3.5 %collective-permute-done.3.west = f32[1,2528]{1,0:T(1,128)S(1)} collective-permute-done((f32[1,2528]{1,0:T(1,128)S(1)}, f32[1,2528]{1,0:T(1,128)S(1)}, u32[]{:S(2)}, u32[]{:S(2)}) %collective-permute-start.3) | collective-permute-done | bytes 10144 | tf_op jit(solution)/shard_map/ppermute | solution.py:303
  27.2 0.0 collective-permute-done.north
  27.2 0.0 collective-permute-done.1.south
  27.2 3.0 %step.3 = (f32[2528,128]{1,0:T(8,128)S(1)}, bf16[316,128]{1,0:T(8,128)(2,1)S(1)}, bf16[316,128]{1,0:T(8,128)(2,1)S(1)}, f32[1,2528]{1,0:T(1,128)S(1)}, f32[1,2528]{1,0:T(1,128)S(1)}, /*index=5*/f32[32,128]{1,0:T(8,128)S(1)}) custom-call(f32[2528,128]{1,0:T(8,128)S(1)} %get-tuple-element.28.mixed, bf16[316,128]{1,0:T(8,128)(2,1)S(1)} %collective-permute-done.north, ...), custom_call_target="tpu_custom_call" | custom-call | tf_op jit(solution)/shard_map/step/pallas_call | solution.py:386
  30.3 2.7 %collective-permute-start.4 = (bf16[316,128]{1,0:T(8,128)(2,1)S(1)}, bf16[316,128]{1,0:T(8,128)(2,1)S(1)}, u32[]{:S(2)}, u32[]{:S(2)}) collective-permute-start(bf16[316,128]{1,0:T(8,128)(2,1)S(1)} %get-tuple-element.35), channel_id=1, source_target_pairs={{0,24},{8,0},{16,8},{24,16},{1,25},{9,1},{17,9},{25,17},{2,26},{10... | collective-permute-start | bytes 242696 | tf_op jit(solution)/shard_map/ppermute | solution.py:301
  33.0 0.0 collective-permute-start.5
  33.0 0.0 collective-permute-start.6
  33.0 0.5 collective-permute-start.7
  33.5 0.9 %collective-permute-done.6.east = f32[1,2528]{1,0:T(1,128)S(1)} collective-permute-done((f32[1,2528]{1,0:T(1,128)S(1)}, f32[1,2528]{1,0:T(1,128)S(1)}, u32[]{:S(2)}, u32[]{:S(2)}) %collective-permute-start.6) | collective-permute-done | bytes 10144 | tf_op jit(solution)/shard_map/ppermute | solution.py:302
  34.4 3.5 %collective-permute-done.7.west = f32[1,2528]{1,0:T(1,128)S(1)} collective-permute-done((f32[1,2528]{1,0:T(1,128)S(1)}, f32[1,2528]{1,0:T(1,128)S(1)}, u32[]{:S(2)}, u32[]{:S(2)}) %collective-permute-start.7) | collective-permute-done | bytes 10144 | tf_op jit(solution)/shard_map/ppermute | solution.py:303
  37.9 0.0 collective-permute-done.4.north
  37.9 0.4 collective-permute-done.5.south
  38.3 3.1 %step.4 = (f32[2528,128]{1,0:T(8,128)S(1)}, bf16[316,128]{1,0:T(8,128)(2,1)S(1)}, bf16[316,128]{1,0:T(8,128)(2,1)S(1)}, f32[1,2528]{1,0:T(1,128)S(1)}, f32[1,2528]{1,0:T(1,128)S(1)}, /*index=5*/f32[32,128]{1,0:T(8,128)S(1)}) custom-call(f32[2528,128]{1,0:T(8,128)S(1)} %get-tuple-element.34.mixed, bf16[316,128]{1,0:T(8,128)(2,1)S(1)} %collective-permute-done.4.north, ...), custom_call_target="tpu_custom_call" | custom-call | tf_op jit(solution)/shard_map/step/pallas_call | solution.py:386
  41.4 2.5 %collective-permute-start.8 = (bf16[316,128]{1,0:T(8,128)(2,1)S(1)}, bf16[316,128]{1,0:T(8,128)(2,1)S(1)}, u32[]{:S(2)}, u32[]{:S(2)}) collective-permute-start(bf16[316,128]{1,0:T(8,128)(2,1)S(1)} %get-tuple-element.41), channel_id=1, source_target_pairs={{0,24},{8,0},{16,8},{24,16},{1,25},{9,1},{17,9},{25,17},{2,26},{10... | collective-permute-start | bytes 242696 | tf_op jit(solution)/shard_map/ppermute | solution.py:301
  43.9 0.0 collective-permute-start.9
  43.9 0.0 collective-permute-start.10
  43.9 0.5 collective-permute-start.11
  44.4 0.9 %collective-permute-done.10.east = f32[1,2528]{1,0:T(1,128)S(1)} collective-permute-done((f32[1,2528]{1,0:T(1,128)S(1)}, f32[1,2528]{1,0:T(1,128)S(1)}, u32[]{:S(2)}, u32[]{:S(2)}) %collective-permute-start.10) | collective-permute-done | bytes 10144 | tf_op jit(solution)/shard_map/ppermute | solution.py:302
  45.3 3.5 %collective-permute-done.11.west = f32[1,2528]{1,0:T(1,128)S(1)} collective-permute-done((f32[1,2528]{1,0:T(1,128)S(1)}, f32[1,2528]{1,0:T(1,128)S(1)}, u32[]{:S(2)}, u32[]{:S(2)}) %collective-permute-start.11) | collective-permute-done | bytes 10144 | tf_op jit(solution)/shard_map/ppermute | solution.py:303
  48.8 0.0 collective-permute-done.8.north
  48.8 0.4 collective-permute-done.9.south
  49.2 3.2 %step.5 = (f32[2528,128]{1,0:T(8,128)S(1)}, bf16[316,128]{1,0:T(8,128)(2,1)S(1)}, bf16[316,128]{1,0:T(8,128)(2,1)S(1)}, f32[1,2528]{1,0:T(1,128)S(1)}, f32[1,2528]{1,0:T(1,128)S(1)}, /*index=5*/f32[32,128]{1,0:T(8,128)S(1)}) custom-call(f32[2528,128]{1,0:T(8,128)S(1)} %get-tuple-element.40.mixed, bf16[316,128]{1,0:T(8,128)(2,1)S(1)} %collective-permute-done.8.north, ...), custom_call_target="tpu_custom_call" | custom-call | tf_op jit(solution)/shard_map/step/pallas_call | solution.py:386
  52.4 1.1 %copy-done.3 = f32[2528,128]{1,0:T(8,128)} copy-done((f32[2528,128]{1,0:T(8,128)}, f32[2528,128]{1,0:T(8,128)S(1)}, u32[]{:S(2)}) %copy-start.3) | copy-done | bytes 1294360
  53.5 2.5 %collective-permute-start.12 = (bf16[316,128]{1,0:T(8,128)(2,1)S(1)}, bf16[316,128]{1,0:T(8,128)(2,1)S(1)}, u32[]{:S(2)}, u32[]{:S(2)}) collective-permute-start(bf16[316,128]{1,0:T(8,128)(2,1)S(1)} %get-tuple-element.47), channel_id=1, source_target_pairs={{0,24},{8,0},{16,8},{24,16},{1,25},{9,1},{17,9},{25,17},{2,26},{10... | collective-permute-start | bytes 242696 | tf_op jit(solution)/shard_map/ppermute | solution.py:301
  56.0 0.0 collective-permute-start.13
  56.0 0.0 collective-permute-start.14
  56.0 0.5 collective-permute-start.15
  56.5 0.0 all-to-all-done
  56.5 1.7 %forcing.1 = f32[640,512]{1,0:T(8,128)S(1)} custom-call(bf16[1536,128]{1,0:T(8,128)(2,1)S(1)} %bitcast.9), custom_call_target="tpu_custom_call" | custom-call | tf_op jit(solution)/shard_map/forcing/pallas_call | solution.py:375
  58.2 0.0 collective-permute-done.14.east
  58.2 2.7 %collective-permute-done.15.west = f32[1,2528]{1,0:T(1,128)S(1)} collective-permute-done((f32[1,2528]{1,0:T(1,128)S(1)}, f32[1,2528]{1,0:T(1,128)S(1)}, u32[]{:S(2)}, u32[]{:S(2)}) %collective-permute-start.15) | collective-permute-done | bytes 10144 | tf_op jit(solution)/shard_map/ppermute | solution.py:303
  60.9 0.0 collective-permute-done.12.north
  60.9 0.4 collective-permute-done.13.south
  61.3 0.0 copy-done
  61.3 0.0 copy-done.4
  61.4 2.2 %last.1 = (f32[2528,128]{1,0:T(8,128)}, bf16[32,128]{1,0:T(8,128)(2,1)S(1)}) custom-call(f32[2528,128]{1,0:T(8,128)S(1)} %copy-done.4, bf16[316,128]{1,0:T(8,128)(2,1)S(1)} %collective-permute-done.12.north, bf16[316,128]{1,0:T(8,128)(2,1)S(1)} %collective-permute-done.13.south, f32[1,2528]{1,0:T(1,128)S(1)} %collective-permute-done.14.east, ...), custom_call_target="tpu_custom_call" | custom-call | tf_op jit(solution)/shard_map/last/pallas_call | solution.py:401
  63.6 8.3 %all_to_all.10.got = bf16[8,32,128]{2,1,0:T(8,128)(2,1)S(1)} all-to-all(bf16[8,32,128]{2,1,0:T(8,128)(2,1)S(1)} %broadcast_in_dim.10), channel_id=1, replica_groups=mesh['lat'=4,'lon'=8] {'lon'}, dimensions={0} | all-to-all | bytes 131072 | tf_op jit(solution)/shard_map/all_to_all | solution.py:415
  71.9 0.0 copy-done.5
  71.9 0.2 lon_smooth.1
  72.1 8.3 %all-gather = bf16[128,128]{1,0:T(8,128)(2,1)S(1)} all-gather(bf16[32,128]{1,0:T(8,128)(2,1)S(1)} %lon_smooth.1), channel_id=2, replica_groups=mesh['lat'=4,'lon'=8] {'lat'}, dimensions={0}, use_global_device_ids=true | all-gather | bytes 40960 | tf_op jit(solution)/shard_map/all_gather | solution.py:422
  80.4 0.0 copy-done.9
  80.4 0.8 %lat_smooth.1 = f32[32,128]{1,0:T(8,128)} custom-call(bf16[4,32,128]{2,1,0:T(8,128)(2,1)S(1)} %bitcast.11, bf16[32,32]{1,0:T(8,128)(2,1)S(1)} %copy-done.9), custom_call_target="tpu_custom_call" | custom-call | tf_op jit(solution)/shard_map/lat_smooth/pallas_call | solution.py:423
  (9 shorter events, 0.0 us)
Async XLA Ops:
  0.6 13.5 %copy-start.1 = (bf16[2,79,8,128]{3,2,1,0:T(8,128)(2,1)S(1)}, bf16[2,79,8,128]{3,2,1,0:T(8,128)(2,1)}, u32[]{:S(2)}) copy-start(bf16[2,79,8,128]{3,2,1,0:T(8,128)(2,1)} %profiles.7) | copy-start | bytes 970756
  0.6 1.0 %copy-start.6 = (bf16[79,1024]{1,0:T(8,128)(2,1)S(1)}, bf16[79,1024]{1,0:T(8,128)(2,1)}, u32[]{:S(2)}) copy-start(bf16[79,1024]{1,0:T(8,128)(2,1)} %weights.1) | copy-start | bytes 485380
  1.6 0.7 copy-start.8
  2.3 0.7 copy-start.10
  3.0 0.7 copy-start.11
  3.6 0.7 copy-start.12
  4.3 9.8 %copy-start.7 = (bf16[79,79]{1,0:T(8,128)(2,1)S(1)}, bf16[79,79]{1,0:T(8,128)(2,1)}, u32[]{:S(2)}) copy-start(bf16[79,79]{1,0:T(8,128)(2,1)} %kernel.1) | copy-start | bytes 37450
  6.8 49.7 %all-to-all-start = ((bf16[32,48,128]{2,1,0:T(8,128)(2,1)}), bf16[32,48,128]{2,1,0:T(8,128)(2,1)S(1)}, u32[]{:S(2)}, u32[]{:S(2)}) async-start(bf16[32,48,128]{2,1,0:T(8,128)(2,1)} %bitcast.4), calls=%async_computation | async-start | bytes 786432 | tf_op jit(solution)/shard_map/all_to_all | solution.py:371
  14.1 1.3 %copy-start.2 = (f32[4,79,8,128]{3,2,1,0:T(8,128)S(1)}, f32[4,79,8,128]{3,2,1,0:T(8,128)}, u32[]{:S(2)}) copy-start(f32[4,79,8,128]{3,2,1,0:T(8,128)} %param.11) | copy-start | bytes 3883012
  16.8 10.4 %collective-permute-start = (bf16[316,128]{1,0:T(8,128)(2,1)S(1)}, bf16[316,128]{1,0:T(8,128)(2,1)S(1)}, u32[]{:S(2)}, u32[]{:S(2)}) collective-permute-start(bf16[316,128]{1,0:T(8,128)(2,1)S(1)} %get-tuple-element.29), channel_id=1, source_target_pairs={{0,24},{8,0},{16,8},{24,16},{1,25},{9,1},{17,9},{25,17},{2,26},{10... | collective-permute-start | bytes 242696 | tf_op jit(solution)/shard_map/ppermute | solution.py:301
  19.5 7.7 %collective-permute-start.1 = (bf16[316,128]{1,0:T(8,128)(2,1)S(1)}, bf16[316,128]{1,0:T(8,128)(2,1)S(1)}, u32[]{:S(2)}, u32[]{:S(2)}) collective-permute-start(bf16[316,128]{1,0:T(8,128)(2,1)S(1)} %get-tuple-element.30), channel_id=1, source_target_pairs={{0,8},{8,16},{16,24},{24,0},{1,9},{9,17},{17,25},{25,1},{2,10},{10... | collective-permute-start | bytes 242696 | tf_op jit(solution)/shard_map/ppermute | solution.py:300
  19.5 4.2 %collective-permute-start.2 = (f32[1,2528]{1,0:T(1,128)S(1)}, f32[1,2528]{1,0:T(1,128)S(1)}, u32[]{:S(2)}, u32[]{:S(2)}) collective-permute-start(f32[1,2528]{1,0:T(1,128)S(1)} %get-tuple-element.31), channel_id=1, source_target_pairs={{0,7},{1,0},{2,1},{3,2},{4,3},{5,4},{6,5},{7,6},{8,15},{9,8},{10,9... | collective-permute-start | bytes 30344 | tf_op jit(solution)/shard_map/ppermute | solution.py:302
  22.3 4.9 %collective-permute-start.3 = (f32[1,2528]{1,0:T(1,128)S(1)}, f32[1,2528]{1,0:T(1,128)S(1)}, u32[]{:S(2)}, u32[]{:S(2)}) collective-permute-start(f32[1,2528]{1,0:T(1,128)S(1)} %get-tuple-element.32), channel_id=1, source_target_pairs={{0,1},{1,2},{2,3},{3,4},{4,5},{5,6},{6,7},{7,0},{8,9},{9,10},{10,1... | collective-permute-start | bytes 30344 | tf_op jit(solution)/shard_map/ppermute | solution.py:303
  30.3 7.6 %collective-permute-start.4 = (bf16[316,128]{1,0:T(8,128)(2,1)S(1)}, bf16[316,128]{1,0:T(8,128)(2,1)S(1)}, u32[]{:S(2)}, u32[]{:S(2)}) collective-permute-start(bf16[316,128]{1,0:T(8,128)(2,1)S(1)} %get-tuple-element.35), channel_id=1, source_target_pairs={{0,24},{8,0},{16,8},{24,16},{1,25},{9,1},{17,9},{25,17},{2,26},{10... | collective-permute-start | bytes 242696 | tf_op jit(solution)/shard_map/ppermute | solution.py:301
  33.0 5.3 %collective-permute-start.5 = (bf16[316,128]{1,0:T(8,128)(2,1)S(1)}, bf16[316,128]{1,0:T(8,128)(2,1)S(1)}, u32[]{:S(2)}, u32[]{:S(2)}) collective-permute-start(bf16[316,128]{1,0:T(8,128)(2,1)S(1)} %get-tuple-element.36), channel_id=1, source_target_pairs={{0,8},{8,16},{16,24},{24,0},{1,9},{9,17},{17,25},{25,1},{2,10},{10... | collective-permute-start | bytes 242696 | tf_op jit(solution)/shard_map/ppermute | solution.py:300
  33.0 1.4 %collective-permute-start.6 = (f32[1,2528]{1,0:T(1,128)S(1)}, f32[1,2528]{1,0:T(1,128)S(1)}, u32[]{:S(2)}, u32[]{:S(2)}) collective-permute-start(f32[1,2528]{1,0:T(1,128)S(1)} %get-tuple-element.37), channel_id=1, source_target_pairs={{0,7},{1,0},{2,1},{3,2},{4,3},{5,4},{6,5},{7,6},{8,15},{9,8},{10,9... | collective-permute-start | bytes 30344 | tf_op jit(solution)/shard_map/ppermute | solution.py:302
  33.0 4.9 %collective-permute-start.7 = (f32[1,2528]{1,0:T(1,128)S(1)}, f32[1,2528]{1,0:T(1,128)S(1)}, u32[]{:S(2)}, u32[]{:S(2)}) collective-permute-start(f32[1,2528]{1,0:T(1,128)S(1)} %get-tuple-element.38), channel_id=1, source_target_pairs={{0,1},{1,2},{2,3},{3,4},{4,5},{5,6},{6,7},{7,0},{8,9},{9,10},{10,1... | collective-permute-start | bytes 30344 | tf_op jit(solution)/shard_map/ppermute | solution.py:303
  41.4 7.4 %collective-permute-start.8 = (bf16[316,128]{1,0:T(8,128)(2,1)S(1)}, bf16[316,128]{1,0:T(8,128)(2,1)S(1)}, u32[]{:S(2)}, u32[]{:S(2)}) collective-permute-start(bf16[316,128]{1,0:T(8,128)(2,1)S(1)} %get-tuple-element.41), channel_id=1, source_target_pairs={{0,24},{8,0},{16,8},{24,16},{1,25},{9,1},{17,9},{25,17},{2,26},{10... | collective-permute-start | bytes 242696 | tf_op jit(solution)/shard_map/ppermute | solution.py:301
  43.9 5.3 %collective-permute-start.9 = (bf16[316,128]{1,0:T(8,128)(2,1)S(1)}, bf16[316,128]{1,0:T(8,128)(2,1)S(1)}, u32[]{:S(2)}, u32[]{:S(2)}) collective-permute-start(bf16[316,128]{1,0:T(8,128)(2,1)S(1)} %get-tuple-element.42), channel_id=1, source_target_pairs={{0,8},{8,16},{16,24},{24,0},{1,9},{9,17},{17,25},{25,1},{2,10},{10... | collective-permute-start | bytes 242696 | tf_op jit(solution)/shard_map/ppermute | solution.py:300
  43.9 1.4 %collective-permute-start.10 = (f32[1,2528]{1,0:T(1,128)S(1)}, f32[1,2528]{1,0:T(1,128)S(1)}, u32[]{:S(2)}, u32[]{:S(2)}) collective-permute-start(f32[1,2528]{1,0:T(1,128)S(1)} %get-tuple-element.43), channel_id=1, source_target_pairs={{0,7},{1,0},{2,1},{3,2},{4,3},{5,4},{6,5},{7,6},{8,15},{9,8},{10,9... | collective-permute-start | bytes 30344 | tf_op jit(solution)/shard_map/ppermute | solution.py:302
  43.9 4.9 %collective-permute-start.11 = (f32[1,2528]{1,0:T(1,128)S(1)}, f32[1,2528]{1,0:T(1,128)S(1)}, u32[]{:S(2)}, u32[]{:S(2)}) collective-permute-start(f32[1,2528]{1,0:T(1,128)S(1)} %get-tuple-element.44), channel_id=1, source_target_pairs={{0,1},{1,2},{2,3},{3,4},{4,5},{5,6},{6,7},{7,0},{8,9},{9,10},{10,1... | collective-permute-start | bytes 30344 | tf_op jit(solution)/shard_map/ppermute | solution.py:303
  49.2 12.1 %copy-start = (bf16[4,4,79,8,128]{4,3,2,1,0:T(8,128)(2,1)S(1)}, bf16[4,4,79,8,128]{4,3,2,1,0:T(8,128)(2,1)}, u32[]{:S(2)}) copy-start(bf16[4,4,79,8,128]{4,3,2,1,0:T(8,128)(2,1)} %fraction.7) | copy-start | bytes 7766020
  52.4 1.1 %copy-start.3 = (f32[2528,128]{1,0:T(8,128)}, f32[2528,128]{1,0:T(8,128)S(1)}, u32[]{:S(2)}) copy-start(f32[2528,128]{1,0:T(8,128)S(1)} %get-tuple-element.46.mixed) | copy-start | bytes 3883012
  53.5 7.4 %collective-permute-start.12 = (bf16[316,128]{1,0:T(8,128)(2,1)S(1)}, bf16[316,128]{1,0:T(8,128)(2,1)S(1)}, u32[]{:S(2)}, u32[]{:S(2)}) collective-permute-start(bf16[316,128]{1,0:T(8,128)(2,1)S(1)} %get-tuple-element.47), channel_id=1, source_target_pairs={{0,24},{8,0},{16,8},{24,16},{1,25},{9,1},{17,9},{25,17},{2,26},{10... | collective-permute-start | bytes 242696 | tf_op jit(solution)/shard_map/ppermute | solution.py:301
  56.0 5.3 %collective-permute-start.13 = (bf16[316,128]{1,0:T(8,128)(2,1)S(1)}, bf16[316,128]{1,0:T(8,128)(2,1)S(1)}, u32[]{:S(2)}, u32[]{:S(2)}) collective-permute-start(bf16[316,128]{1,0:T(8,128)(2,1)S(1)} %get-tuple-element.48), channel_id=1, source_target_pairs={{0,8},{8,16},{16,24},{24,0},{1,9},{9,17},{17,25},{25,1},{2,10},{10... | collective-permute-start | bytes 242696 | tf_op jit(solution)/shard_map/ppermute | solution.py:300
  56.0 2.2 %collective-permute-start.14 = (f32[1,2528]{1,0:T(1,128)S(1)}, f32[1,2528]{1,0:T(1,128)S(1)}, u32[]{:S(2)}, u32[]{:S(2)}) collective-permute-start(f32[1,2528]{1,0:T(1,128)S(1)} %get-tuple-element.49), channel_id=1, source_target_pairs={{0,7},{1,0},{2,1},{3,2},{4,3},{5,4},{6,5},{7,6},{8,15},{9,8},{10,9... | collective-permute-start | bytes 30344 | tf_op jit(solution)/shard_map/ppermute | solution.py:302
  56.0 4.9 %collective-permute-start.15 = (f32[1,2528]{1,0:T(1,128)S(1)}, f32[1,2528]{1,0:T(1,128)S(1)}, u32[]{:S(2)}, u32[]{:S(2)}) collective-permute-start(f32[1,2528]{1,0:T(1,128)S(1)} %get-tuple-element.50), channel_id=1, source_target_pairs={{0,1},{1,2},{2,3},{3,4},{4,5},{5,6},{6,7},{7,0},{8,9},{9,10},{10,1... | collective-permute-start | bytes 30344 | tf_op jit(solution)/shard_map/ppermute | solution.py:303
  56.5 4.8 %copy-start.4 = (f32[2528,128]{1,0:T(8,128)S(1)}, f32[2528,128]{1,0:T(8,128)}, u32[]{:S(2)}) copy-start(f32[2528,128]{1,0:T(8,128)} %copy-done.3) | copy-start | bytes 3883012
  61.3 10.5 %copy-start.5 = (bf16[128,1024]{1,0:T(8,128)(2,1)S(1)}, bf16[128,1024]{1,0:T(8,128)(2,1)}, u32[]{:S(2)}) copy-start(bf16[128,1024]{1,0:T(8,128)(2,1)} %matrix.2) | copy-start | bytes 786436
  61.3 19.0 %copy-start.9 = (bf16[32,32]{1,0:T(8,128)(2,1)S(1)}, bf16[32,32]{1,0:T(8,128)(2,1)}, u32[]{:S(2)}) copy-start(bf16[32,32]{1,0:T(8,128)(2,1)} %matrix.3) | copy-start | bytes 6148

commit v3 on v2

--- a/solution.py
+++ b/solution.py
@@ -65,6 +65,22 @@
     over_levels(levels, body)
 
 
+def end_columns(rows_2d):
+    lane = iota((8, LANES), 1)
+    sub = iota((8, LANES), 0)
+    pick = ((sub == 0) & (lane == 0)) | ((sub == 1) & (lane == LANES - 1))
+    return dot_nt(pick.astype(BF16), rows_2d.astype(BF16))
+
+
+def spread_columns(first, last):
+    lane = iota((8, LANES), 1)
+    sub = iota((8, first.shape[1]), 0)
+    got = jnp.where(sub == 0, last, jnp.where(sub == 1, first, 0.0)).astype(BF16)
+    sub = iota((8, LANES), 0)
+    place = (((sub == 0) & (lane == LANES - 1)) | ((sub == 1) & (lane == 0))).astype(BF16)
+    return dot_tn(got, place)
+
+
 def send_edges(dims, mixed, up, down, west, east):
     tracers, levels, rows = dims
     count = tracers * levels
@@ -72,14 +88,11 @@
     last = lax.axis_size("lat") - 1
     first_row = mixed[pl.ds(0, count, stride=rows), :]
     last_row = mixed[pl.ds(rows - 1, count, stride=rows), :]
-    up[...] = jnp.where(lat < last, last_row, 0.0).astype(BF16)
-    down[...] = jnp.where(lat > 0, first_row, 0.0).astype(BF16)
-    lane = iota((rows, LANES), 1)
-    sub = iota((rows, LANES), 0)
-    pick = ((sub == 0) & (lane == 0)) | ((sub == 1) & (lane == LANES - 1))
-    sides = dot_nt(pick.astype(BF16), mixed[...].astype(BF16))
-    west[...] = sides[0:1]
-    east[...] = sides[1:2]
+    up[0:count, :] = jnp.where(lat < last, last_row, 0.0).astype(BF16)
+    down[0:count, :] = jnp.where(lat > 0, first_row, 0.0).astype(BF16)
+    sides = end_columns(mixed[...])
+    west[:, 0 : count * rows] = sides[0:1]
+    east[:, 0 : count * rows] = sides[1:2]
 
 
 def store_low(low, k2, rows, t, parts):
@@ -95,7 +108,7 @@
         body(levels // 2, (levels - 1,))
 
 
-def first_body(dims, kernel, profiles, adjoint, mixed, kron, up, down, west, east, low, mix):
+def first_body(dims, kernel, profiles, adjoint, fraction, mixed, kron, up, down, west, east, low, mix):
     tracers, levels, rows = dims
     kron[...] = expand_kernel(kernel[...], levels, low.shape[0] // rows, rows)
 
@@ -110,19 +123,24 @@
     over_levels(levels, body)
     convect(dims, adjoint, low, mix, kron, profiles, mixed)
     send_edges(dims, mixed, up, down, west, east)
+    count = tracers * levels
+    lat = lax.axis_index("lat")
+    last = lax.axis_size("lat") - 1
+    f = [fraction[0, d, 0].astype(F32) for d in range(4)]
+    pad = jnp.zeros((up.shape[0] - count - 1, LANES), F32)
+    up[count:, :] = jnp.concatenate([jnp.where(lat < last, f[2][rows - 1 :], 0.0), pad], axis=0).astype(BF16)
+    down[count:, :] = jnp.concatenate([jnp.where(lat > 0, f[3][:1], 0.0), pad], axis=0).astype(BF16)
+    at = (count * rows + LANES - 1) // LANES * LANES
+    west[:, at : at + tracers * rows] = end_columns(jnp.concatenate([f[1]] * tracers, axis=0))[0:1]
+    east[:, at : at + tracers * rows] = end_columns(jnp.concatenate([f[0]] * tracers, axis=0))[1:2]
 
 
 def unpack_halo(dims, north, south, east, west, north_scr, south_scr, sides):
     tracers, levels, rows = dims
     count = tracers * levels
-    north_scr[0:count, :] = north[...].astype(F32)
-    south_scr[0:count, :] = south[...].astype(F32)
-    sub = iota((rows, count * rows), 0)
-    got = jnp.where(sub == 0, east[...], jnp.where(sub == 1, west[...], 0.0)).astype(BF16)
-    lane = iota((rows, LANES), 1)
-    sub = iota((rows, LANES), 0)
-    place = (((sub == 0) & (lane == LANES - 1)) | ((sub == 1) & (lane == 0))).astype(BF16)
-    sides[...] = dot_tn(got, place)
+    north_scr[0:count, :] = north[0:count, :].astype(F32)
+    south_scr[0:count, :] = south[0:count, :].astype(F32)
+    sides[...] = spread_columns(west[:, 0 : count * rows], east[:, 0 : count * rows])
 
 
 def transport(dims, k, fraction, mixed, north_scr, south_scr, sides):
@@ -151,7 +169,9 @@
     return out
 
 
-def step_body(dims, mixed, north, south, east, west, fraction, profiles, kron, surface, *rest):
+def step_body(dims, last, mixed, north, south, east, west, fraction, profiles, kron, surface, *rest):
+    if last:
+        extra, rest = rest[:6], rest[6:]
     new_mixed, up, down, to_west, to_east, new_surface, north_scr, south_scr, sides, adj, low, mix = rest
     tracers, levels, rows = dims
     unpack_halo(dims, north, south, east, west, north_scr, south_scr, sides)
@@ -170,13 +190,53 @@
     over_levels(levels, body)
     convect(dims, adj, low, mix, kron, profiles, new_mixed)
     send_edges(dims, new_mixed, up, down, to_west, to_east)
+    total = [
+        surface[t * rows : (t + 1) * rows, :] + adj[t * levels * rows : t * levels * rows + rows, :]
+        for t in range(tracers)
+    ]
+    if last:
+        patch(dims, new_mixed, total, *extra, new_surface)
+    else:
+        new_surface[...] = jnp.concatenate(total, axis=0)
+
+
+def patch(dims, mixed, total, fraction, forcing, north, south, east, west, out):
+    tracers, levels, rows = dims
+    count = tracers * levels
+    f = [fraction[0, d, 0].astype(F32) for d in range(4)]
+    remain = 1.0 - f[0] - f[1] - f[2] - f[3]
+    lane = iota((rows, LANES), 1)
+    sub = iota((rows, LANES), 0)
+    below = south[count : count + 8, :].astype(F32)[0:1]
+    above = north[count : count + 8, :].astype(F32)[0:1]
+    tile, under, over = [], [], []
     for t in range(tracers):
-        at = t * levels * rows
-        new_surface[t * rows : (t + 1) * rows, :] = surface[t * rows : (t + 1) * rows, :] + adj[at : at + rows, :]
-
-
-def last_body(dims, mixed, north, south, east, west, fraction, forcing, surface, *rest):
-    adjoint, surface_low, north_scr, south_scr, sides = rest
+        m = mixed[t * levels * rows : t * levels * rows + rows, :]
+        value = remain * m
+        value = value + f[0] * jnp.where(lane == LANES - 1, 0.0, pltpu.roll(m, LANES - 1, 1))
+        value = value + f[1] * jnp.where(lane == 0, 0.0, pltpu.roll(m, 1, 1))
+        value = value + f[2] * jnp.where(sub == rows - 1, 0.0, pltpu.roll(m, rows - 1, 0))
+        value = value + f[3] * jnp.where(sub == 0, 0.0, pltpu.roll(m, 1, 0))
+        tile.append(total[t] + value + forcing[0:rows, t * LANES : (t + 1) * LANES])
+        under.append(below * m[0:1])
+        over.append(above * m[rows - 1 : rows])
+    tops = jnp.concatenate([mixed[t * levels * rows : t * levels * rows + rows, :] for t in range(tracers)], axis=0)
+    columns = end_columns(tops)
+    at = (count * rows + LANES - 1) // LANES * LANES
+    size = tracers * rows
+    to_west = columns[0:1] * west[:, at : at + size]
+    to_east = columns[1:2] * east[:, at : at + size]
+    ends = jnp.concatenate([to_west, to_east, jnp.zeros((6, size), F32)], axis=0)
+    ends = jnp.concatenate([ends, jnp.zeros((8, LANES - size), F32)], axis=1)
+    short = (-2 * tracers) % 8
+    filler = [jnp.zeros((short, LANES), F32)] if short else []
+    whole = jnp.concatenate(tile + under + over + filler + [ends], axis=0)
+    for z in range(out.shape[0]):
+        out[z] = whole.astype(BF16)
+
+
+def last_body(dims, mixed, north, south, east, west, fraction, forcing, *rest):
+    adjoint, north_scr, south_scr, sides = rest
     tracers, levels, rows = dims
     unpack_halo(dims, north, south, east, west, north_scr, south_scr, sides)
 
@@ -187,10 +247,6 @@
                 adjoint[at, :] = value + forcing[pl.ds(start, rows), t * LANES : (t + 1) * LANES]
 
     over_levels(levels, body)
-    for t in range(tracers):
-        at = t * levels * rows
-        total = surface[t * rows : (t + 1) * rows, :] + adjoint[at : at + rows, :]
-        surface_low[t * rows : (t + 1) * rows, :] = total.astype(BF16)
 
 
 def pack_body(sizes, owner, count, cols, weights, resid, out):
@@ -266,28 +322,39 @@
     lax.fori_loop(0, got.shape[0] // chunk, body, 0)
 
 
-def lon_body(got, matrix, out):
+def lon_body(size, got, matrix, out):
     count = got.shape[0]
+    body = out.shape[0]
     total = jnp.zeros(out.shape, F32)
+    ends = [got[z, body : body + 8, :].astype(F32)[:, 0:size] for z in range(count)]
     for z in range(count):
-        total = total + dot_nt(got[z], matrix[:, z * LANES : (z + 1) * LANES])
+        side = spread_columns(ends[(z - 1) % count][1:2], ends[(z + 1) % count][0:1])
+        block = got[z, 0:body, :].astype(F32)
+        block = jnp.concatenate([block[0:size] + side, block[size:]], axis=0)
+        total = total + dot_nt(block.astype(BF16), matrix[:, z * LANES : (z + 1) * LANES])
     out[...] = total.astype(BF16)
 
 
 def lat_body(tracers, rows, got, matrix, out):
     bands = got.shape[0]
     size = tracers * rows
+    extra = got.shape[1] - size
     lat = lax.axis_index("lat")
-    own = matrix[pl.ds(aligned(lat * rows, rows), rows), :]
+    own = matrix[pl.ds(pl.multiple_of(lat * rows, rows), rows), :].astype(F32)
     own = jnp.concatenate([own] * tracers, axis=0)
+    tracer = iota((size, extra), 0) // rows
+    column = iota((size, extra), 1)
+    same = iota((size, size), 0) // rows == iota((size, size), 1) // rows
     total = jnp.zeros(out.shape, F32)
     for b in range(bands):
-        block = own[:, b * rows : (b + 1) * rows]
-        block = jnp.concatenate([block] * tracers, axis=1)
-        same = iota((size, size), 0) // rows == iota((size, size), 1) // rows
-        total = total + jnp.dot(
-            jnp.where(same, block, 0.0).astype(BF16), got[b], preferred_element_type=F32
-        )
+        block = jnp.concatenate([own[:, b * rows : (b + 1) * rows]] * tracers, axis=1)
+        block = jnp.where(same, block, 0.0)
+        under = max(b * rows - 1, 0)
+        over = min((b + 1) * rows, bands * rows - 1)
+        ring_part = jnp.where(column == tracer, own[:, under : under + 1], 0.0)
+        ring_part = ring_part + jnp.where(column == tracer + tracers, own[:, over : over + 1], 0.0)
+        weights = jnp.concatenate([block, ring_part], axis=1).astype(BF16)
+        total = total + jnp.dot(weights, got[b], preferred_element_type=F32)
     out[...] = total
 
 
@@ -328,6 +395,10 @@
     row_edge = jax.ShapeDtypeStruct((count, LANES), BF16)
     side_edge = jax.ShapeDtypeStruct((1, cells), F32)
     edges = [row_edge, row_edge, side_edge, side_edge]
+    long_row = jax.ShapeDtypeStruct((count + 16, LANES), BF16)
+    long_side = jax.ShapeDtypeStruct((1, (cells + LANES - 1) // LANES * LANES + LANES), F32)
+    long_edges = [long_row, long_row, long_side, long_side]
+    level_zero = pl.BlockSpec((1, 4, 1, rows, LANES), lambda i: (0, 0, 0, 0, 0))
     kron_type = jax.ShapeDtypeStruct((padded * rows, padded * rows), BF16)
     surface_type = jax.ShapeDtypeStruct((tracers * rows, LANES), F32)
     low_scr = pltpu.VMEM((padded * rows, wide), BF16)
@@ -344,22 +415,32 @@
     mixed, kron, *out = pl.pallas_call(
         functools.partial(first_body, dims),
         grid=(1,),
-        out_shape=[state, kron_type] + edges,
-        in_specs=[full(kernel.shape), full(profiles.shape), spec(state)],
-        out_specs=[spec(s) for s in [state, kron_type] + edges],
+        out_shape=[state, kron_type] + long_edges,
+        in_specs=[full(kernel.shape), full(profiles.shape), spec(state), level_zero],
+        out_specs=[spec(s) for s in [state, kron_type] + long_edges],
         scratch_shapes=[low_scr, mix_scr],
         compiler_params=params(),
         name="first",
-    )(kernel, profiles, adjoint_in.reshape(cells, LANES))
-    halo = exchange(*out)
+    )(kernel, profiles, adjoint_in.reshape(cells, LANES), fractions)
+    halo = first_halo = exchange(*out)
+    obs_count, _ = lax.optimization_barrier((obs_count, out[2]))
 
     blocks = obs_count.shape[0]
     slots = obs_cols.shape[0] // blocks
     rows_out = devices * CAPACITY * slots
     packed = pl.pallas_call(
         functools.partial(pack_body, (devices, blocks, slots, levels, tracers, 8 * CAPACITY * slots)),
+        grid=(1,),
         out_shape=jax.ShapeDtypeStruct((rows_out, LANES), BF16),
-        compiler_params=params(),
+        in_specs=[
+            full((1, blocks)),
+            full((1, blocks)),
+            full((1, blocks * slots)),
+            full(obs_weights.shape),
+            full(obs_resid.shape),
+        ],
+        out_specs=full((rows_out, LANES)),
+        compiler_params=params(60 << 20),
         name="pack",
     )(
         obs_owner.reshape(1, blocks),
@@ -381,41 +462,49 @@
     )(got.reshape(rows_out, LANES))
 
     surface = jnp.zeros(surface_type.shape, F32)
+    lon_count = lax.axis_size("lon")
+    patch_rows = (tracers * (rows + 2) + 7) // 8 * 8
+    patch_type = jax.ShapeDtypeStruct((lon_count, patch_rows + 8, LANES), BF16)
     for step_index in range(STEPS - 1, 0, -1):
+        last = step_index == 1
         frac_spec = pl.BlockSpec((1,) + fractions.shape[1:], lambda i, n=step_index: (n, 0, 0, 0, 0))
+        halo_types = long_edges if step_index == STEPS - 1 else edges
+        ins = [mixed, *halo, fractions, profiles, kron, surface]
+        in_specs = [spec(state)] + [spec(h) for h in halo_types]
+        in_specs += [frac_spec, full(profiles.shape), spec(kron_type), spec(surface_type)]
+        result = surface_type
+        if last:
+            ins += [fractions, forcing, *first_halo]
+            in_specs += [level_zero, pl.BlockSpec((rows, wide), lambda i: (0, 0))] + [spec(h) for h in long_edges]
+            result = patch_type
         mixed, *out, surface = pl.pallas_call(
-            functools.partial(step_body, dims),
+            functools.partial(step_body, dims, last),
             grid=(1,),
-            out_shape=[state] + edges + [surface_type],
-            in_specs=[spec(state), spec(row_edge), spec(row_edge), spec(side_edge), spec(side_edge)]
-            + [frac_spec, full(profiles.shape), spec(kron_type), spec(surface_type)],
-            out_specs=[spec(s) for s in [state] + edges + [surface_type]],
+            out_shape=[state] + edges + [result],
+            in_specs=in_specs,
+            out_specs=[spec(s) for s in [state] + edges + [result]],
             scratch_shapes=halo_scr + [pltpu.VMEM((cells, LANES), F32), low_scr, mix_scr],
             compiler_params=params(),
             name="step",
-        )(mixed, *halo, fractions, profiles, kron, surface)
+        )(*ins)
         halo = exchange(*out)
 
+    band = lax.all_to_all(surface, "lon", split_axis=0, concat_axis=0, tiled=True)
     frac_spec = pl.BlockSpec((1,) + fractions.shape[1:], lambda i: (0, 0, 0, 0, 0))
-    low_type = jax.ShapeDtypeStruct(surface_type.shape, BF16)
-    adjoint, surface_low = pl.pallas_call(
+    adjoint = pl.pallas_call(
         functools.partial(last_body, dims),
         grid=(1,),
-        out_shape=[state, low_type],
-        in_specs=[spec(state), spec(row_edge), spec(row_edge), spec(side_edge), spec(side_edge)]
-        + [frac_spec, full(forcing.shape), spec(surface_type)],
-        out_specs=[spec(state), spec(low_type)],
+        out_shape=state,
+        in_specs=[spec(state)] + [spec(h) for h in edges] + [frac_spec, full(forcing.shape)],
+        out_specs=spec(state),
         scratch_shapes=halo_scr,
         compiler_params=params(),
         name="last",
-    )(mixed, *halo, fractions, forcing, surface)
-
-    lon_count = lax.axis_size("lon")
-    spread = jnp.broadcast_to(surface_low[None], (lon_count,) + surface_low.shape)
-    band = lax.all_to_all(spread, "lon", split_axis=0, concat_axis=0, tiled=True)
+    )(mixed, *halo, fractions, forcing)
+
     across = pl.pallas_call(
-        lon_body,
-        out_shape=low_type,
+        functools.partial(lon_body, tracers * rows),
+        out_shape=jax.ShapeDtypeStruct((patch_rows, LANES), BF16),
         compiler_params=params(),
         name="lon_smooth",
     )(band, lon_matrix)

time: 81.7 us -> 97.1 us (1.19)
  local copies, waits for them, and re-layouts: 6.06 us -> 19.5 us
  blocking collectives: 16.6 us -> 8.54 us
  starting transfers between devices: 22.1 us -> 29.8 us
  Pallas kernels: 18 us -> 20.3 us
    unnamed x26 -> x58, local copies, waits for them, and re-layouts: 6.05 us -> 19.4 us
    all_to_all x1 -> x0, blocking collectives: 8.3 us -> none  [shards(): lax.all_to_all(spread, 'lon', split_axis=0, concat_axis=0, tiled=True)]
    ppermute x4, starting transfers between devices: 2.82 us -> 9.23 us  [exchange(): east = lax.ppermute(to_west, 'lon', ring('lon', -1))]
    all_to_all x0 -> x1, starting transfers between devices: none -> 3.36 us  [shards(): lax.all_to_all(surface, 'lon', split_axis=0, concat_axis=0, tiled=True)]
    ppermute x4, starting transfers between devices: 10.4 us -> 8.83 us  [exchange(): north = lax.ppermute(down, 'lat', ring('lat', -1))]
    ppermute x4, waiting for transfers between devices: 1.3 us -> 0.28 us  [exchange(): south = lax.ppermute(up, 'lat', ring('lat', 1))]
    ppermute x4, starting transfers between devices: 1.52 us -> 0.52 us  [exchange(): west = lax.ppermute(to_east, 'lon', ring('lon', 1))]
    pallas_call x1, Pallas kernels: 2.48 us -> 3.47 us  [shards(): pl.pallas_call(functools.partial(pack_body, (devices, blocks, slots, leve...]
  transfers between devices with their start and end apart: 17 -> 18, of which waited for: 10 -> 7; matrix products, arithmetic and copies ran while one was open for 0% -> 0% of each run, Pallas kernels for 15% -> 10%
where the time goes in v3:
time: 97.1 us; the launch traced here: 96.3 us
  starting transfers between devices  29.8 us (31%)
  Pallas kernels  20.3 us (21%)
  local copies, waits for them, and re-layouts  19.5 us (20%)
  waiting for transfers between devices  17.4 us (18%)
  blocking collectives  8.54 us (9%)
    unnamed x58, local copies, waits for them, and re-layouts  19.4 us
    ppermute x4, waiting for transfers between devices, exchange(): west = lax.ppermute(to_east, 'lon', ring('lon', 1))  14.1 us
    ppermute x4, starting transfers between devices, exchange(): east = lax.ppermute(to_west, 'lon', ring('lon', -1))  9.23 us
    pallas_call x3, Pallas kernels, shards(): pl.pallas_call(functools.partial(step_body, dims, last), grid=(1,), out_s...  9.21 us
    ppermute x4, starting transfers between devices, exchange(): north = lax.ppermute(down, 'lat', ring('lat', -1))  8.83 us
    all_gather x1, blocking collectives, shards(): column = lax.all_gather(across, 'lat', axis=0)  8.54 us
    all_to_all x1, starting transfers between devices, shards(): lax.all_to_all(packed.reshape(devices, CAPACITY * slots, LANES), BOTH, sp...  7.33 us
    pallas_call x1, Pallas kernels, shards(): pl.pallas_call(functools.partial(pack_body, (devices, blocks, slots, leve...  3.47 us
  transfers between devices with their start and end apart: 18, of which 7 were waited for; matrix products, arithmetic and copies ran while one was open for 0% of the time, Pallas kernels for 10%

profile of v3, /device:TPU:0, one launch (start us, length us, event | category | flops | bytes accessed | tf_op | source)
XLA Modules:
  0.0 96.3 jit_solution(8469340193469096972)
XLA Ops:
  0.6 0.0 copy-start.3
  0.6 1.0 %copy-done.3 = bf16[2,79,8,128]{3,2,1,0:T(8,128)(2,1)S(1)} copy-done((bf16[2,79,8,128]{3,2,1,0:T(8,128)(2,1)S(1)}, bf16[2,79,8,128]{3,2,1,0:T(8,128)(2,1)}, u32[]{:S(2)}) %copy-start.3) | copy-done | bytes 323608
  1.6 1.3 %copy-done.6 = f32[4,79,8,128]{3,2,1,0:T(8,128)S(1)} copy-done((f32[4,79,8,128]{3,2,1,0:T(8,128)S(1)}, f32[4,79,8,128]{3,2,1,0:T(8,128)}, u32[]{:S(2)}) %copy-start.6) | copy-done | bytes 1294360
  2.9 0.7 copy-done.21
  3.6 2.0 %first.1 = (f32[2528,128]{1,0:T(8,128)S(1)}, bf16[640,640]{1,0:T(8,128)(2,1)S(1)}, bf16[332,128]{1,0:T(8,128)(2,1)S(1)}, bf16[332,128]{1,0:T(8,128)(2,1)S(1)}, f...) custom-call(bf16[79,79]{1,0:T(8,128)(2,1)S(1)} %copy-done.21, bf16[2,79,8,128]{3,2,1,0:T(8,128)(2,1)S(1)} %copy-done.3, ...), custom_call_target="tpu_custom_call" | custom-call | tf_op jit(solution)/shard_map/first/pallas_call | solution.py:415
  5.7 1.1 %copy-done.9 = f32[2528,128]{1,0:T(8,128)} copy-done((f32[2528,128]{1,0:T(8,128)}, f32[2528,128]{1,0:T(8,128)S(1)}, u32[]{:S(2)}) %copy-start.9) | copy-done | bytes 1294360
  6.8 3.5 %pack.1 = bf16[1536,128]{1,0:T(8,128)(2,1)} custom-call(s32[1,128]{1,0:T(1,128)} %bitcast.16, s32[1,128]{1,0:T(1,128)} %bitcast.17, s32[1,1024]{1,0:T(1,128)} %bitcast.15, bf16[79,1024]{1,0:T(8,128)(2,1)} %weights.1, bf16[4,1024]{1,0:T(4,128)(2,1)} %resid.1), custom_call_target="tpu_custom_call" | custom-call | tf_op jit(solution)/shard_map/pack/pallas_call | solution.py:431
  10.2 7.3 %all-to-all-start = ((bf16[32,48,128]{2,1,0:T(8,128)(2,1)}), bf16[32,48,128]{2,1,0:T(8,128)(2,1)S(1)}, u32[]{:S(2)}, u32[]{:S(2)}) async-start(bf16[32,48,128]{2,1,0:T(8,128)(2,1)} %bitcast.12), calls=%async_computation | async-start | bytes 786432 | tf_op jit(solution)/shard_map/all_to_all | solution.py:452
  17.6 2.7 %collective-permute-start = (bf16[332,128]{1,0:T(8,128)(2,1)S(1)}, bf16[332,128]{1,0:T(8,128)(2,1)S(1)}, u32[]{:S(2)}, u32[]{:S(2)}) collective-permute-start(bf16[332,128]{1,0:T(8,128)(2,1)S(1)} %get-tuple-element.28), channel_id=1, source_target_pairs={{0,24},{8,0},{16,8},{24,16},{1,25},{9,1},{17,9},{25,17},{2,26},{10... | collective-permute-start | bytes 254984 | tf_op jit(solution)/shard_map/ppermute | solution.py:368
  20.3 0.0 collective-permute-start.1
  20.3 0.0 collective-permute-start.3
  20.3 3.5 %collective-permute-start.2 = (f32[1,2688]{1,0:T(1,128)S(1)}, f32[1,2688]{1,0:T(1,128)S(1)}, u32[]{:S(2)}, u32[]{:S(2)}) collective-permute-start(f32[1,2688]{1,0:T(1,128)S(1)} %get-tuple-element.30), channel_id=1, source_target_pairs={{0,7},{1,0},{2,1},{3,2},{4,3},{5,4},{6,5},{7,6},{8,15},{9,8},{10,9... | collective-permute-start | bytes 32264 | tf_op jit(solution)/shard_map/ppermute | solution.py:369
  23.8 4.4 %collective-permute-done.3.west.rest_5_ = f32[1,2688]{1,0:T(1,128)S(1)} collective-permute-done((f32[1,2688]{1,0:T(1,128)S(1)}, f32[1,2688]{1,0:T(1,128)S(1)}, u32[]{:S(2)}, u32[]{:S(2)}) %collective-permute-start.3) | collective-permute-done | bytes 10784 | tf_op jit(solution)/shard_map/ppermute | solution.py:370
  28.2 0.0 collective-permute-done.2.east.rest_4_
  28.2 0.0 collective-permute-done.north.rest_2_
  28.2 0.3 collective-permute-done.1.south.rest_3_
  28.5 1.3 %copy-done.10 = f32[2528,128]{1,0:T(8,128)S(1)} copy-done((f32[2528,128]{1,0:T(8,128)S(1)}, f32[2528,128]{1,0:T(8,128)}, u32[]{:S(2)}) %copy-start.10) | copy-done | bytes 1294360
  29.9 3.0 %step.3 = (f32[2528,128]{1,0:T(8,128)S(1)}, bf16[316,128]{1,0:T(8,128)(2,1)S(1)}, bf16[316,128]{1,0:T(8,128)(2,1)S(1)}, f32[1,2528]{1,0:T(1,128)S(1)}, f32[1,2528]{1,0:T(1,128)S(1)}, /*index=5*/f32[32,128]{1,0:T(8,128)S(1)}) custom-call(f32[2528,128]{1,0:T(8,128)S(1)} %copy-done.10, bf16[332,128]{1,0:T(8,128)(2,1)S(1)} %collective-permute-done.north.rest_2_, ...), custom_call_target="tpu_custom_call" | custom-call | tf_op jit(solution)/shard_map/step/pallas_call | solution.py:480
  32.9 2.2 %collective-permute-start.4 = (bf16[316,128]{1,0:T(8,128)(2,1)S(1)}, bf16[316,128]{1,0:T(8,128)(2,1)S(1)}, u32[]{:S(2)}, u32[]{:S(2)}) collective-permute-start(bf16[316,128]{1,0:T(8,128)(2,1)S(1)} %get-tuple-element.34), channel_id=1, source_target_pairs={{0,24},{8,0},{16,8},{24,16},{1,25},{9,1},{17,9},{25,17},{2,26},{10... | collective-permute-start | bytes 242696 | tf_op jit(solution)/shard_map/ppermute | solution.py:368
  35.1 0.0 collective-permute-start.5
  35.1 2.5 %collective-permute-start.6 = (f32[1,2528]{1,0:T(1,128)S(1)}, f32[1,2528]{1,0:T(1,128)S(1)}, u32[]{:S(2)}, u32[]{:S(2)}) collective-permute-start(f32[1,2528]{1,0:T(1,128)S(1)} %get-tuple-element.36), channel_id=1, source_target_pairs={{0,7},{1,0},{2,1},{3,2},{4,3},{5,4},{6,5},{7,6},{8,15},{9,8},{10,9... | collective-permute-start | bytes 30344 | tf_op jit(solution)/shard_map/ppermute | solution.py:369
  37.6 0.0 collective-permute-start.7
  37.6 1.4 %collective-permute-done.6.east = f32[1,2528]{1,0:T(1,128)S(1)} collective-permute-done((f32[1,2528]{1,0:T(1,128)S(1)}, f32[1,2528]{1,0:T(1,128)S(1)}, u32[]{:S(2)}, u32[]{:S(2)}) %collective-permute-start.6) | collective-permute-done | bytes 10144 | tf_op jit(solution)/shard_map/ppermute | solution.py:369
  39.0 3.5 %collective-permute-done.7.west = f32[1,2528]{1,0:T(1,128)S(1)} collective-permute-done((f32[1,2528]{1,0:T(1,128)S(1)}, f32[1,2528]{1,0:T(1,128)S(1)}, u32[]{:S(2)}, u32[]{:S(2)}) %collective-permute-start.7) | collective-permute-done | bytes 10144 | tf_op jit(solution)/shard_map/ppermute | solution.py:370
  42.5 0.0 collective-permute-done.4.north
  42.5 0.0 collective-permute-done.5.south
  42.5 3.0 %step.4 = (f32[2528,128]{1,0:T(8,128)S(1)}, bf16[316,128]{1,0:T(8,128)(2,1)S(1)}, bf16[316,128]{1,0:T(8,128)(2,1)S(1)}, f32[1,2528]{1,0:T(1,128)S(1)}, f32[1,2528]{1,0:T(1,128)S(1)}, /*index=5*/f32[32,128]{1,0:T(8,128)S(1)}) custom-call(f32[2528,128]{1,0:T(8,128)S(1)} %get-tuple-element.33.mixed, bf16[316,128]{1,0:T(8,128)(2,1)S(1)} %collective-permute-done.4.north, ...), custom_call_target="tpu_custom_call" | custom-call | tf_op jit(solution)/shard_map/step/pallas_call | solution.py:480
  45.5 1.1 %copy-done.11 = f32[2528,128]{1,0:T(8,128)} copy-done((f32[2528,128]{1,0:T(8,128)}, f32[2528,128]{1,0:T(8,128)S(1)}, u32[]{:S(2)}) %copy-start.11) | copy-done | bytes 1294360
  46.6 1.5 %collective-permute-start.8 = (bf16[316,128]{1,0:T(8,128)(2,1)S(1)}, bf16[316,128]{1,0:T(8,128)(2,1)S(1)}, u32[]{:S(2)}, u32[]{:S(2)}) collective-permute-start(bf16[316,128]{1,0:T(8,128)(2,1)S(1)} %get-tuple-element.40), channel_id=1, source_target_pairs={{0,24},{8,0},{16,8},{24,16},{1,25},{9,1},{17,9},{25,17},{2,26},{10... | collective-permute-start | bytes 242696 | tf_op jit(solution)/shard_map/ppermute | solution.py:368
  48.1 0.6 collective-permute-start.9
  48.6 0.0 collective-permute-start.10
  48.6 0.5 collective-permute-start.11
  49.2 1.7 %forcing.1.rest_1_ = f32[640,512]{1,0:T(8,128)S(1)} custom-call(bf16[1536,128]{1,0:T(8,128)(2,1)S(1)} %bitcast.9), custom_call_target="tpu_custom_call" | custom-call | tf_op jit(solution)/shard_map/forcing/pallas_call | solution.py:456
  50.9 2.7 %collective-permute-done.11.west = f32[1,2528]{1,0:T(1,128)S(1)} collective-permute-done((f32[1,2528]{1,0:T(1,128)S(1)}, f32[1,2528]{1,0:T(1,128)S(1)}, u32[]{:S(2)}, u32[]{:S(2)}) %collective-permute-start.11) | collective-permute-done | bytes 10144 | tf_op jit(solution)/shard_map/ppermute | solution.py:370
  53.5 0.6 copy-done.22
  54.1 0.6 copy-done.17
  54.8 0.6 copy-done.19
  55.4 1.0 %copy-done.5 = bf16[2,79,8,128]{3,2,1,0:T(8,128)(2,1)S(1)} copy-done((bf16[2,79,8,128]{3,2,1,0:T(8,128)(2,1)S(1)}, bf16[2,79,8,128]{3,2,1,0:T(8,128)(2,1)}, u32[]{:S(2)}) %copy-start.5) | copy-done | bytes 323608
  56.4 0.9 copy-done.14
  57.3 0.9 copy-done.18
  58.2 0.9 copy-done.20
  59.0 0.7 copy-done.23
  59.8 3.2 %step.5 = (f32[2528,128]{1,0:T(8,128)S(1)}, bf16[316,128]{1,0:T(8,128)(2,1)S(1)}, bf16[316,128]{1,0:T(8,128)(2,1)S(1)}, f32[1,2528]{1,0:T(1,128)S(1)}, f32[1,252...) custom-call(f32[2528,128]{1,0:T(8,128)S(1)} %copy-done.12, bf16[316,128]{1,0:T(8,128)(2,1)S(1)} %copy-done.18, ...), custom_call_target="tpu_custom_call" | custom-call | tf_op jit(solution)/shard_map/step/pallas_call | solution.py:480
  63.0 0.0 copy-start.7
  63.0 1.0 %copy-done.7 = f32[2528,128]{1,0:T(8,128)} copy-done((f32[2528,128]{1,0:T(8,128)}, f32[2528,128]{1,0:T(8,128)S(1)}, u32[]{:S(2)}) %copy-start.7) | copy-done | bytes 1294360
  64.0 0.6 copy-done.16
  64.7 0.6 copy-done.25
  65.3 0.6 copy-done.26
  65.9 0.6 copy-done.27
  66.5 0.6 copy-done.28
  67.1 3.4 %all-to-all-start.1 = ((bf16[8,48,128]{2,1,0:T(8,128)(2,1)}), bf16[8,48,128]{2,1,0:T(8,128)(2,1)S(1)}, u32[]{:S(2)}, u32[]{:S(2)}) async-start(bf16[8,48,128]{2,1,0:T(8,128)(2,1)} %copy-done.16), calls=%async_computation.1 | async-start | bytes 196608 | tf_op jit(solution)/shard_map/all_to_all | solution.py:492
  70.5 2.4 %collective-permute-start.12 = (bf16[316,128]{1,0:T(8,128)(2,1)}, bf16[316,128]{1,0:T(8,128)(2,1)S(1)}, u32[]{:S(2)}, u32[]{:S(2)}) collective-permute-start(bf16[316,128]{1,0:T(8,128)(2,1)} %copy-done.26), channel_id=1, source_target_pairs={{0,24},{8,0},{16,8},{24,16},{1,25},{9,1},{17,9},{25,17},{2,26},{10... | collective-permute-start | bytes 242696 | tf_op jit(solution)/shard_map/ppermute | solution.py:368
  72.9 0.0 collective-permute-start.13
  72.9 3.1 %collective-permute-start.14 = (f32[1,2528]{1,0:T(1,128)}, f32[1,2528]{1,0:T(1,128)S(1)}, u32[]{:S(2)}, u32[]{:S(2)}) collective-permute-start(f32[1,2528]{1,0:T(1,128)} %copy-done.28), channel_id=1, source_target_pairs={{0,7},{1,0},{2,1},{3,2},{4,3},{5,4},{6,5},{7,6},{8,15},{9,8},{10,9... | collective-permute-start | bytes 30344 | tf_op jit(solution)/shard_map/ppermute | solution.py:369
  76.1 1.6 %collective-permute-done.14.east = f32[1,2528]{1,0:T(1,128)S(1)} collective-permute-done((f32[1,2528]{1,0:T(1,128)}, f32[1,2528]{1,0:T(1,128)S(1)}, u32[]{:S(2)}, u32[]{:S(2)}) %collective-permute-start.14) | collective-permute-done | bytes 10144 | tf_op jit(solution)/shard_map/ppermute | solution.py:369
  77.6 3.5 %collective-permute-done.15.west = f32[1,2528]{1,0:T(1,128)S(1)} collective-permute-done((f32[1,2528]{1,0:T(1,128)}, f32[1,2528]{1,0:T(1,128)S(1)}, u32[]{:S(2)}, u32[]{:S(2)}) %collective-permute-start.15) | collective-permute-done | bytes 10144 | tf_op jit(solution)/shard_map/ppermute | solution.py:370
  81.2 0.0 collective-permute-done.12.north
  81.2 0.0 collective-permute-done.13.south
  81.2 1.3 %copy-done.2 = f32[640,512]{1,0:T(8,128)S(1)} copy-done((f32[640,512]{1,0:T(8,128)S(1)}, f32[640,512]{1,0:T(8,128)}, u32[]{:S(2)}) %copy-start.2) | copy-done | bytes 1310744
  82.5 1.3 %copy-done.8 = f32[2528,128]{1,0:T(8,128)S(1)} copy-done((f32[2528,128]{1,0:T(8,128)S(1)}, f32[2528,128]{1,0:T(8,128)}, u32[]{:S(2)}) %copy-start.8) | copy-done | bytes 1294360
  83.8 2.3 %last.1 = f32[2528,128]{1,0:T(8,128)} custom-call(f32[2528,128]{1,0:T(8,128)S(1)} %copy-done.8, bf16[316,128]{1,0:T(8,128)(2,1)S(1)} %collective-permute-done.12.north, bf16[316,128]{1,0:T(8,128)(2,1)S(1)} %collective-permute-done.13.south, f32[1,2528]{1,0:T(1,128)S(1)} %collective-permute-done.14.east, f32[1,2528]{1,0:T(1,128)S(1)} %collective-permute-done.15.west, ...), custom_call_target="tpu_custom_call" | custom-call | tf_op jit(solution)/shard_map/last/pallas_call | solution.py:494
  86.1 0.7 lon_smooth.1
  86.8 8.5 %all-gather = bf16[160,128]{1,0:T(8,128)(2,1)S(1)} all-gather(bf16[40,128]{1,0:T(8,128)(2,1)S(1)} %lon_smooth.1), channel_id=2, replica_groups=mesh['lat'=4,'lon'=8] {'lat'}, dimensions={0}, use_global_device_ids=true | all-gather | bytes 51200 | tf_op jit(solution)/shard_map/all_gather | solution.py:511
  95.4 0.9 lat_smooth.1
  (41 shorter events, 0.1 us)
Async XLA Ops:
  0.6 1.0 %copy-start.3 = (bf16[2,79,8,128]{3,2,1,0:T(8,128)(2,1)S(1)}, bf16[2,79,8,128]{3,2,1,0:T(8,128)(2,1)}, u32[]{:S(2)}) copy-start(bf16[2,79,8,128]{3,2,1,0:T(8,128)(2,1)} %profiles.7) | copy-start | bytes 970756
  1.6 1.3 %copy-start.6 = (f32[4,79,8,128]{3,2,1,0:T(8,128)S(1)}, f32[4,79,8,128]{3,2,1,0:T(8,128)}, u32[]{:S(2)}) copy-start(f32[4,79,8,128]{3,2,1,0:T(8,128)} %param.11) | copy-start | bytes 3883012
  2.9 0.7 copy-start.21
  5.7 1.1 %copy-start.9 = (f32[2528,128]{1,0:T(8,128)}, f32[2528,128]{1,0:T(8,128)S(1)}, u32[]{:S(2)}) copy-start(f32[2528,128]{1,0:T(8,128)S(1)} %get-tuple-element.27.mixed) | copy-start | bytes 3883012
  6.8 21.8 %copy-start.4 = (bf16[2,79,8,128]{3,2,1,0:T(8,128)(2,1)S(1)}, bf16[2,79,8,128]{3,2,1,0:T(8,128)(2,1)}, u32[]{:S(2)}) copy-start(bf16[2,79,8,128]{3,2,1,0:T(8,128)(2,1)} %profiles.7) | copy-start | bytes 970756
  10.2 38.9 %all-to-all-start = ((bf16[32,48,128]{2,1,0:T(8,128)(2,1)}), bf16[32,48,128]{2,1,0:T(8,128)(2,1)S(1)}, u32[]{:S(2)}, u32[]{:S(2)}) async-start(bf16[32,48,128]{2,1,0:T(8,128)(2,1)} %bitcast.12), calls=%async_computation | async-start | bytes 786432 | tf_op jit(solution)/shard_map/all_to_all | solution.py:452
  17.6 10.7 %collective-permute-start = (bf16[332,128]{1,0:T(8,128)(2,1)S(1)}, bf16[332,128]{1,0:T(8,128)(2,1)S(1)}, u32[]{:S(2)}, u32[]{:S(2)}) collective-permute-start(bf16[332,128]{1,0:T(8,128)(2,1)S(1)} %get-tuple-element.28), channel_id=1, source_target_pairs={{0,24},{8,0},{16,8},{24,16},{1,25},{9,1},{17,9},{25,17},{2,26},{10... | collective-permute-start | bytes 254984 | tf_op jit(solution)/shard_map/ppermute | solution.py:368
  20.3 8.2 %collective-permute-start.1 = (bf16[332,128]{1,0:T(8,128)(2,1)S(1)}, bf16[332,128]{1,0:T(8,128)(2,1)S(1)}, u32[]{:S(2)}, u32[]{:S(2)}) collective-permute-start(bf16[332,128]{1,0:T(8,128)(2,1)S(1)} %get-tuple-element.29), channel_id=1, source_target_pairs={{0,8},{8,16},{16,24},{24,0},{1,9},{9,17},{17,25},{25,1},{2,10},{10... | collective-permute-start | bytes 254984 | tf_op jit(solution)/shard_map/ppermute | solution.py:367
  20.3 7.9 %collective-permute-start.3 = (f32[1,2688]{1,0:T(1,128)S(1)}, f32[1,2688]{1,0:T(1,128)S(1)}, u32[]{:S(2)}, u32[]{:S(2)}) collective-permute-start(f32[1,2688]{1,0:T(1,128)S(1)} %get-tuple-element.31), channel_id=1, source_target_pairs={{0,1},{1,2},{2,3},{3,4},{4,5},{5,6},{6,7},{7,0},{8,9},{9,10},{10,1... | collective-permute-start | bytes 32264 | tf_op jit(solution)/shard_map/ppermute | solution.py:370
  20.3 7.9 %collective-permute-start.2 = (f32[1,2688]{1,0:T(1,128)S(1)}, f32[1,2688]{1,0:T(1,128)S(1)}, u32[]{:S(2)}, u32[]{:S(2)}) collective-permute-start(f32[1,2688]{1,0:T(1,128)S(1)} %get-tuple-element.30), channel_id=1, source_target_pairs={{0,7},{1,0},{2,1},{3,2},{4,3},{5,4},{6,5},{7,6},{8,15},{9,8},{10,9... | collective-permute-start | bytes 32264 | tf_op jit(solution)/shard_map/ppermute | solution.py:369
  28.5 4.4 %copy-start.13 = (bf16[332,128]{1,0:T(8,128)(2,1)}, bf16[332,128]{1,0:T(8,128)(2,1)S(1)}, u32[]{:S(2)}) copy-start(bf16[332,128]{1,0:T(8,128)(2,1)S(1)} %collective-permute-done.1.south.rest_3_) | copy-start | bytes 254980
  28.5 1.3 %copy-start.10 = (f32[2528,128]{1,0:T(8,128)S(1)}, f32[2528,128]{1,0:T(8,128)}, u32[]{:S(2)}) copy-start(f32[2528,128]{1,0:T(8,128)} %copy-done.9) | copy-start | bytes 3883012
  32.9 9.7 %collective-permute-start.4 = (bf16[316,128]{1,0:T(8,128)(2,1)S(1)}, bf16[316,128]{1,0:T(8,128)(2,1)S(1)}, u32[]{:S(2)}, u32[]{:S(2)}) collective-permute-start(bf16[316,128]{1,0:T(8,128)(2,1)S(1)} %get-tuple-element.34), channel_id=1, source_target_pairs={{0,24},{8,0},{16,8},{24,16},{1,25},{9,1},{17,9},{25,17},{2,26},{10... | collective-permute-start | bytes 242696 | tf_op jit(solution)/shard_map/ppermute | solution.py:368
  35.1 7.4 %collective-permute-start.5 = (bf16[316,128]{1,0:T(8,128)(2,1)S(1)}, bf16[316,128]{1,0:T(8,128)(2,1)S(1)}, u32[]{:S(2)}, u32[]{:S(2)}) collective-permute-start(bf16[316,128]{1,0:T(8,128)(2,1)S(1)} %get-tuple-element.35), channel_id=1, source_target_pairs={{0,8},{8,16},{16,24},{24,0},{1,9},{9,17},{17,25},{25,1},{2,10},{10... | collective-permute-start | bytes 242696 | tf_op jit(solution)/shard_map/ppermute | solution.py:367
  35.1 3.9 %collective-permute-start.6 = (f32[1,2528]{1,0:T(1,128)S(1)}, f32[1,2528]{1,0:T(1,128)S(1)}, u32[]{:S(2)}, u32[]{:S(2)}) collective-permute-start(f32[1,2528]{1,0:T(1,128)S(1)} %get-tuple-element.36), channel_id=1, source_target_pairs={{0,7},{1,0},{2,1},{3,2},{4,3},{5,4},{6,5},{7,6},{8,15},{9,8},{10,9... | collective-permute-start | bytes 30344 | tf_op jit(solution)/shard_map/ppermute | solution.py:369
  37.6 4.9 %collective-permute-start.7 = (f32[1,2528]{1,0:T(1,128)S(1)}, f32[1,2528]{1,0:T(1,128)S(1)}, u32[]{:S(2)}, u32[]{:S(2)}) collective-permute-start(f32[1,2528]{1,0:T(1,128)S(1)} %get-tuple-element.37), channel_id=1, source_target_pairs={{0,1},{1,2},{2,3},{3,4},{4,5},{5,6},{6,7},{7,0},{8,9},{9,10},{10,1... | collective-permute-start | bytes 30344 | tf_op jit(solution)/shard_map/ppermute | solution.py:370
  45.5 1.1 %copy-start.11 = (f32[2528,128]{1,0:T(8,128)}, f32[2528,128]{1,0:T(8,128)S(1)}, u32[]{:S(2)}) copy-start(f32[2528,128]{1,0:T(8,128)S(1)} %get-tuple-element.39.mixed) | copy-start | bytes 3883012
  46.6 7.5 %collective-permute-start.8 = (bf16[316,128]{1,0:T(8,128)(2,1)S(1)}, bf16[316,128]{1,0:T(8,128)(2,1)S(1)}, u32[]{:S(2)}, u32[]{:S(2)}) collective-permute-start(bf16[316,128]{1,0:T(8,128)(2,1)S(1)} %get-tuple-element.40), channel_id=1, source_target_pairs={{0,24},{8,0},{16,8},{24,16},{1,25},{9,1},{17,9},{25,17},{2,26},{10... | collective-permute-start | bytes 242696 | tf_op jit(solution)/shard_map/ppermute | solution.py:368
  48.1 6.7 %collective-permute-start.9 = (bf16[316,128]{1,0:T(8,128)(2,1)S(1)}, bf16[316,128]{1,0:T(8,128)(2,1)S(1)}, u32[]{:S(2)}, u32[]{:S(2)}) collective-permute-start(bf16[316,128]{1,0:T(8,128)(2,1)S(1)} %get-tuple-element.41), channel_id=1, source_target_pairs={{0,8},{8,16},{16,24},{24,0},{1,9},{9,17},{17,25},{25,1},{2,10},{10... | collective-permute-start | bytes 242696 | tf_op jit(solution)/shard_map/ppermute | solution.py:367
  48.6 2.2 %collective-permute-start.10 = (f32[1,2528]{1,0:T(1,128)S(1)}, f32[1,2528]{1,0:T(1,128)S(1)}, u32[]{:S(2)}, u32[]{:S(2)}) collective-permute-start(f32[1,2528]{1,0:T(1,128)S(1)} %get-tuple-element.42), channel_id=1, source_target_pairs={{0,7},{1,0},{2,1},{3,2},{4,3},{5,4},{6,5},{7,6},{8,15},{9,8},{10,9... | collective-permute-start | bytes 30344 | tf_op jit(solution)/shard_map/ppermute | solution.py:369
  48.6 4.9 %collective-permute-start.11 = (f32[1,2528]{1,0:T(1,128)S(1)}, f32[1,2528]{1,0:T(1,128)S(1)}, u32[]{:S(2)}, u32[]{:S(2)}) collective-permute-start(f32[1,2528]{1,0:T(1,128)S(1)} %get-tuple-element.43), channel_id=1, source_target_pairs={{0,1},{1,2},{2,3},{3,4},{4,5},{5,6},{6,7},{7,0},{8,9},{9,10},{10,1... | collective-permute-start | bytes 30344 | tf_op jit(solution)/shard_map/ppermute | solution.py:370
  49.2 6.3 %copy-start.12 = (f32[2528,128]{1,0:T(8,128)S(1)}, f32[2528,128]{1,0:T(8,128)}, u32[]{:S(2)}) copy-start(f32[2528,128]{1,0:T(8,128)} %copy-done.11) | copy-start | bytes 3883012
  50.8 12.1 %copy-start.1 = (f32[640,512]{1,0:T(8,128)}, f32[640,512]{1,0:T(8,128)S(1)}, u32[]{:S(2)}) copy-start(f32[640,512]{1,0:T(8,128)S(1)} %forcing.1.rest_1_) | copy-start | bytes 3932164
  53.5 0.6 copy-start.22
  54.1 0.6 copy-start.17
  54.8 0.6 copy-start.19
  55.4 1.0 %copy-start.5 = (bf16[2,79,8,128]{3,2,1,0:T(8,128)(2,1)S(1)}, bf16[2,79,8,128]{3,2,1,0:T(8,128)(2,1)}, u32[]{:S(2)}) copy-start(bf16[2,79,8,128]{3,2,1,0:T(8,128)(2,1)} %profiles.7) | copy-start | bytes 970756
  56.4 0.9 copy-start.14
  57.3 0.9 copy-start.18
  58.2 0.9 copy-start.20
  59.0 0.7 copy-start.23
  59.7 21.4 %copy-start = (bf16[4,4,79,8,128]{4,3,2,1,0:T(8,128)(2,1)S(1)}, bf16[4,4,79,8,128]{4,3,2,1,0:T(8,128)(2,1)}, u32[]{:S(2)}) copy-start(bf16[4,4,79,8,128]{4,3,2,1,0:T(8,128)(2,1)} %fraction.9) | copy-start | bytes 7766020
  63.0 1.1 %copy-start.7 = (f32[2528,128]{1,0:T(8,128)}, f32[2528,128]{1,0:T(8,128)S(1)}, u32[]{:S(2)}) copy-start(f32[2528,128]{1,0:T(8,128)S(1)} %get-tuple-element.46.mixed) | copy-start | bytes 3883012
  64.0 0.6 copy-start.16
  64.7 0.6 copy-start.25
  65.3 0.6 copy-start.26
  65.9 0.6 copy-start.27
  66.5 0.6 copy-start.28
  67.1 19.0 %all-to-all-start.1 = ((bf16[8,48,128]{2,1,0:T(8,128)(2,1)}), bf16[8,48,128]{2,1,0:T(8,128)(2,1)S(1)}, u32[]{:S(2)}, u32[]{:S(2)}) async-start(bf16[8,48,128]{2,1,0:T(8,128)(2,1)} %copy-done.16), calls=%async_computation.1 | async-start | bytes 196608 | tf_op jit(solution)/shard_map/all_to_all | solution.py:492
  70.5 10.7 %collective-permute-start.12 = (bf16[316,128]{1,0:T(8,128)(2,1)}, bf16[316,128]{1,0:T(8,128)(2,1)S(1)}, u32[]{:S(2)}, u32[]{:S(2)}) collective-permute-start(bf16[316,128]{1,0:T(8,128)(2,1)} %copy-done.26), channel_id=1, source_target_pairs={{0,24},{8,0},{16,8},{24,16},{1,25},{9,1},{17,9},{25,17},{2,26},{10... | collective-permute-start | bytes 242696 | tf_op jit(solution)/shard_map/ppermute | solution.py:368
  72.9 8.3 %collective-permute-start.13 = (bf16[316,128]{1,0:T(8,128)(2,1)}, bf16[316,128]{1,0:T(8,128)(2,1)S(1)}, u32[]{:S(2)}, u32[]{:S(2)}) collective-permute-start(bf16[316,128]{1,0:T(8,128)(2,1)} %copy-done.25), channel_id=1, source_target_pairs={{0,8},{8,16},{16,24},{24,0},{1,9},{9,17},{17,25},{25,1},{2,10},{10... | collective-permute-start | bytes 242696 | tf_op jit(solution)/shard_map/ppermute | solution.py:367
  72.9 4.7 %collective-permute-start.14 = (f32[1,2528]{1,0:T(1,128)}, f32[1,2528]{1,0:T(1,128)S(1)}, u32[]{:S(2)}, u32[]{:S(2)}) collective-permute-start(f32[1,2528]{1,0:T(1,128)} %copy-done.28), channel_id=1, source_target_pairs={{0,7},{1,0},{2,1},{3,2},{4,3},{5,4},{6,5},{7,6},{8,15},{9,8},{10,9... | collective-permute-start | bytes 30344 | tf_op jit(solution)/shard_map/ppermute | solution.py:369
  76.0 5.1 %collective-permute-start.15 = (f32[1,2528]{1,0:T(1,128)}, f32[1,2528]{1,0:T(1,128)S(1)}, u32[]{:S(2)}, u32[]{:S(2)}) collective-permute-start(f32[1,2528]{1,0:T(1,128)} %copy-done.27), channel_id=1, source_target_pairs={{0,1},{1,2},{2,3},{3,4},{4,5},{5,6},{6,7},{7,0},{8,9},{9,10},{10,1... | collective-permute-start | bytes 30344 | tf_op jit(solution)/shard_map/ppermute | solution.py:370
  81.2 1.3 %copy-start.2 = (f32[640,512]{1,0:T(8,128)S(1)}, f32[640,512]{1,0:T(8,128)}, u32[]{:S(2)}) copy-start(f32[640,512]{1,0:T(8,128)} %copy-done.1) | copy-start | bytes 3932164
  82.5 1.3 %copy-start.8 = (f32[2528,128]{1,0:T(8,128)S(1)}, f32[2528,128]{1,0:T(8,128)}, u32[]{:S(2)}) copy-start(f32[2528,128]{1,0:T(8,128)} %copy-done.7) | copy-start | bytes 3883012
  83.8 2.3 %copy-start.15 = (bf16[128,1024]{1,0:T(8,128)(2,1)S(1)}, bf16[128,1024]{1,0:T(8,128)(2,1)}, u32[]{:S(2)}) copy-start(bf16[128,1024]{1,0:T(8,128)(2,1)} %matrix.2) | copy-start | bytes 786436
  83.8 11.6 %copy-start.24 = (bf16[32,32]{1,0:T(8,128)(2,1)S(1)}, bf16[32,32]{1,0:T(8,128)(2,1)}, u32[]{:S(2)}) copy-start(bf16[32,32]{1,0:T(8,128)(2,1)} %matrix.3) | copy-start | bytes 6148

commit v4 on v3

--- a/solution.py
+++ b/solution.py
@@ -35,7 +35,7 @@
     return pl.BlockSpec(shape, lambda i: (0,) * len(shape))
 
 
-def params(limit=48 << 20):
+def params(limit=24 << 20):
     return pltpu.CompilerParams(vmem_limit_bytes=limit)
 
 
@@ -108,9 +108,12 @@
         body(levels // 2, (levels - 1,))
 
 
-def first_body(dims, kernel, profiles, adjoint, fraction, mixed, kron, up, down, west, east, low, mix):
+def first_body(dims, kernel, profiles, adjoint, fraction, mixed_out, kron_out, up, down, west, east, *rest):
+    low, mix, mixed, kron, mixed_sem, kron_sem = rest
     tracers, levels, rows = dims
     kron[...] = expand_kernel(kernel[...], levels, low.shape[0] // rows, rows)
+    kron_copy = pltpu.make_async_copy(kron, kron_out, kron_sem)
+    kron_copy.start()
 
     def body(k2, ks):
         detrains = [profiles[1, k].astype(F32) for k in ks]
@@ -122,6 +125,8 @@
 
     over_levels(levels, body)
     convect(dims, adjoint, low, mix, kron, profiles, mixed)
+    mixed_copy = pltpu.make_async_copy(mixed, mixed_out, mixed_sem)
+    mixed_copy.start()
     send_edges(dims, mixed, up, down, west, east)
     count = tracers * levels
     lat = lax.axis_index("lat")
@@ -133,6 +138,8 @@
     at = (count * rows + LANES - 1) // LANES * LANES
     west[:, at : at + tracers * rows] = end_columns(jnp.concatenate([f[1]] * tracers, axis=0))[0:1]
     east[:, at : at + tracers * rows] = end_columns(jnp.concatenate([f[0]] * tracers, axis=0))[1:2]
+    kron_copy.wait()
+    mixed_copy.wait()
 
 
 def unpack_halo(dims, north, south, east, west, north_scr, south_scr, sides):
@@ -196,6 +203,9 @@
     ]
     if last:
         patch(dims, new_mixed, total, *extra, new_surface)
+        at = up.shape[0] - new_surface.shape[0]
+        up[at:, :] = new_surface[...]
+        down[at:, :] = new_surface[...]
     else:
         new_surface[...] = jnp.concatenate(total, axis=0)
 
@@ -231,13 +241,12 @@
     short = (-2 * tracers) % 8
     filler = [jnp.zeros((short, LANES), F32)] if short else []
     whole = jnp.concatenate(tile + under + over + filler + [ends], axis=0)
-    for z in range(out.shape[0]):
-        out[z] = whole.astype(BF16)
+    out[...] = whole.astype(BF16)
 
 
 def last_body(dims, mixed, north, south, east, west, fraction, forcing, *rest):
     adjoint, north_scr, south_scr, sides = rest
-    tracers, levels, rows = dims
+    _, levels, rows = dims
     unpack_halo(dims, north, south, east, west, north_scr, south_scr, sides)
 
     def body(k2, ks):
@@ -250,7 +259,7 @@
 
 
 def pack_body(sizes, owner, count, cols, weights, resid, out):
-    devices, blocks, slots, levels, tracers, chunk = sizes
+    _, blocks, slots, levels, tracers, chunk = sizes
     own = owner[...].astype(F32)
     wide = jnp.broadcast_to(own, (blocks, blocks))
     below = iota((blocks, blocks), 0)
@@ -322,39 +331,51 @@
     lax.fori_loop(0, got.shape[0] // chunk, body, 0)
 
 
-def lon_body(size, got, matrix, out):
-    count = got.shape[0]
-    body = out.shape[0]
+def lat_body(tracers, rows, offsets, matrix, *rest):
+    *parts, out = rest
+    size = tracers * rows
+    total_rows = matrix.shape[0]
+    bands = total_rows // rows
+    lat = lax.axis_index("lat")
+    depth = size + (2 * tracers + 7) // 8 * 8
+    each = depth + 8
+    width = each * len(parts)
+    own = matrix[pl.ds(pl.multiple_of(lat * rows, rows), rows), :]
+    own = jnp.concatenate([own] * tracers, axis=0)
+    column = iota((1, width), 1) % each
+    band = jnp.zeros((1, width), jnp.int32)
+    for b, offset in enumerate(offsets):
+        band = jnp.where(iota((1, width), 1) // each == b, lax.rem(lat + offset + bands, bands), band)
+    in_band = jnp.where(column < size, column % rows, jnp.where(column < size + tracers, -1, rows))
+    source = jnp.where(column < size + 2 * tracers, band * rows + in_band, -1)
+    of_tracer = jnp.where(column < size, column // rows, (column - size) % tracers)
+    hit = (iota((total_rows, width), 0) == source).astype(BF16)
+    same = iota((size, width), 0) // rows == of_tracer
+    weights = jnp.where(same, jnp.dot(own, hit, preferred_element_type=F32), 0.0).astype(BF16)
+    patches = jnp.concatenate([p[p.shape[0] - each :, :] for p in parts], axis=0)
+    total = jnp.dot(weights, patches, preferred_element_type=F32)
+    ends = jnp.concatenate([p[p.shape[0] - 8 :, 0:each].astype(F32) for p in parts], axis=1).astype(BF16)
+    ends = dot_nt(ends, weights)
+    ends = jnp.concatenate([ends, jnp.zeros((8, LANES - size), F32)], axis=1)
+    whole = jnp.concatenate([total, ends], axis=0).astype(BF16)
+    out[...] = whole
+
+
+def lon_body(matrix, *rest):
+    *parts, out = rest
+    count = len(parts)
+    size = out.shape[0]
+    lon = lax.axis_index("lon")
+    ends = [p[size : size + 8, :].astype(F32)[:, 0:size] for p in parts]
+    east = jnp.concatenate([ends[(s + 1) % count][1:2] for s in range(count)], axis=1)
+    west = jnp.concatenate([ends[(s - 1) % count][0:1] for s in range(count)], axis=1)
+    sides = spread_columns(east, west)
     total = jnp.zeros(out.shape, F32)
-    ends = [got[z, body : body + 8, :].astype(F32)[:, 0:size] for z in range(count)]
-    for z in range(count):
-        side = spread_columns(ends[(z - 1) % count][1:2], ends[(z + 1) % count][0:1])
-        block = got[z, 0:body, :].astype(F32)
-        block = jnp.concatenate([block[0:size] + side, block[size:]], axis=0)
-        total = total + dot_nt(block.astype(BF16), matrix[:, z * LANES : (z + 1) * LANES])
-    out[...] = total.astype(BF16)
-
-
-def lat_body(tracers, rows, got, matrix, out):
-    bands = got.shape[0]
-    size = tracers * rows
-    extra = got.shape[1] - size
-    lat = lax.axis_index("lat")
-    own = matrix[pl.ds(pl.multiple_of(lat * rows, rows), rows), :].astype(F32)
-    own = jnp.concatenate([own] * tracers, axis=0)
-    tracer = iota((size, extra), 0) // rows
-    column = iota((size, extra), 1)
-    same = iota((size, size), 0) // rows == iota((size, size), 1) // rows
-    total = jnp.zeros(out.shape, F32)
-    for b in range(bands):
-        block = jnp.concatenate([own[:, b * rows : (b + 1) * rows]] * tracers, axis=1)
-        block = jnp.where(same, block, 0.0)
-        under = max(b * rows - 1, 0)
-        over = min((b + 1) * rows, bands * rows - 1)
-        ring_part = jnp.where(column == tracer, own[:, under : under + 1], 0.0)
-        ring_part = ring_part + jnp.where(column == tracer + tracers, own[:, over : over + 1], 0.0)
-        weights = jnp.concatenate([block, ring_part], axis=1).astype(BF16)
-        total = total + jnp.dot(weights, got[b], preferred_element_type=F32)
+    for s, part in enumerate(parts):
+        block = (part[0:size, :].astype(F32) + sides[s * size : (s + 1) * size, :]).astype(BF16)
+        source = lax.rem(lon - s + count, count)
+        own = matrix[:, pl.ds(pl.multiple_of(source * LANES, LANES), LANES)]
+        total = total + dot_nt(block, own)
     out[...] = total
 
 
@@ -371,7 +392,7 @@
     return north, south, east, west
 
 
-def shards(
+def window(
     adjoint_in,
     fractions,
     profiles,
@@ -417,9 +438,16 @@
         grid=(1,),
         out_shape=[state, kron_type] + long_edges,
         in_specs=[full(kernel.shape), full(profiles.shape), spec(state), level_zero],
-        out_specs=[spec(s) for s in [state, kron_type] + long_edges],
-        scratch_shapes=[low_scr, mix_scr],
-        compiler_params=params(),
+        out_specs=[pl.BlockSpec(memory_space=pltpu.HBM)] * 2 + [spec(s) for s in long_edges],
+        scratch_shapes=[
+            low_scr,
+            mix_scr,
+            pltpu.VMEM(state.shape, state.dtype),
+            pltpu.VMEM(kron_type.shape, kron_type.dtype),
+            pltpu.SemaphoreType.DMA,
+            pltpu.SemaphoreType.DMA,
+        ],
+        compiler_params=params(60 << 20),
         name="first",
     )(kernel, profiles, adjoint_in.reshape(cells, LANES), fractions)
     halo = first_halo = exchange(*out)
@@ -464,11 +492,13 @@
     surface = jnp.zeros(surface_type.shape, F32)
     lon_count = lax.axis_size("lon")
     patch_rows = (tracers * (rows + 2) + 7) // 8 * 8
-    patch_type = jax.ShapeDtypeStruct((lon_count, patch_rows + 8, LANES), BF16)
+    patch_type = jax.ShapeDtypeStruct((patch_rows + 8, LANES), BF16)
+    tall = jax.ShapeDtypeStruct(((count + 15) // 16 * 16 + patch_type.shape[0], LANES), BF16)
     for step_index in range(STEPS - 1, 0, -1):
         last = step_index == 1
         frac_spec = pl.BlockSpec((1,) + fractions.shape[1:], lambda i, n=step_index: (n, 0, 0, 0, 0))
         halo_types = long_edges if step_index == STEPS - 1 else edges
+        outs = [tall, tall, side_edge, side_edge] if last else edges
         ins = [mixed, *halo, fractions, profiles, kron, surface]
         in_specs = [spec(state)] + [spec(h) for h in halo_types]
         in_specs += [frac_spec, full(profiles.shape), spec(kron_type), spec(surface_type)]
@@ -480,41 +510,46 @@
         mixed, *out, surface = pl.pallas_call(
             functools.partial(step_body, dims, last),
             grid=(1,),
-            out_shape=[state] + edges + [result],
+            out_shape=[state] + outs + [result],
             in_specs=in_specs,
-            out_specs=[spec(s) for s in [state] + edges + [result]],
+            out_specs=[spec(s) for s in [state] + outs + [result]],
             scratch_shapes=halo_scr + [pltpu.VMEM((cells, LANES), F32), low_scr, mix_scr],
             compiler_params=params(),
             name="step",
         )(*ins)
         halo = exchange(*out)
 
-    band = lax.all_to_all(surface, "lon", split_axis=0, concat_axis=0, tiled=True)
+    lat_count = lax.axis_size("lat")
+    parts = [surface, halo[1], halo[0]]
+    offsets = [0, -1, 1]
+    for shift in range(2, lat_count - 1):
+        parts.append(lax.ppermute(surface, "lat", ring("lat", shift)))
+        offsets.append(-shift)
+    bands = pl.pallas_call(
+        functools.partial(lat_body, tracers, rows, offsets),
+        out_shape=jax.ShapeDtypeStruct((tracers * rows + 8, LANES), BF16),
+        compiler_params=params(),
+        name="lat_smooth",
+    )(lat_matrix, *parts)
+    shifts = [lax.ppermute(bands, "lon", ring("lon", shift)) for shift in range(1, lon_count)]
     frac_spec = pl.BlockSpec((1,) + fractions.shape[1:], lambda i: (0, 0, 0, 0, 0))
     adjoint = pl.pallas_call(
         functools.partial(last_body, dims),
         grid=(1,),
         out_shape=state,
-        in_specs=[spec(state)] + [spec(h) for h in edges] + [frac_spec, full(forcing.shape)],
+        in_specs=[spec(state), spec(tall), spec(tall), spec(side_edge), spec(side_edge)]
+        + [frac_spec, full(forcing.shape)],
         out_specs=spec(state),
         scratch_shapes=halo_scr,
         compiler_params=params(),
         name="last",
     )(mixed, *halo, fractions, forcing)
-
-    across = pl.pallas_call(
-        functools.partial(lon_body, tracers * rows),
-        out_shape=jax.ShapeDtypeStruct((patch_rows, LANES), BF16),
+    smoothed = pl.pallas_call(
+        lon_body,
+        out_shape=surface_type,
         compiler_params=params(),
         name="lon_smooth",
-    )(band, lon_matrix)
-    column = lax.all_gather(across, "lat", axis=0)
-    smoothed = pl.pallas_call(
-        functools.partial(lat_body, tracers, rows),
-        out_shape=surface_type,
-        compiler_params=params(),
-        name="lat_smooth",
-    )(column, lat_matrix)
+    )(lon_matrix, bands, *shifts)
     return adjoint.reshape(adjoint_in.shape), smoothed.reshape(tracers, rows, LANES)
 
 
@@ -533,7 +568,7 @@
         P("lon", None),
     )
     return jax.shard_map(
-        shards,
+        window,
         mesh=mesh,
         in_specs=placed,
         out_specs=(P(None, None, "lat", "lon"), P(None, "lat", "lon")),

time: 97.1 us -> 75.9 us (0.78)
  local copies, waits for them, and re-layouts: 19.5 us -> 3.41 us
  blocking collectives: 8.54 us -> 0 us
  starting transfers between devices: 29.8 us -> 31.5 us
  Pallas kernels: 20.3 us -> 21.6 us
    unnamed x58 -> x28, local copies, waits for them, and re-layouts: 19.4 us -> 3.41 us
    all_gather x1 -> x0, blocking collectives: 8.54 us -> none  [shards(): column = lax.all_gather(across, 'lat', axis=0)]
    ppermute x0 -> x8, starting transfers between devices: none -> 7.05 us  [the longest x7 6.42 us: window(): lax.ppermute(bands, 'lon', ring('lon', shift))]
    ppermute x0 -> x8, waiting for transfers between devices: none -> 5.06 us  [the longest x7 2.63 us: window(): lax.ppermute(bands, 'lon', ring('lon', shift))]
    ppermute x4, waiting for transfers between devices: 14.1 us -> 9.73 us  [exchange(): west = lax.ppermute(to_east, 'lon', ring('lon', 1))]
    all_to_all x2 -> x1, starting transfers between devices: 10.7 us -> 7.44 us  [window(): lax.all_to_all(packed.reshape(devices, CAPACITY * slots, LANES), BOTH, sp...]
    ppermute x4, starting transfers between devices: 9.23 us -> 6.71 us  [exchange(): east = lax.ppermute(to_west, 'lon', ring('lon', -1))]
    ppermute x4, waiting for transfers between devices: 0.28 us -> 2.04 us  [exchange(): south = lax.ppermute(up, 'lat', ring('lat', 1))]
  transfers between devices with their start and end apart: 18 -> 25, of which waited for: 7 -> 9; matrix products, arithmetic and copies ran while one was open for 0% -> 0% of each run, Pallas kernels for 10% -> 13%
where the time goes in v4:
time: 75.9 us; the launch traced here: 75.6 us
  starting transfers between devices  31.5 us (42%)
  Pallas kernels  21.6 us (28%)
  waiting for transfers between devices  18.2 us (24%)
  local copies, waits for them, and re-layouts  3.41 us (4%)
  between operations  0.81 us (1%)
    ppermute x4, waiting for transfers between devices, exchange(): west = lax.ppermute(to_east, 'lon', ring('lon', 1))  9.73 us
    ppermute x4, starting transfers between devices, exchange(): north = lax.ppermute(down, 'lat', ring('lat', -1))  8.77 us
    all_to_all x1, starting transfers between devices, window(): lax.all_to_all(packed.reshape(devices, CAPACITY * slots, LANES), BOTH, sp...  7.44 us
    pallas_call x3, Pallas kernels, window(): pl.pallas_call(functools.partial(step_body, dims, last), grid=(1,), out_s...  7.25 us
    ppermute x4, starting transfers between devices, exchange(): east = lax.ppermute(to_west, 'lon', ring('lon', -1))  6.71 us
    ppermute x7, starting transfers between devices, window(): lax.ppermute(bands, 'lon', ring('lon', shift))  6.42 us
    pallas_call x1, Pallas kernels, window(): pl.pallas_call(functools.partial(first_body, dims), grid=(1,), out_shape=...  4.45 us
    pallas_call x1, Pallas kernels, window(): pl.pallas_call(functools.partial(pack_body, (devices, blocks, slots, leve...  3.5 us
  transfers between devices with their start and end apart: 25, of which 9 were waited for; matrix products, arithmetic and copies ran while one was open for 0% of the time, Pallas kernels for 13%

profile of v4, /device:TPU:0, one launch (start us, length us, event | category | flops | bytes accessed | tf_op | source)
XLA Modules:
  0.0 75.6 jit_solution(6635334537392774416)
XLA Ops:
  0.6 4.5 %first.1 = (f32[2528,128]{1,0:T(8,128)}, bf16[640,640]{1,0:T(8,128)(2,1)}, bf16[332,128]{1,0:T(8,128)(2,1)}, bf16[332,128]{1,0:T(8,128)(2,1)}, f32[1,2688]{1,0:T(1,128)}, /*index=5*/f32[1,2688]{1,0:T(1,128)}) custom-call(bf16[79,79]{1,0:T(8,128)(2,1)} %kernel.1, bf16[2,79,8,128]{3,2,1,0:T(8,128)(2,1)} %profiles.7, f32[2528,128]{1,0:T(8,128)} %bitcast.9, ...), custom_call_target="tpu_custom_call" | custom-call | tf_op jit(solution)/shard_map/first/pallas_call | solution.py:436
  5.1 0.0 copy-start.12
  5.1 3.5 %pack.1 = bf16[1536,128]{1,0:T(8,128)(2,1)} custom-call(s32[1,128]{1,0:T(1,128)} %bitcast.13, s32[1,128]{1,0:T(1,128)} %bitcast.14, s32[1,1024]{1,0:T(1,128)} %bitcast.12, bf16[79,1024]{1,0:T(8,128)(2,1)} %weights.1, bf16[4,1024]{1,0:T(4,128)(2,1)} %resid.1), custom_call_target="tpu_custom_call" | custom-call | tf_op jit(solution)/shard_map/pack/pallas_call | solution.py:459
  8.6 7.4 %all-to-all-start = ((bf16[32,48,128]{2,1,0:T(8,128)(2,1)}), bf16[32,48,128]{2,1,0:T(8,128)(2,1)}, u32[]{:S(2)}, u32[]{:S(2)}) async-start(bf16[32,48,128]{2,1,0:T(8,128)(2,1)} %bitcast.8), calls=%async_computation | async-start | bytes 786432 | tf_op jit(solution)/shard_map/all_to_all | solution.py:480
  16.1 2.7 %collective-permute-start = (bf16[332,128]{1,0:T(8,128)(2,1)}, bf16[332,128]{1,0:T(8,128)(2,1)S(1)}, u32[]{:S(2)}, u32[]{:S(2)}) collective-permute-start(bf16[332,128]{1,0:T(8,128)(2,1)} %get-tuple-element.28), channel_id=1, source_target_pairs={{0,24},{8,0},{16,8},{24,16},{1,25},{9,1},{17,9},{25,17},{2,26},{10... | collective-permute-start | bytes 254984 | tf_op jit(solution)/shard_map/ppermute | solution.py:389
  18.7 0.0 collective-permute-start.1
  18.7 0.0 collective-permute-start.3
  18.8 3.5 %collective-permute-start.2 = (f32[1,2688]{1,0:T(1,128)S(1)}, f32[1,2688]{1,0:T(1,128)S(1)}, u32[]{:S(2)}, u32[]{:S(2)}) collective-permute-start(f32[1,2688]{1,0:T(1,128)S(1)} %copy-done.12), channel_id=1, source_target_pairs={{0,7},{1,0},{2,1},{3,2},{4,3},{5,4},{6,5},{7,6},{8,15},{9,8},{10,9... | collective-permute-start | bytes 32264 | tf_op jit(solution)/shard_map/ppermute | solution.py:390
  22.3 4.3 %collective-permute-done.3.west.rest_5_ = f32[1,2688]{1,0:T(1,128)S(1)} collective-permute-done((f32[1,2688]{1,0:T(1,128)S(1)}, f32[1,2688]{1,0:T(1,128)S(1)}, u32[]{:S(2)}, u32[]{:S(2)}) %collective-permute-start.3) | collective-permute-done | bytes 10784 | tf_op jit(solution)/shard_map/ppermute | solution.py:391
  26.6 0.0 collective-permute-done.2.east.rest_4_
  26.6 0.0 collective-permute-done.north.rest_2_
  26.6 0.3 collective-permute-done.1.south.rest_3_
  26.9 0.0 copy-start.2
  26.9 1.0 %copy-done.2 = bf16[2,79,8,128]{3,2,1,0:T(8,128)(2,1)S(1)} copy-done((bf16[2,79,8,128]{3,2,1,0:T(8,128)(2,1)S(1)}, bf16[2,79,8,128]{3,2,1,0:T(8,128)(2,1)}, u32[]{:S(2)}) %copy-start.2) | copy-done | bytes 323608
  27.9 1.3 %copy-done.5 = f32[2528,128]{1,0:T(8,128)S(1)} copy-done((f32[2528,128]{1,0:T(8,128)S(1)}, f32[2528,128]{1,0:T(8,128)}, u32[]{:S(2)}) %copy-start.5) | copy-done | bytes 1294360
  29.2 1.9 %step.3 = (f32[2528,128]{1,0:T(8,128)S(1)}, bf16[316,128]{1,0:T(8,128)(2,1)S(1)}, bf16[316,128]{1,0:T(8,128)(2,1)S(1)}, f32[1,2528]{1,0:T(1,128)S(1)}, f32[1,2528]{1,0:T(1,128)S(1)}, /*index=5*/f32[32,128]{1,0:T(8,128)S(1)}) custom-call(f32[2528,128]{1,0:T(8,128)S(1)} %copy-done.5, bf16[332,128]{1,0:T(8,128)(2,1)S(1)} %collective-permute-done.north.rest_2_, ...), custom_call_target="tpu_custom_call" | custom-call | tf_op jit(solution)/shard_map/step/pallas_call | solution.py:510
  31.2 2.2 %collective-permute-start.4 = (bf16[316,128]{1,0:T(8,128)(2,1)S(1)}, bf16[316,128]{1,0:T(8,128)(2,1)S(1)}, u32[]{:S(2)}, u32[]{:S(2)}) collective-permute-start(bf16[316,128]{1,0:T(8,128)(2,1)S(1)} %get-tuple-element.34), channel_id=1, source_target_pairs={{0,24},{8,0},{16,8},{24,16},{1,25},{9,1},{17,9},{25,17},{2,26},{10... | collective-permute-start | bytes 242696 | tf_op jit(solution)/shard_map/ppermute | solution.py:389
  33.4 0.0 collective-permute-start.5
  33.4 2.5 %collective-permute-start.6 = (f32[1,2528]{1,0:T(1,128)S(1)}, f32[1,2528]{1,0:T(1,128)S(1)}, u32[]{:S(2)}, u32[]{:S(2)}) collective-permute-start(f32[1,2528]{1,0:T(1,128)S(1)} %get-tuple-element.36), channel_id=1, source_target_pairs={{0,7},{1,0},{2,1},{3,2},{4,3},{5,4},{6,5},{7,6},{8,15},{9,8},{10,9... | collective-permute-start | bytes 30344 | tf_op jit(solution)/shard_map/ppermute | solution.py:390
  35.9 0.0 collective-permute-start.7
  35.9 1.4 %collective-permute-done.6.east = f32[1,2528]{1,0:T(1,128)S(1)} collective-permute-done((f32[1,2528]{1,0:T(1,128)S(1)}, f32[1,2528]{1,0:T(1,128)S(1)}, u32[]{:S(2)}, u32[]{:S(2)}) %collective-permute-start.6) | collective-permute-done | bytes 10144 | tf_op jit(solution)/shard_map/ppermute | solution.py:390
  37.3 3.5 %collective-permute-done.7.west = f32[1,2528]{1,0:T(1,128)S(1)} collective-permute-done((f32[1,2528]{1,0:T(1,128)S(1)}, f32[1,2528]{1,0:T(1,128)S(1)}, u32[]{:S(2)}, u32[]{:S(2)}) %collective-permute-start.7) | collective-permute-done | bytes 10144 | tf_op jit(solution)/shard_map/ppermute | solution.py:391
  40.8 0.0 collective-permute-done.4.north
  40.8 0.0 collective-permute-done.5.south
  40.8 2.4 %step.4 = (f32[2528,128]{1,0:T(8,128)S(1)}, bf16[316,128]{1,0:T(8,128)(2,1)}, bf16[316,128]{1,0:T(8,128)(2,1)}, f32[1,2528]{1,0:T(1,128)}, f32[1,2528]{1,0:T(1,128)}, /*index=5*/f32[32,128]{1,0:T(8,128)S(1)}) custom-call(f32[2528,128]{1,0:T(8,128)S(1)} %get-tuple-element.33.mixed, bf16[316,128]{1,0:T(8,128)(2,1)S(1)} %collective-permute-done.4.north, ...), custom_call_target="tpu_custom_call" | custom-call | tf_op jit(solution)/shard_map/step/pallas_call | solution.py:510
  43.3 1.0 %copy-done.6 = f32[2528,128]{1,0:T(8,128)} copy-done((f32[2528,128]{1,0:T(8,128)}, f32[2528,128]{1,0:T(8,128)S(1)}, u32[]{:S(2)}) %copy-start.6) | copy-done | bytes 1294360
  44.3 1.5 %collective-permute-start.8 = (bf16[316,128]{1,0:T(8,128)(2,1)}, bf16[316,128]{1,0:T(8,128)(2,1)}, u32[]{:S(2)}, u32[]{:S(2)}) collective-permute-start(bf16[316,128]{1,0:T(8,128)(2,1)} %get-tuple-element.40), channel_id=1, source_target_pairs={{0,24},{8,0},{16,8},{24,16},{1,25},{9,1},{17,9},{25,17},{2,26},{10... | collective-permute-start | bytes 242696 | tf_op jit(solution)/shard_map/ppermute | solution.py:389
  45.8 0.6 collective-permute-start.9
  46.3 0.0 collective-permute-start.10
  46.3 0.5 collective-permute-start.11
  46.9 0.0 all-to-all-done
  46.9 2.8 %forcing.1.rest_1_ = f32[640,512]{1,0:T(8,128)S(1)} custom-call(bf16[1536,128]{1,0:T(8,128)(2,1)} %bitcast.5.got), custom_call_target="tpu_custom_call" | custom-call | tf_op jit(solution)/shard_map/forcing/pallas_call | solution.py:484
  49.7 0.0 collective-permute-done.10.east
  49.7 1.9 %collective-permute-done.11.west = f32[1,2528]{1,0:T(1,128)} collective-permute-done((f32[1,2528]{1,0:T(1,128)}, f32[1,2528]{1,0:T(1,128)}, u32[]{:S(2)}, u32[]{:S(2)}) %collective-permute-start.11) | collective-permute-done | bytes 10144 | tf_op jit(solution)/shard_map/ppermute | solution.py:391
  51.6 0.0 collective-permute-done.8.north
  51.6 0.0 collective-permute-done.9.south
  51.6 0.0 copy-start.11
  51.6 2.9 %step.5 = (f32[2528,128]{1,0:T(8,128)S(1)}, bf16[368,128]{1,0:T(8,128)(2,1)S(1)}, bf16[368,128]{1,0:T(8,128)(2,1)S(1)}, f32[1,2528]{1,0:T(1,128)S(1)}, f32[1,252...) custom-call(f32[2528,128]{1,0:T(8,128)S(1)} %copy-done.7, bf16[316,128]{1,0:T(8,128)(2,1)} %collective-permute-done.8.north, ...), custom_call_target="tpu_custom_call" | custom-call | tf_op jit(solution)/shard_map/step/pallas_call | solution.py:510
  54.5 2.4 %collective-permute-start.12 = (bf16[368,128]{1,0:T(8,128)(2,1)S(1)}, bf16[368,128]{1,0:T(8,128)(2,1)S(1)}, u32[]{:S(2)}, u32[]{:S(2)}) collective-permute-start(bf16[368,128]{1,0:T(8,128)(2,1)S(1)} %get-tuple-element.47), channel_id=1, source_target_pairs={{0,24},{8,0},{16,8},{24,16},{1,25},{9,1},{17,9},{25,17},{2,26},{10... | collective-permute-start | bytes 282632 | tf_op jit(solution)/shard_map/ppermute | solution.py:389
  56.9 0.0 collective-permute-start.13
  56.9 0.6 collective-permute-start.16
  57.6 0.6 collective-permute-start.14
  58.2 2.4 %collective-permute-done.16.rest_3_ = bf16[48,128]{1,0:T(8,128)(2,1)S(1)} collective-permute-done((bf16[48,128]{1,0:T(8,128)(2,1)S(1)}, bf16[48,128]{1,0:T(8,128)(2,1)S(1)}, u32[]{:S(2)}, u32[]{:S(2)}) %collective-permute-start.16) | collective-permute-done | bytes 12320 | tf_op jit(solution)/shard_map/ppermute | solution.py:526
  60.6 0.0 collective-permute-done.12.north.rest_2_
  60.6 1.8 %collective-permute-done.13.south.rest_1_ = bf16[368,128]{1,0:T(8,128)(2,1)S(1)} collective-permute-done((bf16[368,128]{1,0:T(8,128)(2,1)S(1)}, bf16[368,128]{1,0:T(8,128)(2,1)S(1)}, u32[]{:S(2)}, u32[]{:S(2)}) %collective-permute-start.13) | collective-permute-done | bytes 94240 | tf_op jit(solution)/shard_map/ppermute | solution.py:388
  62.4 0.3 lat_smooth.1.rest_0_
  62.7 0.0 collective-permute-start.23
  62.7 0.5 collective-permute-start.15
  63.2 0.0 collective-permute-start.22
  63.2 0.0 collective-permute-start.21
  63.2 0.0 collective-permute-done.14.east
  63.2 5.7 %collective-permute-start.20 = (bf16[40,128]{1,0:T(8,128)(2,1)S(1)}, bf16[40,128]{1,0:T(8,128)(2,1)S(1)}, u32[]{:S(2)}, u32[]{:S(2)}) collective-permute-start(bf16[40,128]{1,0:T(8,128)(2,1)S(1)} %lat_smooth.1.rest_0_), channel_id=1, source_target_pairs={{0,4},{1,5},{2,6},{3,7},{4,0},{5,1},{6,2},{7,3},{8,12},{9,13},{10,... | collective-permute-start | bytes 30728 | tf_op jit(solution)/shard_map/ppermute | solution.py:534
  68.9 0.0 collective-permute-done.15.west
  68.9 0.0 collective-permute-start.19
  68.9 0.0 collective-permute-done.23.rest_7_
  69.0 0.3 collective-permute-start.18
  69.2 0.0 collective-permute-done.22.rest_6_
  69.2 0.4 collective-permute-start.17
  69.6 2.2 %last.1 = f32[2528,128]{1,0:T(8,128)} custom-call(f32[2528,128]{1,0:T(8,128)S(1)} %get-tuple-element.46.mixed, bf16[368,128]{1,0:T(8,128)(2,1)S(1)} %collective-permute-done.12.north.rest_2_, bf16[368,128]{1,0:T(8,128)(2,1)S(1)} %collective-permute-done.13.south.rest_1_, f32[1,2528]{1,0:T(1,128)S(1)} %collective-permute-done.14.east, ...), custom_call_target="tpu_custom_call" | custom-call | tf_op jit(solution)/shard_map/last/pallas_call | solution.py:536
  71.9 0.0 collective-permute-done.21.rest_5_
  71.9 0.0 collective-permute-done.20.rest_4_
  71.9 1.1 %collective-permute-done.19.rest_3_ = bf16[40,128]{1,0:T(8,128)(2,1)S(1)} collective-permute-done((bf16[40,128]{1,0:T(8,128)(2,1)S(1)}, bf16[40,128]{1,0:T(8,128)(2,1)S(1)}, u32[]{:S(2)}, u32[]{:S(2)}) %collective-permute-start.19) | collective-permute-done | bytes 10272 | tf_op jit(solution)/shard_map/ppermute | solution.py:534
  72.9 1.5 %collective-permute-done.18.rest_2_ = bf16[40,128]{1,0:T(8,128)(2,1)S(1)} collective-permute-done((bf16[40,128]{1,0:T(8,128)(2,1)S(1)}, bf16[40,128]{1,0:T(8,128)(2,1)S(1)}, u32[]{:S(2)}, u32[]{:S(2)}) %collective-permute-start.18) | collective-permute-done | bytes 10272 | tf_op jit(solution)/shard_map/ppermute | solution.py:534
  74.5 1.1 %lon_smooth.1 = f32[32,128]{1,0:T(8,128)} custom-call(bf16[128,1024]{1,0:T(8,128)(2,1)S(1)} %copy-done.10, bf16[40,128]{1,0:T(8,128)(2,1)S(1)} %lat_smooth.1.rest_0_, bf16[40,128]{1,0:T(8,128)(2,1)S(1)} %collective-permute-done.17.rest_1_, bf16[40,128]{1,0:T(8,128)(2,1)S(1)} %collective-permute-done.18.rest_2_, ...), custom_call_target="tpu_custom_call" | custom-call | tf_op jit(solution)/shard_map/lon_smooth/pallas_call | solution.py:547
  (24 shorter events, 0.0 us)
Async XLA Ops:
  0.6 26.3 %copy-start = (bf16[4,4,79,8,128]{4,3,2,1,0:T(8,128)(2,1)S(1)}, bf16[4,4,79,8,128]{4,3,2,1,0:T(8,128)(2,1)}, u32[]{:S(2)}) copy-start(bf16[4,4,79,8,128]{4,3,2,1,0:T(8,128)(2,1)} %fraction.9) | copy-start | bytes 7766020
  5.1 13.6 %copy-start.13 = (f32[1,2688]{1,0:T(1,128)S(1)}, f32[1,2688]{1,0:T(1,128)}, u32[]{:S(2)}) copy-start(f32[1,2688]{1,0:T(1,128)} %get-tuple-element.31) | copy-start | bytes 32260
  5.1 13.6 %copy-start.12 = (f32[1,2688]{1,0:T(1,128)S(1)}, f32[1,2688]{1,0:T(1,128)}, u32[]{:S(2)}) copy-start(f32[1,2688]{1,0:T(1,128)} %get-tuple-element.30) | copy-start | bytes 32260
  5.1 21.8 %copy-start.1 = (bf16[640,640]{1,0:T(8,128)(2,1)S(1)}, bf16[640,640]{1,0:T(8,128)(2,1)}, u32[]{:S(2)}) copy-start(bf16[640,640]{1,0:T(8,128)(2,1)} %get-tuple-element.32.kron) | copy-start | bytes 2457604
  8.6 38.2 %all-to-all-start = ((bf16[32,48,128]{2,1,0:T(8,128)(2,1)}), bf16[32,48,128]{2,1,0:T(8,128)(2,1)}, u32[]{:S(2)}, u32[]{:S(2)}) async-start(bf16[32,48,128]{2,1,0:T(8,128)(2,1)} %bitcast.8), calls=%async_computation | async-start | bytes 786432 | tf_op jit(solution)/shard_map/all_to_all | solution.py:480
  16.1 10.6 %collective-permute-start = (bf16[332,128]{1,0:T(8,128)(2,1)}, bf16[332,128]{1,0:T(8,128)(2,1)S(1)}, u32[]{:S(2)}, u32[]{:S(2)}) collective-permute-start(bf16[332,128]{1,0:T(8,128)(2,1)} %get-tuple-element.28), channel_id=1, source_target_pairs={{0,24},{8,0},{16,8},{24,16},{1,25},{9,1},{17,9},{25,17},{2,26},{10... | collective-permute-start | bytes 254984 | tf_op jit(solution)/shard_map/ppermute | solution.py:389
  18.7 8.2 %collective-permute-start.1 = (bf16[332,128]{1,0:T(8,128)(2,1)}, bf16[332,128]{1,0:T(8,128)(2,1)S(1)}, u32[]{:S(2)}, u32[]{:S(2)}) collective-permute-start(bf16[332,128]{1,0:T(8,128)(2,1)} %get-tuple-element.29), channel_id=1, source_target_pairs={{0,8},{8,16},{16,24},{24,0},{1,9},{9,17},{17,25},{25,1},{2,10},{10... | collective-permute-start | bytes 254984 | tf_op jit(solution)/shard_map/ppermute | solution.py:388
  18.7 7.9 %collective-permute-start.3 = (f32[1,2688]{1,0:T(1,128)S(1)}, f32[1,2688]{1,0:T(1,128)S(1)}, u32[]{:S(2)}, u32[]{:S(2)}) collective-permute-start(f32[1,2688]{1,0:T(1,128)S(1)} %copy-done.13), channel_id=1, source_target_pairs={{0,1},{1,2},{2,3},{3,4},{4,5},{5,6},{6,7},{7,0},{8,9},{9,10},{10,1... | collective-permute-start | bytes 32264 | tf_op jit(solution)/shard_map/ppermute | solution.py:391
  18.8 7.9 %collective-permute-start.2 = (f32[1,2688]{1,0:T(1,128)S(1)}, f32[1,2688]{1,0:T(1,128)S(1)}, u32[]{:S(2)}, u32[]{:S(2)}) collective-permute-start(f32[1,2688]{1,0:T(1,128)S(1)} %copy-done.12), channel_id=1, source_target_pairs={{0,7},{1,0},{2,1},{3,2},{4,3},{5,4},{6,5},{7,6},{8,15},{9,8},{10,9... | collective-permute-start | bytes 32264 | tf_op jit(solution)/shard_map/ppermute | solution.py:390
  26.9 4.2 %copy-start.8 = (bf16[332,128]{1,0:T(8,128)(2,1)}, bf16[332,128]{1,0:T(8,128)(2,1)S(1)}, u32[]{:S(2)}) copy-start(bf16[332,128]{1,0:T(8,128)(2,1)S(1)} %collective-permute-done.1.south.rest_3_) | copy-start | bytes 254980
  26.9 1.0 %copy-start.2 = (bf16[2,79,8,128]{3,2,1,0:T(8,128)(2,1)S(1)}, bf16[2,79,8,128]{3,2,1,0:T(8,128)(2,1)}, u32[]{:S(2)}) copy-start(bf16[2,79,8,128]{3,2,1,0:T(8,128)(2,1)} %profiles.7) | copy-start | bytes 970756
  27.9 1.3 %copy-start.5 = (f32[2528,128]{1,0:T(8,128)S(1)}, f32[2528,128]{1,0:T(8,128)}, u32[]{:S(2)}) copy-start(f32[2528,128]{1,0:T(8,128)} %get-tuple-element.27.mixed) | copy-start | bytes 3883012
  29.2 11.6 %copy-start.3 = (bf16[2,79,8,128]{3,2,1,0:T(8,128)(2,1)S(1)}, bf16[2,79,8,128]{3,2,1,0:T(8,128)(2,1)}, u32[]{:S(2)}) copy-start(bf16[2,79,8,128]{3,2,1,0:T(8,128)(2,1)} %profiles.7) | copy-start | bytes 970756
  31.2 9.7 %collective-permute-start.4 = (bf16[316,128]{1,0:T(8,128)(2,1)S(1)}, bf16[316,128]{1,0:T(8,128)(2,1)S(1)}, u32[]{:S(2)}, u32[]{:S(2)}) collective-permute-start(bf16[316,128]{1,0:T(8,128)(2,1)S(1)} %get-tuple-element.34), channel_id=1, source_target_pairs={{0,24},{8,0},{16,8},{24,16},{1,25},{9,1},{17,9},{25,17},{2,26},{10... | collective-permute-start | bytes 242696 | tf_op jit(solution)/shard_map/ppermute | solution.py:389
  33.4 7.5 %collective-permute-start.5 = (bf16[316,128]{1,0:T(8,128)(2,1)S(1)}, bf16[316,128]{1,0:T(8,128)(2,1)S(1)}, u32[]{:S(2)}, u32[]{:S(2)}) collective-permute-start(bf16[316,128]{1,0:T(8,128)(2,1)S(1)} %get-tuple-element.35), channel_id=1, source_target_pairs={{0,8},{8,16},{16,24},{24,0},{1,9},{9,17},{17,25},{25,1},{2,10},{10... | collective-permute-start | bytes 242696 | tf_op jit(solution)/shard_map/ppermute | solution.py:388
  33.4 3.9 %collective-permute-start.6 = (f32[1,2528]{1,0:T(1,128)S(1)}, f32[1,2528]{1,0:T(1,128)S(1)}, u32[]{:S(2)}, u32[]{:S(2)}) collective-permute-start(f32[1,2528]{1,0:T(1,128)S(1)} %get-tuple-element.36), channel_id=1, source_target_pairs={{0,7},{1,0},{2,1},{3,2},{4,3},{5,4},{6,5},{7,6},{8,15},{9,8},{10,9... | collective-permute-start | bytes 30344 | tf_op jit(solution)/shard_map/ppermute | solution.py:390
  35.9 4.9 %collective-permute-start.7 = (f32[1,2528]{1,0:T(1,128)S(1)}, f32[1,2528]{1,0:T(1,128)S(1)}, u32[]{:S(2)}, u32[]{:S(2)}) collective-permute-start(f32[1,2528]{1,0:T(1,128)S(1)} %get-tuple-element.37), channel_id=1, source_target_pairs={{0,1},{1,2},{2,3},{3,4},{4,5},{5,6},{6,7},{7,0},{8,9},{9,10},{10,1... | collective-permute-start | bytes 30344 | tf_op jit(solution)/shard_map/ppermute | solution.py:391
  43.3 1.1 %copy-start.6 = (f32[2528,128]{1,0:T(8,128)}, f32[2528,128]{1,0:T(8,128)S(1)}, u32[]{:S(2)}) copy-start(f32[2528,128]{1,0:T(8,128)S(1)} %get-tuple-element.39.mixed) | copy-start | bytes 3883012
  44.3 7.2 %collective-permute-start.8 = (bf16[316,128]{1,0:T(8,128)(2,1)}, bf16[316,128]{1,0:T(8,128)(2,1)}, u32[]{:S(2)}, u32[]{:S(2)}) collective-permute-start(bf16[316,128]{1,0:T(8,128)(2,1)} %get-tuple-element.40), channel_id=1, source_target_pairs={{0,24},{8,0},{16,8},{24,16},{1,25},{9,1},{17,9},{25,17},{2,26},{10... | collective-permute-start | bytes 242696 | tf_op jit(solution)/shard_map/ppermute | solution.py:389
  45.8 5.8 %collective-permute-start.9 = (bf16[316,128]{1,0:T(8,128)(2,1)}, bf16[316,128]{1,0:T(8,128)(2,1)}, u32[]{:S(2)}, u32[]{:S(2)}) collective-permute-start(bf16[316,128]{1,0:T(8,128)(2,1)} %get-tuple-element.41), channel_id=1, source_target_pairs={{0,8},{8,16},{16,24},{24,0},{1,9},{9,17},{17,25},{25,1},{2,10},{10... | collective-permute-start | bytes 242696 | tf_op jit(solution)/shard_map/ppermute | solution.py:388
  46.3 3.3 %collective-permute-start.10 = (f32[1,2528]{1,0:T(1,128)}, f32[1,2528]{1,0:T(1,128)S(1)}, u32[]{:S(2)}, u32[]{:S(2)}) collective-permute-start(f32[1,2528]{1,0:T(1,128)} %get-tuple-element.42), channel_id=1, source_target_pairs={{0,7},{1,0},{2,1},{3,2},{4,3},{5,4},{6,5},{7,6},{8,15},{9,8},{10,9... | collective-permute-start | bytes 30344 | tf_op jit(solution)/shard_map/ppermute | solution.py:390
  46.3 5.2 %collective-permute-start.11 = (f32[1,2528]{1,0:T(1,128)}, f32[1,2528]{1,0:T(1,128)}, u32[]{:S(2)}, u32[]{:S(2)}) collective-permute-start(f32[1,2528]{1,0:T(1,128)} %get-tuple-element.43), channel_id=1, source_target_pairs={{0,1},{1,2},{2,3},{3,4},{4,5},{5,6},{6,7},{7,0},{8,9},{9,10},{10,1... | collective-permute-start | bytes 30344 | tf_op jit(solution)/shard_map/ppermute | solution.py:391
  46.9 4.7 %copy-start.4 = (bf16[2,79,8,128]{3,2,1,0:T(8,128)(2,1)S(1)}, bf16[2,79,8,128]{3,2,1,0:T(8,128)(2,1)}, u32[]{:S(2)}) copy-start(bf16[2,79,8,128]{3,2,1,0:T(8,128)(2,1)} %profiles.7) | copy-start | bytes 970756
  46.9 4.7 %copy-start.7 = (f32[2528,128]{1,0:T(8,128)S(1)}, f32[2528,128]{1,0:T(8,128)}, u32[]{:S(2)}) copy-start(f32[2528,128]{1,0:T(8,128)} %copy-done.6) | copy-start | bytes 3883012
  46.9 4.7 %copy-start.9 = (bf16[332,128]{1,0:T(8,128)(2,1)S(1)}, bf16[332,128]{1,0:T(8,128)(2,1)}, u32[]{:S(2)}) copy-start(bf16[332,128]{1,0:T(8,128)(2,1)} %copy-done.8) | copy-start | bytes 254980
  51.6 10.8 %copy-start.11 = (bf16[32,32]{1,0:T(8,128)(2,1)S(1)}, bf16[32,32]{1,0:T(8,128)(2,1)}, u32[]{:S(2)}) copy-start(bf16[32,32]{1,0:T(8,128)(2,1)} %matrix.2) | copy-start | bytes 6148
  54.5 6.1 %collective-permute-start.12 = (bf16[368,128]{1,0:T(8,128)(2,1)S(1)}, bf16[368,128]{1,0:T(8,128)(2,1)S(1)}, u32[]{:S(2)}, u32[]{:S(2)}) collective-permute-start(bf16[368,128]{1,0:T(8,128)(2,1)S(1)} %get-tuple-element.47), channel_id=1, source_target_pairs={{0,24},{8,0},{16,8},{24,16},{1,25},{9,1},{17,9},{25,17},{2,26},{10... | collective-permute-start | bytes 282632 | tf_op jit(solution)/shard_map/ppermute | solution.py:389
  56.9 5.5 %collective-permute-start.13 = (bf16[368,128]{1,0:T(8,128)(2,1)S(1)}, bf16[368,128]{1,0:T(8,128)(2,1)S(1)}, u32[]{:S(2)}, u32[]{:S(2)}) collective-permute-start(bf16[368,128]{1,0:T(8,128)(2,1)S(1)} %get-tuple-element.48), channel_id=1, source_target_pairs={{0,8},{8,16},{16,24},{24,0},{1,9},{9,17},{17,25},{25,1},{2,10},{10... | collective-permute-start | bytes 282632 | tf_op jit(solution)/shard_map/ppermute | solution.py:388
  56.9 3.7 %collective-permute-start.16 = (bf16[48,128]{1,0:T(8,128)(2,1)S(1)}, bf16[48,128]{1,0:T(8,128)(2,1)S(1)}, u32[]{:S(2)}, u32[]{:S(2)}) collective-permute-start(bf16[48,128]{1,0:T(8,128)(2,1)S(1)} %get-tuple-element.51.rest_0_), channel_id=1, source_target_pairs={{0,16},{8,24},{16,0},{24,8},{1,17},{9,25},{17,1},{25,9},{2,18},{10... | collective-permute-start | bytes 36872 | tf_op jit(solution)/shard_map/ppermute | solution.py:526
  57.6 5.6 %collective-permute-start.14 = (f32[1,2528]{1,0:T(1,128)S(1)}, f32[1,2528]{1,0:T(1,128)S(1)}, u32[]{:S(2)}, u32[]{:S(2)}) collective-permute-start(f32[1,2528]{1,0:T(1,128)S(1)} %get-tuple-element.49), channel_id=1, source_target_pairs={{0,7},{1,0},{2,1},{3,2},{4,3},{5,4},{6,5},{7,6},{8,15},{9,8},{10,9... | collective-permute-start | bytes 30344 | tf_op jit(solution)/shard_map/ppermute | solution.py:390
  62.7 6.3 %collective-permute-start.23 = (bf16[40,128]{1,0:T(8,128)(2,1)S(1)}, bf16[40,128]{1,0:T(8,128)(2,1)S(1)}, u32[]{:S(2)}, u32[]{:S(2)}) collective-permute-start(bf16[40,128]{1,0:T(8,128)(2,1)S(1)} %lat_smooth.1.rest_0_), channel_id=1, source_target_pairs={{0,7},{1,0},{2,1},{3,2},{4,3},{5,4},{6,5},{7,6},{8,15},{9,8},{10,9... | collective-permute-start | bytes 30728 | tf_op jit(solution)/shard_map/ppermute | solution.py:534
  62.7 6.2 %collective-permute-start.15 = (f32[1,2528]{1,0:T(1,128)S(1)}, f32[1,2528]{1,0:T(1,128)S(1)}, u32[]{:S(2)}, u32[]{:S(2)}) collective-permute-start(f32[1,2528]{1,0:T(1,128)S(1)} %get-tuple-element.50), channel_id=1, source_target_pairs={{0,1},{1,2},{2,3},{3,4},{4,5},{5,6},{6,7},{7,0},{8,9},{9,10},{10,1... | collective-permute-start | bytes 30344 | tf_op jit(solution)/shard_map/ppermute | solution.py:391
  63.2 6.0 %collective-permute-start.22 = (bf16[40,128]{1,0:T(8,128)(2,1)S(1)}, bf16[40,128]{1,0:T(8,128)(2,1)S(1)}, u32[]{:S(2)}, u32[]{:S(2)}) collective-permute-start(bf16[40,128]{1,0:T(8,128)(2,1)S(1)} %lat_smooth.1.rest_0_), channel_id=1, source_target_pairs={{0,6},{1,7},{2,0},{3,1},{4,2},{5,3},{6,4},{7,5},{8,14},{9,15},{10,... | collective-permute-start | bytes 30728 | tf_op jit(solution)/shard_map/ppermute | solution.py:534
  63.2 8.7 %collective-permute-start.21 = (bf16[40,128]{1,0:T(8,128)(2,1)S(1)}, bf16[40,128]{1,0:T(8,128)(2,1)S(1)}, u32[]{:S(2)}, u32[]{:S(2)}) collective-permute-start(bf16[40,128]{1,0:T(8,128)(2,1)S(1)} %lat_smooth.1.rest_0_), channel_id=1, source_target_pairs={{0,5},{1,6},{2,7},{3,0},{4,1},{5,2},{6,3},{7,4},{8,13},{9,14},{10,... | collective-permute-start | bytes 30728 | tf_op jit(solution)/shard_map/ppermute | solution.py:534
  63.2 8.7 %collective-permute-start.20 = (bf16[40,128]{1,0:T(8,128)(2,1)S(1)}, bf16[40,128]{1,0:T(8,128)(2,1)S(1)}, u32[]{:S(2)}, u32[]{:S(2)}) collective-permute-start(bf16[40,128]{1,0:T(8,128)(2,1)S(1)} %lat_smooth.1.rest_0_), channel_id=1, source_target_pairs={{0,4},{1,5},{2,6},{3,7},{4,0},{5,1},{6,2},{7,3},{8,12},{9,13},{10,... | collective-permute-start | bytes 30728 | tf_op jit(solution)/shard_map/ppermute | solution.py:534
  68.9 4.0 %collective-permute-start.19 = (bf16[40,128]{1,0:T(8,128)(2,1)S(1)}, bf16[40,128]{1,0:T(8,128)(2,1)S(1)}, u32[]{:S(2)}, u32[]{:S(2)}) collective-permute-start(bf16[40,128]{1,0:T(8,128)(2,1)S(1)} %lat_smooth.1.rest_0_), channel_id=1, source_target_pairs={{0,3},{1,4},{2,5},{3,6},{4,7},{5,0},{6,1},{7,2},{8,11},{9,12},{10,... | collective-permute-start | bytes 30728 | tf_op jit(solution)/shard_map/ppermute | solution.py:534
  69.0 5.5 %collective-permute-start.18 = (bf16[40,128]{1,0:T(8,128)(2,1)S(1)}, bf16[40,128]{1,0:T(8,128)(2,1)S(1)}, u32[]{:S(2)}, u32[]{:S(2)}) collective-permute-start(bf16[40,128]{1,0:T(8,128)(2,1)S(1)} %lat_smooth.1.rest_0_), channel_id=1, source_target_pairs={{0,2},{1,3},{2,4},{3,5},{4,6},{5,7},{6,0},{7,1},{8,10},{9,11},{10,... | collective-permute-start | bytes 30728 | tf_op jit(solution)/shard_map/ppermute | solution.py:534
  69.2 5.2 %collective-permute-start.17 = (bf16[40,128]{1,0:T(8,128)(2,1)S(1)}, bf16[40,128]{1,0:T(8,128)(2,1)S(1)}, u32[]{:S(2)}, u32[]{:S(2)}) collective-permute-start(bf16[40,128]{1,0:T(8,128)(2,1)S(1)} %lat_smooth.1.rest_0_), channel_id=1, source_target_pairs={{0,1},{1,2},{2,3},{3,4},{4,5},{5,6},{6,7},{7,0},{8,9},{9,10},{10,1... | collective-permute-start | bytes 30728 | tf_op jit(solution)/shard_map/ppermute | solution.py:534
  69.6 4.8 %copy-start.10 = (bf16[128,1024]{1,0:T(8,128)(2,1)S(1)}, bf16[128,1024]{1,0:T(8,128)(2,1)}, u32[]{:S(2)}) copy-start(bf16[128,1024]{1,0:T(8,128)(2,1)} %matrix.3) | copy-start | bytes 786436

commit v5 on v4

--- a/solution.py
+++ b/solution.py
@@ -176,7 +176,10 @@
     return out
 
 
-def step_body(dims, last, mixed, north, south, east, west, fraction, profiles, kron, surface, *rest):
+def step_body(dims, opening, last, mixed, north, south, east, west, fraction, profiles, kron, *rest):
+    surface = None
+    if not opening:
+        surface, *rest = rest
     if last:
         extra, rest = rest[:6], rest[6:]
     new_mixed, up, down, to_west, to_east, new_surface, north_scr, south_scr, sides, adj, low, mix = rest
@@ -197,10 +200,9 @@
     over_levels(levels, body)
     convect(dims, adj, low, mix, kron, profiles, new_mixed)
     send_edges(dims, new_mixed, up, down, to_west, to_east)
-    total = [
-        surface[t * rows : (t + 1) * rows, :] + adj[t * levels * rows : t * levels * rows + rows, :]
-        for t in range(tracers)
-    ]
+    total = [adj[t * levels * rows : t * levels * rows + rows, :] for t in range(tracers)]
+    if surface is not None:
+        total = [surface[t * rows : (t + 1) * rows, :] + total[t] for t in range(tracers)]
     if last:
         patch(dims, new_mixed, total, *extra, new_surface)
         at = up.shape[0] - new_surface.shape[0]
@@ -357,15 +359,23 @@
     ends = jnp.concatenate([p[p.shape[0] - 8 :, 0:each].astype(F32) for p in parts], axis=1).astype(BF16)
     ends = dot_nt(ends, weights)
     ends = jnp.concatenate([ends, jnp.zeros((8, LANES - size), F32)], axis=1)
-    whole = jnp.concatenate([total, ends], axis=0).astype(BF16)
-    out[...] = whole
+    out[...] = jnp.concatenate([total, ends], axis=0)
+
+
+def pair_body(own, other, out):
+    half = own.shape[0]
+    first_core = lax.axis_index("lon") % 2 == 0
+    out[0:half, :] = jnp.where(first_core, own[...], other[...])
+    out[half:, :] = jnp.where(first_core, other[...], own[...])
 
 
 def lon_body(matrix, *rest):
-    *parts, out = rest
+    *pairs, out = rest
+    half = pairs[0].shape[0] // 2
+    parts = [p[at : at + half, :] for p in pairs for at in (half, 0)]
     count = len(parts)
     size = out.shape[0]
-    lon = lax.axis_index("lon")
+    lon = lax.axis_index("lon") // 2 * 2 + 1
     ends = [p[size : size + 8, :].astype(F32)[:, 0:size] for p in parts]
     east = jnp.concatenate([ends[(s + 1) % count][1:2] for s in range(count)], axis=1)
     west = jnp.concatenate([ends[(s - 1) % count][0:1] for s in range(count)], axis=1)
@@ -468,7 +478,7 @@
             full(obs_resid.shape),
         ],
         out_specs=full((rows_out, LANES)),
-        compiler_params=params(60 << 20),
+        compiler_params=params(),
         name="pack",
     )(
         obs_owner.reshape(1, blocks),
@@ -489,7 +499,6 @@
         name="forcing",
     )(got.reshape(rows_out, LANES))
 
-    surface = jnp.zeros(surface_type.shape, F32)
     lon_count = lax.axis_size("lon")
     patch_rows = (tracers * (rows + 2) + 7) // 8 * 8
     patch_type = jax.ShapeDtypeStruct((patch_rows + 8, LANES), BF16)
@@ -499,16 +508,20 @@
         frac_spec = pl.BlockSpec((1,) + fractions.shape[1:], lambda i, n=step_index: (n, 0, 0, 0, 0))
         halo_types = long_edges if step_index == STEPS - 1 else edges
         outs = [tall, tall, side_edge, side_edge] if last else edges
-        ins = [mixed, *halo, fractions, profiles, kron, surface]
+        opening = step_index == STEPS - 1
+        ins = [mixed, *halo, fractions, profiles, kron]
         in_specs = [spec(state)] + [spec(h) for h in halo_types]
-        in_specs += [frac_spec, full(profiles.shape), spec(kron_type), spec(surface_type)]
+        in_specs += [frac_spec, full(profiles.shape), spec(kron_type)]
+        if not opening:
+            ins.append(surface)
+            in_specs.append(spec(surface_type))
         result = surface_type
         if last:
             ins += [fractions, forcing, *first_halo]
             in_specs += [level_zero, pl.BlockSpec((rows, wide), lambda i: (0, 0))] + [spec(h) for h in long_edges]
             result = patch_type
         mixed, *out, surface = pl.pallas_call(
-            functools.partial(step_body, dims, last),
+            functools.partial(step_body, dims, opening, last),
             grid=(1,),
             out_shape=[state] + outs + [result],
             in_specs=in_specs,
@@ -527,11 +540,18 @@
         offsets.append(-shift)
     bands = pl.pallas_call(
         functools.partial(lat_body, tracers, rows, offsets),
-        out_shape=jax.ShapeDtypeStruct((tracers * rows + 8, LANES), BF16),
+        out_shape=jax.ShapeDtypeStruct((tracers * rows + 8, LANES), F32),
         compiler_params=params(),
         name="lat_smooth",
     )(lat_matrix, *parts)
-    shifts = [lax.ppermute(bands, "lon", ring("lon", shift)) for shift in range(1, lon_count)]
+    other = lax.ppermute(bands, "lon", [(i, i ^ 1) for i in range(lon_count)])
+    pair = pl.pallas_call(
+        pair_body,
+        out_shape=jax.ShapeDtypeStruct((2 * bands.shape[0], LANES), F32),
+        compiler_params=params(),
+        name="pair",
+    )(bands, other)
+    shifts = [lax.ppermute(pair, "lon", ring("lon", shift)) for shift in range(2, lon_count, 2)]
     frac_spec = pl.BlockSpec((1,) + fractions.shape[1:], lambda i: (0, 0, 0, 0, 0))
     adjoint = pl.pallas_call(
         functools.partial(last_body, dims),
@@ -549,7 +569,7 @@
         out_shape=surface_type,
         compiler_params=params(),
         name="lon_smooth",
-    )(lon_matrix, bands, *shifts)
+    )(lon_matrix, pair, *shifts)
     return adjoint.reshape(adjoint_in.shape), smoothed.reshape(tracers, rows, LANES)
 
 

time: 75.9 us -> 75.2 us (level)
  waiting for transfers between devices: 18.2 us -> 22.3 us
  starting transfers between devices: 31.5 us -> 27.6 us
  Pallas kernels: 21.6 us -> 19.8 us
  local copies, waits for them, and re-layouts: 3.41 us -> 4.21 us
    ppermute x7 -> x4, starting transfers between devices: 6.42 us -> 2.06 us  [the longest x3 2.06 us: window(): lax.ppermute(pair, 'lon', ring('lon', shift))]
    ppermute x4, waiting for transfers between devices: 9.73 us -> 13.2 us  [exchange(): west = lax.ppermute(to_east, 'lon', ring('lon', 1))]
    pallas_call x1, Pallas kernels: 3.5 us -> 1.73 us  [window(): pl.pallas_call(functools.partial(pack_body, (devices, blocks, slots, leve...]
    ppermute x7 -> x4, waiting for transfers between devices: 2.63 us -> 1.2 us  [the longest x1 1.2 us: window(): other = lax.ppermute(bands, 'lon', [(i, i ^ 1) for i in range(lon_count)])]
    ppermute x4, waiting for transfers between devices: 1.39 us -> 2.77 us  [exchange(): east = lax.ppermute(to_west, 'lon', ring('lon', -1))]
    ppermute x4, starting transfers between devices: 6.71 us -> 7.6 us  [exchange(): east = lax.ppermute(to_west, 'lon', ring('lon', -1))]
    unnamed x28 -> x40, local copies, waits for them, and re-layouts: 3.41 us -> 4.21 us
    pallas_call x3 -> x4, Pallas kernels: 7.25 us -> 7.3 us  [the longest x3 7.29 us: window(): pl.pallas_call(functools.partial(step_body, dims, opening, last), grid=(1...]
  transfers between devices with their start and end apart: 25 -> 22, of which waited for: 9 -> 10; matrix products, arithmetic and copies ran while one was open for 0% -> 0% of each run, Pallas kernels for 13% -> 13%
where the time goes in v5:
time: 75.2 us; the launch traced here: 74.9 us
  starting transfers between devices  27.6 us (37%)
  waiting for transfers between devices  22.3 us (30%)
  Pallas kernels  19.8 us (26%)
  local copies, waits for them, and re-layouts  4.21 us (6%)
  between operations  0.91 us (1%)
    ppermute x4, waiting for transfers between devices, exchange(): west = lax.ppermute(to_east, 'lon', ring('lon', 1))  13.2 us
    ppermute x4, starting transfers between devices, exchange(): north = lax.ppermute(down, 'lat', ring('lat', -1))  8.77 us
    ppermute x4, starting transfers between devices, exchange(): east = lax.ppermute(to_west, 'lon', ring('lon', -1))  7.6 us
    all_to_all x1, starting transfers between devices, window(): lax.all_to_all(packed.reshape(devices, CAPACITY * slots, LANES), BOTH, sp...  7.44 us
    pallas_call x3, Pallas kernels, window(): pl.pallas_call(functools.partial(step_body, dims, opening, last), grid=(1...  7.29 us
    pallas_call x1, Pallas kernels, window(): pl.pallas_call(functools.partial(first_body, dims), grid=(1,), out_shape=...  4.45 us
    unnamed x40, local copies, waits for them, and re-layouts  4.21 us
    ppermute x1, waiting for transfers between devices, window(): parts.append(lax.ppermute(surface, 'lat', ring('lat', shift)))  3.07 us
  transfers between devices with their start and end apart: 22, of which 10 were waited for; matrix products, arithmetic and copies ran while one was open for 0% of the time, Pallas kernels for 13%

profile of v5, /device:TPU:0, one launch (start us, length us, event | category | flops | bytes accessed | tf_op | source)
XLA Modules:
  0.0 74.9 jit_solution(9659978090969165999)
XLA Ops:
  0.6 0.0 copy-start.12
  0.6 0.0 copy-start.13
  0.7 0.0 copy-start.15
  0.7 0.0 copy-start.16
  0.7 0.0 copy-start.17
  0.7 4.4 %first.1 = (f32[2528,128]{1,0:T(8,128)}, bf16[640,640]{1,0:T(8,128)(2,1)}, bf16[332,128]{1,0:T(8,128)(2,1)}, bf16[332,128]{1,0:T(8,128)(2,1)}, f32[1,2688]{1,0:T(1,128)}, /*index=5*/f32[1,2688]{1,0:T(1,128)}) custom-call(bf16[79,79]{1,0:T(8,128)(2,1)} %kernel.1, bf16[2,79,8,128]{3,2,1,0:T(8,128)(2,1)} %profiles.7, f32[2528,128]{1,0:T(8,128)} %bitcast.12, ...), custom_call_target="tpu_custom_call" | custom-call | tf_op jit(solution)/shard_map/first/pallas_call | solution.py:446
  5.2 0.0 copy-start.18
  5.2 1.7 %pack.1 = bf16[1536,128]{1,0:T(8,128)(2,1)S(1)} custom-call(s32[1,128]{1,0:T(1,128)S(1)} %bitcast.10, s32[1,128]{1,0:T(1,128)S(1)} %bitcast.11, s32[1,1024]{1,0:T(1,128)S(1)} %bitcast.9, bf16[79,1024]{1,0:T(8,128)(2,1)S(1)} %copy-done.12, bf16[4,1024]{1,0:T(4,128)(2,1)S(1)} %copy-done.13), custom_call_target="tpu_custom_call" | custom-call | tf_op jit(solution)/shard_map/pack/pallas_call | solution.py:469
  7.0 0.8 %copy-done.5 = bf16[1536,128]{1,0:T(8,128)(2,1)} copy-done((bf16[1536,128]{1,0:T(8,128)(2,1)}, bf16[1536,128]{1,0:T(8,128)(2,1)S(1)}, u32[]{:S(2)}) %copy-start.5) | copy-done | bytes 393240
  7.8 7.4 %all-to-all-start = ((bf16[32,48,128]{2,1,0:T(8,128)(2,1)}), bf16[32,48,128]{2,1,0:T(8,128)(2,1)}, u32[]{:S(2)}, u32[]{:S(2)}) async-start(bf16[32,48,128]{2,1,0:T(8,128)(2,1)} %bitcast.8), calls=%async_computation | async-start | bytes 786432 | tf_op jit(solution)/shard_map/all_to_all | solution.py:490
  15.2 2.7 %collective-permute-start = (bf16[332,128]{1,0:T(8,128)(2,1)}, bf16[332,128]{1,0:T(8,128)(2,1)S(1)}, u32[]{:S(2)}, u32[]{:S(2)}) collective-permute-start(bf16[332,128]{1,0:T(8,128)(2,1)} %get-tuple-element.28), channel_id=1, source_target_pairs={{0,24},{8,0},{16,8},{24,16},{1,25},{9,1},{17,9},{25,17},{2,26},{10... | collective-permute-start | bytes 254984 | tf_op jit(solution)/shard_map/ppermute | solution.py:399
  17.9 0.0 collective-permute-start.1
  17.9 0.0 collective-permute-start.3
  17.9 3.5 %collective-permute-start.2 = (f32[1,2688]{1,0:T(1,128)S(1)}, f32[1,2688]{1,0:T(1,128)S(1)}, u32[]{:S(2)}, u32[]{:S(2)}) collective-permute-start(f32[1,2688]{1,0:T(1,128)S(1)} %copy-done.18), channel_id=1, source_target_pairs={{0,7},{1,0},{2,1},{3,2},{4,3},{5,4},{6,5},{7,6},{8,15},{9,8},{10,9... | collective-permute-start | bytes 32264 | tf_op jit(solution)/shard_map/ppermute | solution.py:400
  21.4 4.3 %collective-permute-done.3.west.rest_6_ = f32[1,2688]{1,0:T(1,128)S(1)} collective-permute-done((f32[1,2688]{1,0:T(1,128)S(1)}, f32[1,2688]{1,0:T(1,128)S(1)}, u32[]{:S(2)}, u32[]{:S(2)}) %collective-permute-start.3) | collective-permute-done | bytes 10784 | tf_op jit(solution)/shard_map/ppermute | solution.py:401
  25.8 0.0 collective-permute-done.2.east.rest_5_
  25.8 0.0 collective-permute-done.north.rest_3_
  25.8 0.3 collective-permute-done.1.south.rest_4_
  26.0 1.0 %copy-done.2 = bf16[2,79,8,128]{3,2,1,0:T(8,128)(2,1)S(1)} copy-done((bf16[2,79,8,128]{3,2,1,0:T(8,128)(2,1)S(1)}, bf16[2,79,8,128]{3,2,1,0:T(8,128)(2,1)}, u32[]{:S(2)}) %copy-start.2) | copy-done | bytes 323608
  27.0 1.3 %copy-done.6 = f32[2528,128]{1,0:T(8,128)S(1)} copy-done((f32[2528,128]{1,0:T(8,128)S(1)}, f32[2528,128]{1,0:T(8,128)}, u32[]{:S(2)}) %copy-start.6) | copy-done | bytes 1294360
  28.4 1.9 %step.3 = (f32[2528,128]{1,0:T(8,128)S(1)}, bf16[316,128]{1,0:T(8,128)(2,1)S(1)}, bf16[316,128]{1,0:T(8,128)(2,1)S(1)}, f32[1,2528]{1,0:T(1,128)S(1)}, f32[1,2528]{1,0:T(1,128)S(1)}, /*index=5*/f32[32,128]{1,0:T(8,128)S(1)}) custom-call(f32[2528,128]{1,0:T(8,128)S(1)} %copy-done.6, bf16[332,128]{1,0:T(8,128)(2,1)S(1)} %collective-permute-done.north.rest_3_, ...), custom_call_target="tpu_custom_call" | custom-call | tf_op jit(solution)/shard_map/step/pallas_call | solution.py:523
  30.3 2.2 %collective-permute-start.4 = (bf16[316,128]{1,0:T(8,128)(2,1)S(1)}, bf16[316,128]{1,0:T(8,128)(2,1)S(1)}, u32[]{:S(2)}, u32[]{:S(2)}) collective-permute-start(bf16[316,128]{1,0:T(8,128)(2,1)S(1)} %get-tuple-element.34), channel_id=1, source_target_pairs={{0,24},{8,0},{16,8},{24,16},{1,25},{9,1},{17,9},{25,17},{2,26},{10... | collective-permute-start | bytes 242696 | tf_op jit(solution)/shard_map/ppermute | solution.py:399
  32.5 0.0 collective-permute-start.5
  32.5 2.5 %collective-permute-start.6 = (f32[1,2528]{1,0:T(1,128)S(1)}, f32[1,2528]{1,0:T(1,128)S(1)}, u32[]{:S(2)}, u32[]{:S(2)}) collective-permute-start(f32[1,2528]{1,0:T(1,128)S(1)} %get-tuple-element.36), channel_id=1, source_target_pairs={{0,7},{1,0},{2,1},{3,2},{4,3},{5,4},{6,5},{7,6},{8,15},{9,8},{10,9... | collective-permute-start | bytes 30344 | tf_op jit(solution)/shard_map/ppermute | solution.py:400
  35.0 0.0 collective-permute-start.7
  35.0 1.4 %collective-permute-done.6.east = f32[1,2528]{1,0:T(1,128)S(1)} collective-permute-done((f32[1,2528]{1,0:T(1,128)S(1)}, f32[1,2528]{1,0:T(1,128)S(1)}, u32[]{:S(2)}, u32[]{:S(2)}) %collective-permute-start.6) | collective-permute-done | bytes 10144 | tf_op jit(solution)/shard_map/ppermute | solution.py:400
  36.4 3.5 %collective-permute-done.7.west = f32[1,2528]{1,0:T(1,128)S(1)} collective-permute-done((f32[1,2528]{1,0:T(1,128)S(1)}, f32[1,2528]{1,0:T(1,128)S(1)}, u32[]{:S(2)}, u32[]{:S(2)}) %collective-permute-start.7) | collective-permute-done | bytes 10144 | tf_op jit(solution)/shard_map/ppermute | solution.py:401
  39.9 0.0 collective-permute-done.4.north
  39.9 0.0 collective-permute-done.5.south
  39.9 2.4 %step.4 = (f32[2528,128]{1,0:T(8,128)S(1)}, bf16[316,128]{1,0:T(8,128)(2,1)}, bf16[316,128]{1,0:T(8,128)(2,1)}, f32[1,2528]{1,0:T(1,128)}, f32[1,2528]{1,0:T(1,128)}, /*index=5*/f32[32,128]{1,0:T(8,128)S(1)}) custom-call(f32[2528,128]{1,0:T(8,128)S(1)} %get-tuple-element.33.mixed, bf16[316,128]{1,0:T(8,128)(2,1)S(1)} %collective-permute-done.4.north, ...), custom_call_target="tpu_custom_call" | custom-call | tf_op jit(solution)/shard_map/step/pallas_call | solution.py:523
  42.4 1.0 %copy-done.7 = f32[2528,128]{1,0:T(8,128)} copy-done((f32[2528,128]{1,0:T(8,128)}, f32[2528,128]{1,0:T(8,128)S(1)}, u32[]{:S(2)}) %copy-start.7) | copy-done | bytes 1294360
  43.4 1.5 %collective-permute-start.8 = (bf16[316,128]{1,0:T(8,128)(2,1)}, bf16[316,128]{1,0:T(8,128)(2,1)}, u32[]{:S(2)}, u32[]{:S(2)}) collective-permute-start(bf16[316,128]{1,0:T(8,128)(2,1)} %get-tuple-element.40), channel_id=1, source_target_pairs={{0,24},{8,0},{16,8},{24,16},{1,25},{9,1},{17,9},{25,17},{2,26},{10... | collective-permute-start | bytes 242696 | tf_op jit(solution)/shard_map/ppermute | solution.py:399
  44.9 0.6 collective-permute-start.9
  45.5 0.0 collective-permute-start.10
  45.5 0.5 collective-permute-start.11
  46.0 0.0 all-to-all-done
  46.0 2.8 %forcing.1.rest_2_ = f32[640,512]{1,0:T(8,128)S(1)} custom-call(bf16[1536,128]{1,0:T(8,128)(2,1)} %bitcast.5.got), custom_call_target="tpu_custom_call" | custom-call | tf_op jit(solution)/shard_map/forcing/pallas_call | solution.py:494
  48.8 0.0 collective-permute-done.10.east
  48.8 1.9 %collective-permute-done.11.west = f32[1,2528]{1,0:T(1,128)} collective-permute-done((f32[1,2528]{1,0:T(1,128)}, f32[1,2528]{1,0:T(1,128)}, u32[]{:S(2)}, u32[]{:S(2)}) %collective-permute-start.11) | collective-permute-done | bytes 10144 | tf_op jit(solution)/shard_map/ppermute | solution.py:401
  50.7 0.0 collective-permute-done.8.north
  50.7 0.0 collective-permute-done.9.south
  50.7 0.0 copy-start.14
  50.7 2.9 %step.5 = (f32[2528,128]{1,0:T(8,128)S(1)}, bf16[368,128]{1,0:T(8,128)(2,1)S(1)}, bf16[368,128]{1,0:T(8,128)(2,1)S(1)}, f32[1,2528]{1,0:T(1,128)S(1)}, f32[1,252...) custom-call(f32[2528,128]{1,0:T(8,128)S(1)} %copy-done.8, bf16[316,128]{1,0:T(8,128)(2,1)} %collective-permute-done.8.north, ...), custom_call_target="tpu_custom_call" | custom-call | tf_op jit(solution)/shard_map/step/pallas_call | solution.py:523
  53.7 2.4 %collective-permute-start.12 = (bf16[368,128]{1,0:T(8,128)(2,1)S(1)}, bf16[368,128]{1,0:T(8,128)(2,1)S(1)}, u32[]{:S(2)}, u32[]{:S(2)}) collective-permute-start(bf16[368,128]{1,0:T(8,128)(2,1)S(1)} %get-tuple-element.47), channel_id=1, source_target_pairs={{0,24},{8,0},{16,8},{24,16},{1,25},{9,1},{17,9},{25,17},{2,26},{10... | collective-permute-start | bytes 282632 | tf_op jit(solution)/shard_map/ppermute | solution.py:399
  56.1 0.0 collective-permute-start.13
  56.1 0.6 collective-permute-start.16
  56.7 3.1 %collective-permute-done.16.rest_3_ = bf16[48,128]{1,0:T(8,128)(2,1)S(1)} collective-permute-done((bf16[48,128]{1,0:T(8,128)(2,1)S(1)}, bf16[48,128]{1,0:T(8,128)(2,1)S(1)}, u32[]{:S(2)}, u32[]{:S(2)}) %collective-permute-start.16) | collective-permute-done | bytes 12320 | tf_op jit(solution)/shard_map/ppermute | solution.py:539
  59.8 0.0 collective-permute-done.12.north.rest_2_
  59.8 1.8 %collective-permute-done.13.south.rest_1_ = bf16[368,128]{1,0:T(8,128)(2,1)S(1)} collective-permute-done((bf16[368,128]{1,0:T(8,128)(2,1)S(1)}, bf16[368,128]{1,0:T(8,128)(2,1)S(1)}, u32[]{:S(2)}, u32[]{:S(2)}) %collective-permute-start.13) | collective-permute-done | bytes 94240 | tf_op jit(solution)/shard_map/ppermute | solution.py:398
  61.6 0.3 lat_smooth.1.own
  61.8 0.0 collective-permute-start.17
  61.8 1.2 %collective-permute-done.17.other = f32[40,128]{1,0:T(8,128)S(1)} collective-permute-done((f32[40,128]{1,0:T(8,128)S(1)}, f32[40,128]{1,0:T(8,128)S(1)}, u32[]{:S(2)}, u32[]{:S(2)}) %collective-permute-start.17) | collective-permute-done | bytes 20512 | tf_op jit(solution)/shard_map/ppermute | solution.py:547
  63.0 0.1 collective-permute-start.20
  63.1 0.1 collective-permute-start.19
  63.2 1.9 %collective-permute-start.18 = (f32[80,128]{1,0:T(8,128)S(1)}, f32[80,128]{1,0:T(8,128)S(1)}, u32[]{:S(2)}, u32[]{:S(2)}) collective-permute-start(f32[80,128]{1,0:T(8,128)S(1)} %pair.1.rest_0_), channel_id=1, source_target_pairs={{0,2},{1,3},{2,4},{3,5},{4,6},{5,7},{6,0},{7,1},{8,10},{9,11},{10,... | collective-permute-start | bytes 122888 | tf_op jit(solution)/shard_map/ppermute | solution.py:554
  65.1 1.5 %collective-permute-start.14 = (f32[1,2528]{1,0:T(1,128)S(1)}, f32[1,2528]{1,0:T(1,128)S(1)}, u32[]{:S(2)}, u32[]{:S(2)}) collective-permute-start(f32[1,2528]{1,0:T(1,128)S(1)} %get-tuple-element.49), channel_id=1, source_target_pairs={{0,7},{1,0},{2,1},{3,2},{4,3},{5,4},{6,5},{7,6},{8,15},{9,8},{10,9... | collective-permute-start | bytes 30344 | tf_op jit(solution)/shard_map/ppermute | solution.py:400
  66.6 0.0 collective-permute-start.15
  66.6 1.4 %collective-permute-done.14.east = f32[1,2528]{1,0:T(1,128)S(1)} collective-permute-done((f32[1,2528]{1,0:T(1,128)S(1)}, f32[1,2528]{1,0:T(1,128)S(1)}, u32[]{:S(2)}, u32[]{:S(2)}) %collective-permute-start.14) | collective-permute-done | bytes 10144 | tf_op jit(solution)/shard_map/ppermute | solution.py:400
  68.0 3.5 %collective-permute-done.15.west = f32[1,2528]{1,0:T(1,128)S(1)} collective-permute-done((f32[1,2528]{1,0:T(1,128)S(1)}, f32[1,2528]{1,0:T(1,128)S(1)}, u32[]{:S(2)}, u32[]{:S(2)}) %collective-permute-start.15) | collective-permute-done | bytes 10144 | tf_op jit(solution)/shard_map/ppermute | solution.py:401
  71.5 2.2 %last.1 = f32[2528,128]{1,0:T(8,128)} custom-call(f32[2528,128]{1,0:T(8,128)S(1)} %get-tuple-element.46.mixed, bf16[368,128]{1,0:T(8,128)(2,1)S(1)} %collective-permute-done.12.north.rest_2_, bf16[368,128]{1,0:T(8,128)(2,1)S(1)} %collective-permute-done.13.south.rest_1_, f32[1,2528]{1,0:T(1,128)S(1)} %collective-permute-done.14.east, ...), custom_call_target="tpu_custom_call" | custom-call | tf_op jit(solution)/shard_map/last/pallas_call | solution.py:556
  73.8 0.0 collective-permute-done.20.rest_3_
  73.8 0.0 collective-permute-done.19.rest_2_
  73.8 0.0 collective-permute-done.18.rest_1_
  73.8 1.1 %lon_smooth.1 = f32[32,128]{1,0:T(8,128)} custom-call(bf16[128,1024]{1,0:T(8,128)(2,1)S(1)} %copy-done.11, f32[80,128]{1,0:T(8,128)S(1)} %pair.1.rest_0_, f32[80,128]{1,0:T(8,128)S(1)} %collective-permute-done.18.rest_1_, f32[80,128]{1,0:T(8,128)S(1)} %collective-permute-done.19.rest_2_, f32[80,128]{1,0:T(8,128)S(1)} %collective-permute-done.20.rest_3_), custom_call_target="tpu_custom_call" | custom-call | tf_op jit(solution)/shard_map/lon_smooth/pallas_call | solution.py:567
  (30 shorter events, 0.1 us)
Async XLA Ops:
  0.6 4.5 %copy-start.12 = (bf16[79,1024]{1,0:T(8,128)(2,1)S(1)}, bf16[79,1024]{1,0:T(8,128)(2,1)}, u32[]{:S(2)}) copy-start(bf16[79,1024]{1,0:T(8,128)(2,1)} %weights.1) | copy-start | bytes 485380
  0.6 4.5 %copy-start.13 = (bf16[4,1024]{1,0:T(4,128)(2,1)S(1)}, bf16[4,1024]{1,0:T(4,128)(2,1)}, u32[]{:S(2)}) copy-start(bf16[4,1024]{1,0:T(4,128)(2,1)} %resid.1) | copy-start | bytes 24580
  0.7 4.5 %copy-start.15 = (s32[1024]{0:T(1024)S(1)}, s32[1024]{0:T(1024)}, u32[]{:S(2)}) copy-start(s32[1024]{0:T(1024)} %param.17) | copy-start | bytes 12292
  0.7 4.5 %copy-start.16 = (s32[128,1]{0,1:T(1,128)S(1)}, s32[128,1]{0,1:T(1,128)}, u32[]{:S(2)}) copy-start(s32[128,1]{0,1:T(1,128)} %param.18) | copy-start | bytes 1540
  0.7 4.5 %copy-start.17 = (s32[128]{0:T(128)S(1)}, s32[128]{0:T(128)}, u32[]{:S(2)}) copy-start(s32[128]{0:T(128)} %param.19) | copy-start | bytes 1540
  0.7 25.4 %copy-start = (bf16[4,4,79,8,128]{4,3,2,1,0:T(8,128)(2,1)S(1)}, bf16[4,4,79,8,128]{4,3,2,1,0:T(8,128)(2,1)}, u32[]{:S(2)}) copy-start(bf16[4,4,79,8,128]{4,3,2,1,0:T(8,128)(2,1)} %fraction.9) | copy-start | bytes 7766020
  5.1 12.7 %copy-start.19 = (f32[1,2688]{1,0:T(1,128)S(1)}, f32[1,2688]{1,0:T(1,128)}, u32[]{:S(2)}) copy-start(f32[1,2688]{1,0:T(1,128)} %get-tuple-element.31) | copy-start | bytes 32260
  5.2 12.7 %copy-start.18 = (f32[1,2688]{1,0:T(1,128)S(1)}, f32[1,2688]{1,0:T(1,128)}, u32[]{:S(2)}) copy-start(f32[1,2688]{1,0:T(1,128)} %get-tuple-element.30) | copy-start | bytes 32260
  5.2 20.9 %copy-start.1 = (bf16[640,640]{1,0:T(8,128)(2,1)S(1)}, bf16[640,640]{1,0:T(8,128)(2,1)}, u32[]{:S(2)}) copy-start(bf16[640,640]{1,0:T(8,128)(2,1)} %get-tuple-element.32.kron) | copy-start | bytes 2457604
  7.0 0.8 %copy-start.5 = (bf16[1536,128]{1,0:T(8,128)(2,1)}, bf16[1536,128]{1,0:T(8,128)(2,1)S(1)}, u32[]{:S(2)}) copy-start(bf16[1536,128]{1,0:T(8,128)(2,1)S(1)} %pack.1) | copy-start | bytes 1179652
  7.8 38.2 %all-to-all-start = ((bf16[32,48,128]{2,1,0:T(8,128)(2,1)}), bf16[32,48,128]{2,1,0:T(8,128)(2,1)}, u32[]{:S(2)}, u32[]{:S(2)}) async-start(bf16[32,48,128]{2,1,0:T(8,128)(2,1)} %bitcast.8), calls=%async_computation | async-start | bytes 786432 | tf_op jit(solution)/shard_map/all_to_all | solution.py:490
  15.2 10.6 %collective-permute-start = (bf16[332,128]{1,0:T(8,128)(2,1)}, bf16[332,128]{1,0:T(8,128)(2,1)S(1)}, u32[]{:S(2)}, u32[]{:S(2)}) collective-permute-start(bf16[332,128]{1,0:T(8,128)(2,1)} %get-tuple-element.28), channel_id=1, source_target_pairs={{0,24},{8,0},{16,8},{24,16},{1,25},{9,1},{17,9},{25,17},{2,26},{10... | collective-permute-start | bytes 254984 | tf_op jit(solution)/shard_map/ppermute | solution.py:399
  17.9 8.2 %collective-permute-start.1 = (bf16[332,128]{1,0:T(8,128)(2,1)}, bf16[332,128]{1,0:T(8,128)(2,1)S(1)}, u32[]{:S(2)}, u32[]{:S(2)}) collective-permute-start(bf16[332,128]{1,0:T(8,128)(2,1)} %get-tuple-element.29), channel_id=1, source_target_pairs={{0,8},{8,16},{16,24},{24,0},{1,9},{9,17},{17,25},{25,1},{2,10},{10... | collective-permute-start | bytes 254984 | tf_op jit(solution)/shard_map/ppermute | solution.py:398
  17.9 7.9 %collective-permute-start.3 = (f32[1,2688]{1,0:T(1,128)S(1)}, f32[1,2688]{1,0:T(1,128)S(1)}, u32[]{:S(2)}, u32[]{:S(2)}) collective-permute-start(f32[1,2688]{1,0:T(1,128)S(1)} %copy-done.19), channel_id=1, source_target_pairs={{0,1},{1,2},{2,3},{3,4},{4,5},{5,6},{6,7},{7,0},{8,9},{9,10},{10,1... | collective-permute-start | bytes 32264 | tf_op jit(solution)/shard_map/ppermute | solution.py:401
  17.9 7.9 %collective-permute-start.2 = (f32[1,2688]{1,0:T(1,128)S(1)}, f32[1,2688]{1,0:T(1,128)S(1)}, u32[]{:S(2)}, u32[]{:S(2)}) collective-permute-start(f32[1,2688]{1,0:T(1,128)S(1)} %copy-done.18), channel_id=1, source_target_pairs={{0,7},{1,0},{2,1},{3,2},{4,3},{5,4},{6,5},{7,6},{8,15},{9,8},{10,9... | collective-permute-start | bytes 32264 | tf_op jit(solution)/shard_map/ppermute | solution.py:400
  26.0 4.2 %copy-start.9 = (bf16[332,128]{1,0:T(8,128)(2,1)}, bf16[332,128]{1,0:T(8,128)(2,1)S(1)}, u32[]{:S(2)}) copy-start(bf16[332,128]{1,0:T(8,128)(2,1)S(1)} %collective-permute-done.1.south.rest_4_) | copy-start | bytes 254980
  26.0 1.0 %copy-start.2 = (bf16[2,79,8,128]{3,2,1,0:T(8,128)(2,1)S(1)}, bf16[2,79,8,128]{3,2,1,0:T(8,128)(2,1)}, u32[]{:S(2)}) copy-start(bf16[2,79,8,128]{3,2,1,0:T(8,128)(2,1)} %profiles.7) | copy-start | bytes 970756
  27.0 1.3 %copy-start.6 = (f32[2528,128]{1,0:T(8,128)S(1)}, f32[2528,128]{1,0:T(8,128)}, u32[]{:S(2)}) copy-start(f32[2528,128]{1,0:T(8,128)} %get-tuple-element.27.mixed) | copy-start | bytes 3883012
  28.4 11.6 %copy-start.3 = (bf16[2,79,8,128]{3,2,1,0:T(8,128)(2,1)S(1)}, bf16[2,79,8,128]{3,2,1,0:T(8,128)(2,1)}, u32[]{:S(2)}) copy-start(bf16[2,79,8,128]{3,2,1,0:T(8,128)(2,1)} %profiles.7) | copy-start | bytes 970756
  30.3 9.7 %collective-permute-start.4 = (bf16[316,128]{1,0:T(8,128)(2,1)S(1)}, bf16[316,128]{1,0:T(8,128)(2,1)S(1)}, u32[]{:S(2)}, u32[]{:S(2)}) collective-permute-start(bf16[316,128]{1,0:T(8,128)(2,1)S(1)} %get-tuple-element.34), channel_id=1, source_target_pairs={{0,24},{8,0},{16,8},{24,16},{1,25},{9,1},{17,9},{25,17},{2,26},{10... | collective-permute-start | bytes 242696 | tf_op jit(solution)/shard_map/ppermute | solution.py:399
  32.5 7.4 %collective-permute-start.5 = (bf16[316,128]{1,0:T(8,128)(2,1)S(1)}, bf16[316,128]{1,0:T(8,128)(2,1)S(1)}, u32[]{:S(2)}, u32[]{:S(2)}) collective-permute-start(bf16[316,128]{1,0:T(8,128)(2,1)S(1)} %get-tuple-element.35), channel_id=1, source_target_pairs={{0,8},{8,16},{16,24},{24,0},{1,9},{9,17},{17,25},{25,1},{2,10},{10... | collective-permute-start | bytes 242696 | tf_op jit(solution)/shard_map/ppermute | solution.py:398
  32.5 3.9 %collective-permute-start.6 = (f32[1,2528]{1,0:T(1,128)S(1)}, f32[1,2528]{1,0:T(1,128)S(1)}, u32[]{:S(2)}, u32[]{:S(2)}) collective-permute-start(f32[1,2528]{1,0:T(1,128)S(1)} %get-tuple-element.36), channel_id=1, source_target_pairs={{0,7},{1,0},{2,1},{3,2},{4,3},{5,4},{6,5},{7,6},{8,15},{9,8},{10,9... | collective-permute-start | bytes 30344 | tf_op jit(solution)/shard_map/ppermute | solution.py:400
  35.0 4.9 %collective-permute-start.7 = (f32[1,2528]{1,0:T(1,128)S(1)}, f32[1,2528]{1,0:T(1,128)S(1)}, u32[]{:S(2)}, u32[]{:S(2)}) collective-permute-start(f32[1,2528]{1,0:T(1,128)S(1)} %get-tuple-element.37), channel_id=1, source_target_pairs={{0,1},{1,2},{2,3},{3,4},{4,5},{5,6},{6,7},{7,0},{8,9},{9,10},{10,1... | collective-permute-start | bytes 30344 | tf_op jit(solution)/shard_map/ppermute | solution.py:401
  42.4 1.1 %copy-start.7 = (f32[2528,128]{1,0:T(8,128)}, f32[2528,128]{1,0:T(8,128)S(1)}, u32[]{:S(2)}) copy-start(f32[2528,128]{1,0:T(8,128)S(1)} %get-tuple-element.39.mixed) | copy-start | bytes 3883012
  43.4 7.2 %collective-permute-start.8 = (bf16[316,128]{1,0:T(8,128)(2,1)}, bf16[316,128]{1,0:T(8,128)(2,1)}, u32[]{:S(2)}, u32[]{:S(2)}) collective-permute-start(bf16[316,128]{1,0:T(8,128)(2,1)} %get-tuple-element.40), channel_id=1, source_target_pairs={{0,24},{8,0},{16,8},{24,16},{1,25},{9,1},{17,9},{25,17},{2,26},{10... | collective-permute-start | bytes 242696 | tf_op jit(solution)/shard_map/ppermute | solution.py:399
  44.9 5.8 %collective-permute-start.9 = (bf16[316,128]{1,0:T(8,128)(2,1)}, bf16[316,128]{1,0:T(8,128)(2,1)}, u32[]{:S(2)}, u32[]{:S(2)}) collective-permute-start(bf16[316,128]{1,0:T(8,128)(2,1)} %get-tuple-element.41), channel_id=1, source_target_pairs={{0,8},{8,16},{16,24},{24,0},{1,9},{9,17},{17,25},{25,1},{2,10},{10... | collective-permute-start | bytes 242696 | tf_op jit(solution)/shard_map/ppermute | solution.py:398
  45.5 3.3 %collective-permute-start.10 = (f32[1,2528]{1,0:T(1,128)}, f32[1,2528]{1,0:T(1,128)S(1)}, u32[]{:S(2)}, u32[]{:S(2)}) collective-permute-start(f32[1,2528]{1,0:T(1,128)} %get-tuple-element.42), channel_id=1, source_target_pairs={{0,7},{1,0},{2,1},{3,2},{4,3},{5,4},{6,5},{7,6},{8,15},{9,8},{10,9... | collective-permute-start | bytes 30344 | tf_op jit(solution)/shard_map/ppermute | solution.py:400
  45.5 5.2 %collective-permute-start.11 = (f32[1,2528]{1,0:T(1,128)}, f32[1,2528]{1,0:T(1,128)}, u32[]{:S(2)}, u32[]{:S(2)}) collective-permute-start(f32[1,2528]{1,0:T(1,128)} %get-tuple-element.43), channel_id=1, source_target_pairs={{0,1},{1,2},{2,3},{3,4},{4,5},{5,6},{6,7},{7,0},{8,9},{9,10},{10,1... | collective-permute-start | bytes 30344 | tf_op jit(solution)/shard_map/ppermute | solution.py:401
  46.0 4.7 %copy-start.4 = (bf16[2,79,8,128]{3,2,1,0:T(8,128)(2,1)S(1)}, bf16[2,79,8,128]{3,2,1,0:T(8,128)(2,1)}, u32[]{:S(2)}) copy-start(bf16[2,79,8,128]{3,2,1,0:T(8,128)(2,1)} %profiles.7) | copy-start | bytes 970756
  46.0 4.7 %copy-start.8 = (f32[2528,128]{1,0:T(8,128)S(1)}, f32[2528,128]{1,0:T(8,128)}, u32[]{:S(2)}) copy-start(f32[2528,128]{1,0:T(8,128)} %copy-done.7) | copy-start | bytes 3883012
  46.0 4.7 %copy-start.10 = (bf16[332,128]{1,0:T(8,128)(2,1)S(1)}, bf16[332,128]{1,0:T(8,128)(2,1)}, u32[]{:S(2)}) copy-start(bf16[332,128]{1,0:T(8,128)(2,1)} %copy-done.9) | copy-start | bytes 254980
  50.7 10.9 %copy-start.14 = (bf16[32,32]{1,0:T(8,128)(2,1)S(1)}, bf16[32,32]{1,0:T(8,128)(2,1)}, u32[]{:S(2)}) copy-start(bf16[32,32]{1,0:T(8,128)(2,1)} %matrix.2) | copy-start | bytes 6148
  53.7 6.1 %collective-permute-start.12 = (bf16[368,128]{1,0:T(8,128)(2,1)S(1)}, bf16[368,128]{1,0:T(8,128)(2,1)S(1)}, u32[]{:S(2)}, u32[]{:S(2)}) collective-permute-start(bf16[368,128]{1,0:T(8,128)(2,1)S(1)} %get-tuple-element.47), channel_id=1, source_target_pairs={{0,24},{8,0},{16,8},{24,16},{1,25},{9,1},{17,9},{25,17},{2,26},{10... | collective-permute-start | bytes 282632 | tf_op jit(solution)/shard_map/ppermute | solution.py:399
  56.1 5.5 %collective-permute-start.13 = (bf16[368,128]{1,0:T(8,128)(2,1)S(1)}, bf16[368,128]{1,0:T(8,128)(2,1)S(1)}, u32[]{:S(2)}, u32[]{:S(2)}) collective-permute-start(bf16[368,128]{1,0:T(8,128)(2,1)S(1)} %get-tuple-element.48), channel_id=1, source_target_pairs={{0,8},{8,16},{16,24},{24,0},{1,9},{9,17},{17,25},{25,1},{2,10},{10... | collective-permute-start | bytes 282632 | tf_op jit(solution)/shard_map/ppermute | solution.py:398
  56.1 3.7 %collective-permute-start.16 = (bf16[48,128]{1,0:T(8,128)(2,1)S(1)}, bf16[48,128]{1,0:T(8,128)(2,1)S(1)}, u32[]{:S(2)}, u32[]{:S(2)}) collective-permute-start(bf16[48,128]{1,0:T(8,128)(2,1)S(1)} %get-tuple-element.51.rest_0_), channel_id=1, source_target_pairs={{0,16},{8,24},{16,0},{24,8},{1,17},{9,25},{17,1},{25,9},{2,18},{10... | collective-permute-start | bytes 36872 | tf_op jit(solution)/shard_map/ppermute | solution.py:539
  61.8 1.2 %collective-permute-start.17 = (f32[40,128]{1,0:T(8,128)S(1)}, f32[40,128]{1,0:T(8,128)S(1)}, u32[]{:S(2)}, u32[]{:S(2)}) collective-permute-start(f32[40,128]{1,0:T(8,128)S(1)} %lat_smooth.1.own), channel_id=1, source_target_pairs={{0,1},{1,0},{2,3},{3,2},{4,5},{5,4},{6,7},{7,6},{8,9},{9,8},{10,11... | collective-permute-start | bytes 61448 | tf_op jit(solution)/shard_map/ppermute | solution.py:547
  63.0 10.7 %collective-permute-start.20 = (f32[80,128]{1,0:T(8,128)S(1)}, f32[80,128]{1,0:T(8,128)S(1)}, u32[]{:S(2)}, u32[]{:S(2)}) collective-permute-start(f32[80,128]{1,0:T(8,128)S(1)} %pair.1.rest_0_), channel_id=1, source_target_pairs={{0,6},{1,7},{2,0},{3,1},{4,2},{5,3},{6,4},{7,5},{8,14},{9,15},{10,... | collective-permute-start | bytes 122888 | tf_op jit(solution)/shard_map/ppermute | solution.py:554
  63.1 10.7 %collective-permute-start.19 = (f32[80,128]{1,0:T(8,128)S(1)}, f32[80,128]{1,0:T(8,128)S(1)}, u32[]{:S(2)}, u32[]{:S(2)}) collective-permute-start(f32[80,128]{1,0:T(8,128)S(1)} %pair.1.rest_0_), channel_id=1, source_target_pairs={{0,4},{1,5},{2,6},{3,7},{4,0},{5,1},{6,2},{7,3},{8,12},{9,13},{10,... | collective-permute-start | bytes 122888 | tf_op jit(solution)/shard_map/ppermute | solution.py:554
  63.2 10.6 %collective-permute-start.18 = (f32[80,128]{1,0:T(8,128)S(1)}, f32[80,128]{1,0:T(8,128)S(1)}, u32[]{:S(2)}, u32[]{:S(2)}) collective-permute-start(f32[80,128]{1,0:T(8,128)S(1)} %pair.1.rest_0_), channel_id=1, source_target_pairs={{0,2},{1,3},{2,4},{3,5},{4,6},{5,7},{6,0},{7,1},{8,10},{9,11},{10,... | collective-permute-start | bytes 122888 | tf_op jit(solution)/shard_map/ppermute | solution.py:554
  65.1 2.9 %collective-permute-start.14 = (f32[1,2528]{1,0:T(1,128)S(1)}, f32[1,2528]{1,0:T(1,128)S(1)}, u32[]{:S(2)}, u32[]{:S(2)}) collective-permute-start(f32[1,2528]{1,0:T(1,128)S(1)} %get-tuple-element.49), channel_id=1, source_target_pairs={{0,7},{1,0},{2,1},{3,2},{4,3},{5,4},{6,5},{7,6},{8,15},{9,8},{10,9... | collective-permute-start | bytes 30344 | tf_op jit(solution)/shard_map/ppermute | solution.py:400
  66.6 4.9 %collective-permute-start.15 = (f32[1,2528]{1,0:T(1,128)S(1)}, f32[1,2528]{1,0:T(1,128)S(1)}, u32[]{:S(2)}, u32[]{:S(2)}) collective-permute-start(f32[1,2528]{1,0:T(1,128)S(1)} %get-tuple-element.50), channel_id=1, source_target_pairs={{0,1},{1,2},{2,3},{3,4},{4,5},{5,6},{6,7},{7,0},{8,9},{9,10},{10,1... | collective-permute-start | bytes 30344 | tf_op jit(solution)/shard_map/ppermute | solution.py:401
  71.5 2.2 %copy-start.11 = (bf16[128,1024]{1,0:T(8,128)(2,1)S(1)}, bf16[128,1024]{1,0:T(8,128)(2,1)}, u32[]{:S(2)}) copy-start(bf16[128,1024]{1,0:T(8,128)(2,1)} %matrix.3) | copy-start | bytes 786436

commit v6 on v5

--- a/solution.py
+++ b/solution.py
@@ -380,13 +380,12 @@
     east = jnp.concatenate([ends[(s + 1) % count][1:2] for s in range(count)], axis=1)
     west = jnp.concatenate([ends[(s - 1) % count][0:1] for s in range(count)], axis=1)
     sides = spread_columns(east, west)
-    total = jnp.zeros(out.shape, F32)
+    blocks, owns = [], []
     for s, part in enumerate(parts):
-        block = (part[0:size, :].astype(F32) + sides[s * size : (s + 1) * size, :]).astype(BF16)
+        blocks.append((part[0:size, :].astype(F32) + sides[s * size : (s + 1) * size, :]).astype(BF16))
         source = lax.rem(lon - s + count, count)
-        own = matrix[:, pl.ds(pl.multiple_of(source * LANES, LANES), LANES)]
-        total = total + dot_nt(block, own)
-    out[...] = total
+        owns.append(matrix[:, pl.ds(pl.multiple_of(source * LANES, LANES), LANES)])
+    out[...] = dot_nt(jnp.concatenate(blocks, axis=1), jnp.concatenate(owns, axis=1))
 
 
 def ring(axis, step):

time: 75.2 us -> 75.1 us (level)
  no operation moved by 1% of the time
where the time goes in v6:
time: 75.1 us; the launch traced here: 74.8 us
  starting transfers between devices  27.6 us (37%)
  waiting for transfers between devices  22.3 us (30%)
  Pallas kernels  19.8 us (26%)
  local copies, waits for them, and re-layouts  4.21 us (6%)
  between operations  0.91 us (1%)
    ppermute x4, waiting for transfers between devices, exchange(): west = lax.ppermute(to_east, 'lon', ring('lon', 1))  13.2 us
    ppermute x4, starting transfers between devices, exchange(): north = lax.ppermute(down, 'lat', ring('lat', -1))  8.77 us
    ppermute x4, starting transfers between devices, exchange(): east = lax.ppermute(to_west, 'lon', ring('lon', -1))  7.6 us
    all_to_all x1, starting transfers between devices, window(): lax.all_to_all(packed.reshape(devices, CAPACITY * slots, LANES), BOTH, sp...  7.44 us
    pallas_call x3, Pallas kernels, window(): pl.pallas_call(functools.partial(step_body, dims, opening, last), grid=(1...  7.29 us
    pallas_call x1, Pallas kernels, window(): pl.pallas_call(functools.partial(first_body, dims), grid=(1,), out_shape=...  4.45 us
    unnamed x40, local copies, waits for them, and re-layouts  4.21 us
    ppermute x1, waiting for transfers between devices, window(): parts.append(lax.ppermute(surface, 'lat', ring('lat', shift)))  3.07 us
  transfers between devices with their start and end apart: 22, of which 10 were waited for; matrix products, arithmetic and copies ran while one was open for 0% of the time, Pallas kernels for 13%

profile of v6, /device:TPU:0, one launch (start us, length us, event | category | flops | bytes accessed | tf_op | source)
XLA Modules:
  0.0 74.8 jit_solution(10946103527678002519)
XLA Ops:
  0.6 0.0 copy-start.12
  0.6 0.0 copy-start.13
  0.7 0.0 copy-start.15
  0.7 0.0 copy-start.16
  0.7 0.0 copy-start.17
  0.7 4.4 %first.1 = (f32[2528,128]{1,0:T(8,128)}, bf16[640,640]{1,0:T(8,128)(2,1)}, bf16[332,128]{1,0:T(8,128)(2,1)}, bf16[332,128]{1,0:T(8,128)(2,1)}, f32[1,2688]{1,0:T(1,128)}, /*index=5*/f32[1,2688]{1,0:T(1,128)}) custom-call(bf16[79,79]{1,0:T(8,128)(2,1)} %kernel.1, bf16[2,79,8,128]{3,2,1,0:T(8,128)(2,1)} %profiles.7, f32[2528,128]{1,0:T(8,128)} %bitcast.12, ...), custom_call_target="tpu_custom_call" | custom-call | tf_op jit(solution)/shard_map/first/pallas_call | solution.py:445
  5.2 0.0 copy-start.18
  5.2 1.7 %pack.1 = bf16[1536,128]{1,0:T(8,128)(2,1)S(1)} custom-call(s32[1,128]{1,0:T(1,128)S(1)} %bitcast.10, s32[1,128]{1,0:T(1,128)S(1)} %bitcast.11, s32[1,1024]{1,0:T(1,128)S(1)} %bitcast.9, bf16[79,1024]{1,0:T(8,128)(2,1)S(1)} %copy-done.12, bf16[4,1024]{1,0:T(4,128)(2,1)S(1)} %copy-done.13), custom_call_target="tpu_custom_call" | custom-call | tf_op jit(solution)/shard_map/pack/pallas_call | solution.py:468
  7.0 0.8 %copy-done.5 = bf16[1536,128]{1,0:T(8,128)(2,1)} copy-done((bf16[1536,128]{1,0:T(8,128)(2,1)}, bf16[1536,128]{1,0:T(8,128)(2,1)S(1)}, u32[]{:S(2)}) %copy-start.5) | copy-done | bytes 393240
  7.8 7.4 %all-to-all-start = ((bf16[32,48,128]{2,1,0:T(8,128)(2,1)}), bf16[32,48,128]{2,1,0:T(8,128)(2,1)}, u32[]{:S(2)}, u32[]{:S(2)}) async-start(bf16[32,48,128]{2,1,0:T(8,128)(2,1)} %bitcast.8), calls=%async_computation | async-start | bytes 786432 | tf_op jit(solution)/shard_map/all_to_all | solution.py:489
  15.2 2.7 %collective-permute-start = (bf16[332,128]{1,0:T(8,128)(2,1)}, bf16[332,128]{1,0:T(8,128)(2,1)S(1)}, u32[]{:S(2)}, u32[]{:S(2)}) collective-permute-start(bf16[332,128]{1,0:T(8,128)(2,1)} %get-tuple-element.28), channel_id=1, source_target_pairs={{0,24},{8,0},{16,8},{24,16},{1,25},{9,1},{17,9},{25,17},{2,26},{10... | collective-permute-start | bytes 254984 | tf_op jit(solution)/shard_map/ppermute | solution.py:398
  17.9 0.0 collective-permute-start.1
  17.9 0.0 collective-permute-start.3
  17.9 3.5 %collective-permute-start.2 = (f32[1,2688]{1,0:T(1,128)S(1)}, f32[1,2688]{1,0:T(1,128)S(1)}, u32[]{:S(2)}, u32[]{:S(2)}) collective-permute-start(f32[1,2688]{1,0:T(1,128)S(1)} %copy-done.18), channel_id=1, source_target_pairs={{0,7},{1,0},{2,1},{3,2},{4,3},{5,4},{6,5},{7,6},{8,15},{9,8},{10,9... | collective-permute-start | bytes 32264 | tf_op jit(solution)/shard_map/ppermute | solution.py:399
  21.4 4.3 %collective-permute-done.3.west.rest_6_ = f32[1,2688]{1,0:T(1,128)S(1)} collective-permute-done((f32[1,2688]{1,0:T(1,128)S(1)}, f32[1,2688]{1,0:T(1,128)S(1)}, u32[]{:S(2)}, u32[]{:S(2)}) %collective-permute-start.3) | collective-permute-done | bytes 10784 | tf_op jit(solution)/shard_map/ppermute | solution.py:400
  25.8 0.0 collective-permute-done.2.east.rest_5_
  25.8 0.0 collective-permute-done.north.rest_3_
  25.8 0.3 collective-permute-done.1.south.rest_4_
  26.0 1.0 %copy-done.2 = bf16[2,79,8,128]{3,2,1,0:T(8,128)(2,1)S(1)} copy-done((bf16[2,79,8,128]{3,2,1,0:T(8,128)(2,1)S(1)}, bf16[2,79,8,128]{3,2,1,0:T(8,128)(2,1)}, u32[]{:S(2)}) %copy-start.2) | copy-done | bytes 323608
  27.0 1.3 %copy-done.6 = f32[2528,128]{1,0:T(8,128)S(1)} copy-done((f32[2528,128]{1,0:T(8,128)S(1)}, f32[2528,128]{1,0:T(8,128)}, u32[]{:S(2)}) %copy-start.6) | copy-done | bytes 1294360
  28.4 1.9 %step.3 = (f32[2528,128]{1,0:T(8,128)S(1)}, bf16[316,128]{1,0:T(8,128)(2,1)S(1)}, bf16[316,128]{1,0:T(8,128)(2,1)S(1)}, f32[1,2528]{1,0:T(1,128)S(1)}, f32[1,2528]{1,0:T(1,128)S(1)}, /*index=5*/f32[32,128]{1,0:T(8,128)S(1)}) custom-call(f32[2528,128]{1,0:T(8,128)S(1)} %copy-done.6, bf16[332,128]{1,0:T(8,128)(2,1)S(1)} %collective-permute-done.north.rest_3_, ...), custom_call_target="tpu_custom_call" | custom-call | tf_op jit(solution)/shard_map/step/pallas_call | solution.py:522
  30.3 2.2 %collective-permute-start.4 = (bf16[316,128]{1,0:T(8,128)(2,1)S(1)}, bf16[316,128]{1,0:T(8,128)(2,1)S(1)}, u32[]{:S(2)}, u32[]{:S(2)}) collective-permute-start(bf16[316,128]{1,0:T(8,128)(2,1)S(1)} %get-tuple-element.34), channel_id=1, source_target_pairs={{0,24},{8,0},{16,8},{24,16},{1,25},{9,1},{17,9},{25,17},{2,26},{10... | collective-permute-start | bytes 242696 | tf_op jit(solution)/shard_map/ppermute | solution.py:398
  32.5 0.0 collective-permute-start.5
  32.5 2.5 %collective-permute-start.6 = (f32[1,2528]{1,0:T(1,128)S(1)}, f32[1,2528]{1,0:T(1,128)S(1)}, u32[]{:S(2)}, u32[]{:S(2)}) collective-permute-start(f32[1,2528]{1,0:T(1,128)S(1)} %get-tuple-element.36), channel_id=1, source_target_pairs={{0,7},{1,0},{2,1},{3,2},{4,3},{5,4},{6,5},{7,6},{8,15},{9,8},{10,9... | collective-permute-start | bytes 30344 | tf_op jit(solution)/shard_map/ppermute | solution.py:399
  35.0 0.0 collective-permute-start.7
  35.0 1.4 %collective-permute-done.6.east = f32[1,2528]{1,0:T(1,128)S(1)} collective-permute-done((f32[1,2528]{1,0:T(1,128)S(1)}, f32[1,2528]{1,0:T(1,128)S(1)}, u32[]{:S(2)}, u32[]{:S(2)}) %collective-permute-start.6) | collective-permute-done | bytes 10144 | tf_op jit(solution)/shard_map/ppermute | solution.py:399
  36.4 3.5 %collective-permute-done.7.west = f32[1,2528]{1,0:T(1,128)S(1)} collective-permute-done((f32[1,2528]{1,0:T(1,128)S(1)}, f32[1,2528]{1,0:T(1,128)S(1)}, u32[]{:S(2)}, u32[]{:S(2)}) %collective-permute-start.7) | collective-permute-done | bytes 10144 | tf_op jit(solution)/shard_map/ppermute | solution.py:400
  39.9 0.0 collective-permute-done.4.north
  39.9 0.0 collective-permute-done.5.south
  39.9 2.4 %step.4 = (f32[2528,128]{1,0:T(8,128)S(1)}, bf16[316,128]{1,0:T(8,128)(2,1)}, bf16[316,128]{1,0:T(8,128)(2,1)}, f32[1,2528]{1,0:T(1,128)}, f32[1,2528]{1,0:T(1,128)}, /*index=5*/f32[32,128]{1,0:T(8,128)S(1)}) custom-call(f32[2528,128]{1,0:T(8,128)S(1)} %get-tuple-element.33.mixed, bf16[316,128]{1,0:T(8,128)(2,1)S(1)} %collective-permute-done.4.north, ...), custom_call_target="tpu_custom_call" | custom-call | tf_op jit(solution)/shard_map/step/pallas_call | solution.py:522
  42.4 1.0 %copy-done.7 = f32[2528,128]{1,0:T(8,128)} copy-done((f32[2528,128]{1,0:T(8,128)}, f32[2528,128]{1,0:T(8,128)S(1)}, u32[]{:S(2)}) %copy-start.7) | copy-done | bytes 1294360
  43.4 1.5 %collective-permute-start.8 = (bf16[316,128]{1,0:T(8,128)(2,1)}, bf16[316,128]{1,0:T(8,128)(2,1)}, u32[]{:S(2)}, u32[]{:S(2)}) collective-permute-start(bf16[316,128]{1,0:T(8,128)(2,1)} %get-tuple-element.40), channel_id=1, source_target_pairs={{0,24},{8,0},{16,8},{24,16},{1,25},{9,1},{17,9},{25,17},{2,26},{10... | collective-permute-start | bytes 242696 | tf_op jit(solution)/shard_map/ppermute | solution.py:398
  44.9 0.6 collective-permute-start.9
  45.5 0.0 collective-permute-start.10
  45.5 0.5 collective-permute-start.11
  46.0 0.0 all-to-all-done
  46.0 2.8 %forcing.1.rest_2_ = f32[640,512]{1,0:T(8,128)S(1)} custom-call(bf16[1536,128]{1,0:T(8,128)(2,1)} %bitcast.5.got), custom_call_target="tpu_custom_call" | custom-call | tf_op jit(solution)/shard_map/forcing/pallas_call | solution.py:493
  48.8 0.0 collective-permute-done.10.east
  48.8 1.9 %collective-permute-done.11.west = f32[1,2528]{1,0:T(1,128)} collective-permute-done((f32[1,2528]{1,0:T(1,128)}, f32[1,2528]{1,0:T(1,128)}, u32[]{:S(2)}, u32[]{:S(2)}) %collective-permute-start.11) | collective-permute-done | bytes 10144 | tf_op jit(solution)/shard_map/ppermute | solution.py:400
  50.7 0.0 collective-permute-done.8.north
  50.7 0.0 collective-permute-done.9.south
  50.7 0.0 copy-start.14
  50.7 2.9 %step.5 = (f32[2528,128]{1,0:T(8,128)S(1)}, bf16[368,128]{1,0:T(8,128)(2,1)S(1)}, bf16[368,128]{1,0:T(8,128)(2,1)S(1)}, f32[1,2528]{1,0:T(1,128)S(1)}, f32[1,252...) custom-call(f32[2528,128]{1,0:T(8,128)S(1)} %copy-done.8, bf16[316,128]{1,0:T(8,128)(2,1)} %collective-permute-done.8.north, ...), custom_call_target="tpu_custom_call" | custom-call | tf_op jit(solution)/shard_map/step/pallas_call | solution.py:522
  53.7 2.4 %collective-permute-start.12 = (bf16[368,128]{1,0:T(8,128)(2,1)S(1)}, bf16[368,128]{1,0:T(8,128)(2,1)S(1)}, u32[]{:S(2)}, u32[]{:S(2)}) collective-permute-start(bf16[368,128]{1,0:T(8,128)(2,1)S(1)} %get-tuple-element.47), channel_id=1, source_target_pairs={{0,24},{8,0},{16,8},{24,16},{1,25},{9,1},{17,9},{25,17},{2,26},{10... | collective-permute-start | bytes 282632 | tf_op jit(solution)/shard_map/ppermute | solution.py:398
  56.1 0.0 collective-permute-start.13
  56.1 0.6 collective-permute-start.16
  56.7 3.1 %collective-permute-done.16.rest_3_ = bf16[48,128]{1,0:T(8,128)(2,1)S(1)} collective-permute-done((bf16[48,128]{1,0:T(8,128)(2,1)S(1)}, bf16[48,128]{1,0:T(8,128)(2,1)S(1)}, u32[]{:S(2)}, u32[]{:S(2)}) %collective-permute-start.16) | collective-permute-done | bytes 12320 | tf_op jit(solution)/shard_map/ppermute | solution.py:538
  59.8 0.0 collective-permute-done.12.north.rest_2_
  59.8 1.8 %collective-permute-done.13.south.rest_1_ = bf16[368,128]{1,0:T(8,128)(2,1)S(1)} collective-permute-done((bf16[368,128]{1,0:T(8,128)(2,1)S(1)}, bf16[368,128]{1,0:T(8,128)(2,1)S(1)}, u32[]{:S(2)}, u32[]{:S(2)}) %collective-permute-start.13) | collective-permute-done | bytes 94240 | tf_op jit(solution)/shard_map/ppermute | solution.py:397
  61.6 0.3 lat_smooth.1.own
  61.8 0.0 collective-permute-start.17
  61.8 1.2 %collective-permute-done.17.other = f32[40,128]{1,0:T(8,128)S(1)} collective-permute-done((f32[40,128]{1,0:T(8,128)S(1)}, f32[40,128]{1,0:T(8,128)S(1)}, u32[]{:S(2)}, u32[]{:S(2)}) %collective-permute-start.17) | collective-permute-done | bytes 20512 | tf_op jit(solution)/shard_map/ppermute | solution.py:546
  63.0 0.1 collective-permute-start.20
  63.1 0.1 collective-permute-start.19
  63.2 1.9 %collective-permute-start.18 = (f32[80,128]{1,0:T(8,128)S(1)}, f32[80,128]{1,0:T(8,128)S(1)}, u32[]{:S(2)}, u32[]{:S(2)}) collective-permute-start(f32[80,128]{1,0:T(8,128)S(1)} %pair.1.rest_0_), channel_id=1, source_target_pairs={{0,2},{1,3},{2,4},{3,5},{4,6},{5,7},{6,0},{7,1},{8,10},{9,11},{10,... | collective-permute-start | bytes 122888 | tf_op jit(solution)/shard_map/ppermute | solution.py:553
  65.1 1.5 %collective-permute-start.14 = (f32[1,2528]{1,0:T(1,128)S(1)}, f32[1,2528]{1,0:T(1,128)S(1)}, u32[]{:S(2)}, u32[]{:S(2)}) collective-permute-start(f32[1,2528]{1,0:T(1,128)S(1)} %get-tuple-element.49), channel_id=1, source_target_pairs={{0,7},{1,0},{2,1},{3,2},{4,3},{5,4},{6,5},{7,6},{8,15},{9,8},{10,9... | collective-permute-start | bytes 30344 | tf_op jit(solution)/shard_map/ppermute | solution.py:399
  66.6 0.0 collective-permute-start.15
  66.6 1.4 %collective-permute-done.14.east = f32[1,2528]{1,0:T(1,128)S(1)} collective-permute-done((f32[1,2528]{1,0:T(1,128)S(1)}, f32[1,2528]{1,0:T(1,128)S(1)}, u32[]{:S(2)}, u32[]{:S(2)}) %collective-permute-start.14) | collective-permute-done | bytes 10144 | tf_op jit(solution)/shard_map/ppermute | solution.py:399
  68.0 3.5 %collective-permute-done.15.west = f32[1,2528]{1,0:T(1,128)S(1)} collective-permute-done((f32[1,2528]{1,0:T(1,128)S(1)}, f32[1,2528]{1,0:T(1,128)S(1)}, u32[]{:S(2)}, u32[]{:S(2)}) %collective-permute-start.15) | collective-permute-done | bytes 10144 | tf_op jit(solution)/shard_map/ppermute | solution.py:400
  71.5 2.2 %last.1 = f32[2528,128]{1,0:T(8,128)} custom-call(f32[2528,128]{1,0:T(8,128)S(1)} %get-tuple-element.46.mixed, bf16[368,128]{1,0:T(8,128)(2,1)S(1)} %collective-permute-done.12.north.rest_2_, bf16[368,128]{1,0:T(8,128)(2,1)S(1)} %collective-permute-done.13.south.rest_1_, f32[1,2528]{1,0:T(1,128)S(1)} %collective-permute-done.14.east, ...), custom_call_target="tpu_custom_call" | custom-call | tf_op jit(solution)/shard_map/last/pallas_call | solution.py:555
  73.8 0.0 collective-permute-done.20.rest_3_
  73.8 0.0 collective-permute-done.19.rest_2_
  73.8 0.0 collective-permute-done.18.rest_1_
  73.8 1.0 %lon_smooth.1 = f32[32,128]{1,0:T(8,128)} custom-call(bf16[128,1024]{1,0:T(8,128)(2,1)S(1)} %copy-done.11, f32[80,128]{1,0:T(8,128)S(1)} %pair.1.rest_0_, f32[80,128]{1,0:T(8,128)S(1)} %collective-permute-done.18.rest_1_, f32[80,128]{1,0:T(8,128)S(1)} %collective-permute-done.19.rest_2_, f32[80,128]{1,0:T(8,128)S(1)} %collective-permute-done.20.rest_3_), custom_call_target="tpu_custom_call" | custom-call | tf_op jit(solution)/shard_map/lon_smooth/pallas_call | solution.py:566
  (30 shorter events, 0.1 us)
Async XLA Ops:
  0.6 4.5 %copy-start.12 = (bf16[79,1024]{1,0:T(8,128)(2,1)S(1)}, bf16[79,1024]{1,0:T(8,128)(2,1)}, u32[]{:S(2)}) copy-start(bf16[79,1024]{1,0:T(8,128)(2,1)} %weights.1) | copy-start | bytes 485380
  0.6 4.5 %copy-start.13 = (bf16[4,1024]{1,0:T(4,128)(2,1)S(1)}, bf16[4,1024]{1,0:T(4,128)(2,1)}, u32[]{:S(2)}) copy-start(bf16[4,1024]{1,0:T(4,128)(2,1)} %resid.1) | copy-start | bytes 24580
  0.7 4.5 %copy-start.15 = (s32[1024]{0:T(1024)S(1)}, s32[1024]{0:T(1024)}, u32[]{:S(2)}) copy-start(s32[1024]{0:T(1024)} %param.17) | copy-start | bytes 12292
  0.7 4.5 %copy-start.16 = (s32[128,1]{0,1:T(1,128)S(1)}, s32[128,1]{0,1:T(1,128)}, u32[]{:S(2)}) copy-start(s32[128,1]{0,1:T(1,128)} %param.18) | copy-start | bytes 1540
  0.7 4.5 %copy-start.17 = (s32[128]{0:T(128)S(1)}, s32[128]{0:T(128)}, u32[]{:S(2)}) copy-start(s32[128]{0:T(128)} %param.19) | copy-start | bytes 1540
  0.7 25.4 %copy-start = (bf16[4,4,79,8,128]{4,3,2,1,0:T(8,128)(2,1)S(1)}, bf16[4,4,79,8,128]{4,3,2,1,0:T(8,128)(2,1)}, u32[]{:S(2)}) copy-start(bf16[4,4,79,8,128]{4,3,2,1,0:T(8,128)(2,1)} %fraction.9) | copy-start | bytes 7766020
  5.1 12.7 %copy-start.19 = (f32[1,2688]{1,0:T(1,128)S(1)}, f32[1,2688]{1,0:T(1,128)}, u32[]{:S(2)}) copy-start(f32[1,2688]{1,0:T(1,128)} %get-tuple-element.31) | copy-start | bytes 32260
  5.2 12.7 %copy-start.18 = (f32[1,2688]{1,0:T(1,128)S(1)}, f32[1,2688]{1,0:T(1,128)}, u32[]{:S(2)}) copy-start(f32[1,2688]{1,0:T(1,128)} %get-tuple-element.30) | copy-start | bytes 32260
  5.2 20.9 %copy-start.1 = (bf16[640,640]{1,0:T(8,128)(2,1)S(1)}, bf16[640,640]{1,0:T(8,128)(2,1)}, u32[]{:S(2)}) copy-start(bf16[640,640]{1,0:T(8,128)(2,1)} %get-tuple-element.32.kron) | copy-start | bytes 2457604
  7.0 0.8 %copy-start.5 = (bf16[1536,128]{1,0:T(8,128)(2,1)}, bf16[1536,128]{1,0:T(8,128)(2,1)S(1)}, u32[]{:S(2)}) copy-start(bf16[1536,128]{1,0:T(8,128)(2,1)S(1)} %pack.1) | copy-start | bytes 1179652
  7.8 38.2 %all-to-all-start = ((bf16[32,48,128]{2,1,0:T(8,128)(2,1)}), bf16[32,48,128]{2,1,0:T(8,128)(2,1)}, u32[]{:S(2)}, u32[]{:S(2)}) async-start(bf16[32,48,128]{2,1,0:T(8,128)(2,1)} %bitcast.8), calls=%async_computation | async-start | bytes 786432 | tf_op jit(solution)/shard_map/all_to_all | solution.py:489
  15.2 10.6 %collective-permute-start = (bf16[332,128]{1,0:T(8,128)(2,1)}, bf16[332,128]{1,0:T(8,128)(2,1)S(1)}, u32[]{:S(2)}, u32[]{:S(2)}) collective-permute-start(bf16[332,128]{1,0:T(8,128)(2,1)} %get-tuple-element.28), channel_id=1, source_target_pairs={{0,24},{8,0},{16,8},{24,16},{1,25},{9,1},{17,9},{25,17},{2,26},{10... | collective-permute-start | bytes 254984 | tf_op jit(solution)/shard_map/ppermute | solution.py:398
  17.9 8.2 %collective-permute-start.1 = (bf16[332,128]{1,0:T(8,128)(2,1)}, bf16[332,128]{1,0:T(8,128)(2,1)S(1)}, u32[]{:S(2)}, u32[]{:S(2)}) collective-permute-start(bf16[332,128]{1,0:T(8,128)(2,1)} %get-tuple-element.29), channel_id=1, source_target_pairs={{0,8},{8,16},{16,24},{24,0},{1,9},{9,17},{17,25},{25,1},{2,10},{10... | collective-permute-start | bytes 254984 | tf_op jit(solution)/shard_map/ppermute | solution.py:397
  17.9 7.9 %collective-permute-start.3 = (f32[1,2688]{1,0:T(1,128)S(1)}, f32[1,2688]{1,0:T(1,128)S(1)}, u32[]{:S(2)}, u32[]{:S(2)}) collective-permute-start(f32[1,2688]{1,0:T(1,128)S(1)} %copy-done.19), channel_id=1, source_target_pairs={{0,1},{1,2},{2,3},{3,4},{4,5},{5,6},{6,7},{7,0},{8,9},{9,10},{10,1... | collective-permute-start | bytes 32264 | tf_op jit(solution)/shard_map/ppermute | solution.py:400
  17.9 7.9 %collective-permute-start.2 = (f32[1,2688]{1,0:T(1,128)S(1)}, f32[1,2688]{1,0:T(1,128)S(1)}, u32[]{:S(2)}, u32[]{:S(2)}) collective-permute-start(f32[1,2688]{1,0:T(1,128)S(1)} %copy-done.18), channel_id=1, source_target_pairs={{0,7},{1,0},{2,1},{3,2},{4,3},{5,4},{6,5},{7,6},{8,15},{9,8},{10,9... | collective-permute-start | bytes 32264 | tf_op jit(solution)/shard_map/ppermute | solution.py:399
  26.0 4.2 %copy-start.9 = (bf16[332,128]{1,0:T(8,128)(2,1)}, bf16[332,128]{1,0:T(8,128)(2,1)S(1)}, u32[]{:S(2)}) copy-start(bf16[332,128]{1,0:T(8,128)(2,1)S(1)} %collective-permute-done.1.south.rest_4_) | copy-start | bytes 254980
  26.0 1.0 %copy-start.2 = (bf16[2,79,8,128]{3,2,1,0:T(8,128)(2,1)S(1)}, bf16[2,79,8,128]{3,2,1,0:T(8,128)(2,1)}, u32[]{:S(2)}) copy-start(bf16[2,79,8,128]{3,2,1,0:T(8,128)(2,1)} %profiles.7) | copy-start | bytes 970756
  27.0 1.3 %copy-start.6 = (f32[2528,128]{1,0:T(8,128)S(1)}, f32[2528,128]{1,0:T(8,128)}, u32[]{:S(2)}) copy-start(f32[2528,128]{1,0:T(8,128)} %get-tuple-element.27.mixed) | copy-start | bytes 3883012
  28.4 11.6 %copy-start.3 = (bf16[2,79,8,128]{3,2,1,0:T(8,128)(2,1)S(1)}, bf16[2,79,8,128]{3,2,1,0:T(8,128)(2,1)}, u32[]{:S(2)}) copy-start(bf16[2,79,8,128]{3,2,1,0:T(8,128)(2,1)} %profiles.7) | copy-start | bytes 970756
  30.3 9.7 %collective-permute-start.4 = (bf16[316,128]{1,0:T(8,128)(2,1)S(1)}, bf16[316,128]{1,0:T(8,128)(2,1)S(1)}, u32[]{:S(2)}, u32[]{:S(2)}) collective-permute-start(bf16[316,128]{1,0:T(8,128)(2,1)S(1)} %get-tuple-element.34), channel_id=1, source_target_pairs={{0,24},{8,0},{16,8},{24,16},{1,25},{9,1},{17,9},{25,17},{2,26},{10... | collective-permute-start | bytes 242696 | tf_op jit(solution)/shard_map/ppermute | solution.py:398
  32.5 7.4 %collective-permute-start.5 = (bf16[316,128]{1,0:T(8,128)(2,1)S(1)}, bf16[316,128]{1,0:T(8,128)(2,1)S(1)}, u32[]{:S(2)}, u32[]{:S(2)}) collective-permute-start(bf16[316,128]{1,0:T(8,128)(2,1)S(1)} %get-tuple-element.35), channel_id=1, source_target_pairs={{0,8},{8,16},{16,24},{24,0},{1,9},{9,17},{17,25},{25,1},{2,10},{10... | collective-permute-start | bytes 242696 | tf_op jit(solution)/shard_map/ppermute | solution.py:397
  32.5 3.9 %collective-permute-start.6 = (f32[1,2528]{1,0:T(1,128)S(1)}, f32[1,2528]{1,0:T(1,128)S(1)}, u32[]{:S(2)}, u32[]{:S(2)}) collective-permute-start(f32[1,2528]{1,0:T(1,128)S(1)} %get-tuple-element.36), channel_id=1, source_target_pairs={{0,7},{1,0},{2,1},{3,2},{4,3},{5,4},{6,5},{7,6},{8,15},{9,8},{10,9... | collective-permute-start | bytes 30344 | tf_op jit(solution)/shard_map/ppermute | solution.py:399
  35.0 4.9 %collective-permute-start.7 = (f32[1,2528]{1,0:T(1,128)S(1)}, f32[1,2528]{1,0:T(1,128)S(1)}, u32[]{:S(2)}, u32[]{:S(2)}) collective-permute-start(f32[1,2528]{1,0:T(1,128)S(1)} %get-tuple-element.37), channel_id=1, source_target_pairs={{0,1},{1,2},{2,3},{3,4},{4,5},{5,6},{6,7},{7,0},{8,9},{9,10},{10,1... | collective-permute-start | bytes 30344 | tf_op jit(solution)/shard_map/ppermute | solution.py:400
  42.4 1.1 %copy-start.7 = (f32[2528,128]{1,0:T(8,128)}, f32[2528,128]{1,0:T(8,128)S(1)}, u32[]{:S(2)}) copy-start(f32[2528,128]{1,0:T(8,128)S(1)} %get-tuple-element.39.mixed) | copy-start | bytes 3883012
  43.4 7.2 %collective-permute-start.8 = (bf16[316,128]{1,0:T(8,128)(2,1)}, bf16[316,128]{1,0:T(8,128)(2,1)}, u32[]{:S(2)}, u32[]{:S(2)}) collective-permute-start(bf16[316,128]{1,0:T(8,128)(2,1)} %get-tuple-element.40), channel_id=1, source_target_pairs={{0,24},{8,0},{16,8},{24,16},{1,25},{9,1},{17,9},{25,17},{2,26},{10... | collective-permute-start | bytes 242696 | tf_op jit(solution)/shard_map/ppermute | solution.py:398
  44.9 5.8 %collective-permute-start.9 = (bf16[316,128]{1,0:T(8,128)(2,1)}, bf16[316,128]{1,0:T(8,128)(2,1)}, u32[]{:S(2)}, u32[]{:S(2)}) collective-permute-start(bf16[316,128]{1,0:T(8,128)(2,1)} %get-tuple-element.41), channel_id=1, source_target_pairs={{0,8},{8,16},{16,24},{24,0},{1,9},{9,17},{17,25},{25,1},{2,10},{10... | collective-permute-start | bytes 242696 | tf_op jit(solution)/shard_map/ppermute | solution.py:397
  45.5 3.3 %collective-permute-start.10 = (f32[1,2528]{1,0:T(1,128)}, f32[1,2528]{1,0:T(1,128)S(1)}, u32[]{:S(2)}, u32[]{:S(2)}) collective-permute-start(f32[1,2528]{1,0:T(1,128)} %get-tuple-element.42), channel_id=1, source_target_pairs={{0,7},{1,0},{2,1},{3,2},{4,3},{5,4},{6,5},{7,6},{8,15},{9,8},{10,9... | collective-permute-start | bytes 30344 | tf_op jit(solution)/shard_map/ppermute | solution.py:399
  45.5 5.2 %collective-permute-start.11 = (f32[1,2528]{1,0:T(1,128)}, f32[1,2528]{1,0:T(1,128)}, u32[]{:S(2)}, u32[]{:S(2)}) collective-permute-start(f32[1,2528]{1,0:T(1,128)} %get-tuple-element.43), channel_id=1, source_target_pairs={{0,1},{1,2},{2,3},{3,4},{4,5},{5,6},{6,7},{7,0},{8,9},{9,10},{10,1... | collective-permute-start | bytes 30344 | tf_op jit(solution)/shard_map/ppermute | solution.py:400
  46.0 4.7 %copy-start.4 = (bf16[2,79,8,128]{3,2,1,0:T(8,128)(2,1)S(1)}, bf16[2,79,8,128]{3,2,1,0:T(8,128)(2,1)}, u32[]{:S(2)}) copy-start(bf16[2,79,8,128]{3,2,1,0:T(8,128)(2,1)} %profiles.7) | copy-start | bytes 970756
  46.0 4.7 %copy-start.8 = (f32[2528,128]{1,0:T(8,128)S(1)}, f32[2528,128]{1,0:T(8,128)}, u32[]{:S(2)}) copy-start(f32[2528,128]{1,0:T(8,128)} %copy-done.7) | copy-start | bytes 3883012
  46.0 4.7 %copy-start.10 = (bf16[332,128]{1,0:T(8,128)(2,1)S(1)}, bf16[332,128]{1,0:T(8,128)(2,1)}, u32[]{:S(2)}) copy-start(bf16[332,128]{1,0:T(8,128)(2,1)} %copy-done.9) | copy-start | bytes 254980
  50.7 10.9 %copy-start.14 = (bf16[32,32]{1,0:T(8,128)(2,1)S(1)}, bf16[32,32]{1,0:T(8,128)(2,1)}, u32[]{:S(2)}) copy-start(bf16[32,32]{1,0:T(8,128)(2,1)} %matrix.2) | copy-start | bytes 6148
  53.7 6.1 %collective-permute-start.12 = (bf16[368,128]{1,0:T(8,128)(2,1)S(1)}, bf16[368,128]{1,0:T(8,128)(2,1)S(1)}, u32[]{:S(2)}, u32[]{:S(2)}) collective-permute-start(bf16[368,128]{1,0:T(8,128)(2,1)S(1)} %get-tuple-element.47), channel_id=1, source_target_pairs={{0,24},{8,0},{16,8},{24,16},{1,25},{9,1},{17,9},{25,17},{2,26},{10... | collective-permute-start | bytes 282632 | tf_op jit(solution)/shard_map/ppermute | solution.py:398
  56.1 5.5 %collective-permute-start.13 = (bf16[368,128]{1,0:T(8,128)(2,1)S(1)}, bf16[368,128]{1,0:T(8,128)(2,1)S(1)}, u32[]{:S(2)}, u32[]{:S(2)}) collective-permute-start(bf16[368,128]{1,0:T(8,128)(2,1)S(1)} %get-tuple-element.48), channel_id=1, source_target_pairs={{0,8},{8,16},{16,24},{24,0},{1,9},{9,17},{17,25},{25,1},{2,10},{10... | collective-permute-start | bytes 282632 | tf_op jit(solution)/shard_map/ppermute | solution.py:397
  56.1 3.7 %collective-permute-start.16 = (bf16[48,128]{1,0:T(8,128)(2,1)S(1)}, bf16[48,128]{1,0:T(8,128)(2,1)S(1)}, u32[]{:S(2)}, u32[]{:S(2)}) collective-permute-start(bf16[48,128]{1,0:T(8,128)(2,1)S(1)} %get-tuple-element.51.rest_0_), channel_id=1, source_target_pairs={{0,16},{8,24},{16,0},{24,8},{1,17},{9,25},{17,1},{25,9},{2,18},{10... | collective-permute-start | bytes 36872 | tf_op jit(solution)/shard_map/ppermute | solution.py:538
  61.8 1.2 %collective-permute-start.17 = (f32[40,128]{1,0:T(8,128)S(1)}, f32[40,128]{1,0:T(8,128)S(1)}, u32[]{:S(2)}, u32[]{:S(2)}) collective-permute-start(f32[40,128]{1,0:T(8,128)S(1)} %lat_smooth.1.own), channel_id=1, source_target_pairs={{0,1},{1,0},{2,3},{3,2},{4,5},{5,4},{6,7},{7,6},{8,9},{9,8},{10,11... | collective-permute-start | bytes 61448 | tf_op jit(solution)/shard_map/ppermute | solution.py:546
  63.0 10.7 %collective-permute-start.20 = (f32[80,128]{1,0:T(8,128)S(1)}, f32[80,128]{1,0:T(8,128)S(1)}, u32[]{:S(2)}, u32[]{:S(2)}) collective-permute-start(f32[80,128]{1,0:T(8,128)S(1)} %pair.1.rest_0_), channel_id=1, source_target_pairs={{0,6},{1,7},{2,0},{3,1},{4,2},{5,3},{6,4},{7,5},{8,14},{9,15},{10,... | collective-permute-start | bytes 122888 | tf_op jit(solution)/shard_map/ppermute | solution.py:553
  63.1 10.7 %collective-permute-start.19 = (f32[80,128]{1,0:T(8,128)S(1)}, f32[80,128]{1,0:T(8,128)S(1)}, u32[]{:S(2)}, u32[]{:S(2)}) collective-permute-start(f32[80,128]{1,0:T(8,128)S(1)} %pair.1.rest_0_), channel_id=1, source_target_pairs={{0,4},{1,5},{2,6},{3,7},{4,0},{5,1},{6,2},{7,3},{8,12},{9,13},{10,... | collective-permute-start | bytes 122888 | tf_op jit(solution)/shard_map/ppermute | solution.py:553
  63.2 10.6 %collective-permute-start.18 = (f32[80,128]{1,0:T(8,128)S(1)}, f32[80,128]{1,0:T(8,128)S(1)}, u32[]{:S(2)}, u32[]{:S(2)}) collective-permute-start(f32[80,128]{1,0:T(8,128)S(1)} %pair.1.rest_0_), channel_id=1, source_target_pairs={{0,2},{1,3},{2,4},{3,5},{4,6},{5,7},{6,0},{7,1},{8,10},{9,11},{10,... | collective-permute-start | bytes 122888 | tf_op jit(solution)/shard_map/ppermute | solution.py:553
  65.1 2.9 %collective-permute-start.14 = (f32[1,2528]{1,0:T(1,128)S(1)}, f32[1,2528]{1,0:T(1,128)S(1)}, u32[]{:S(2)}, u32[]{:S(2)}) collective-permute-start(f32[1,2528]{1,0:T(1,128)S(1)} %get-tuple-element.49), channel_id=1, source_target_pairs={{0,7},{1,0},{2,1},{3,2},{4,3},{5,4},{6,5},{7,6},{8,15},{9,8},{10,9... | collective-permute-start | bytes 30344 | tf_op jit(solution)/shard_map/ppermute | solution.py:399
  66.6 4.9 %collective-permute-start.15 = (f32[1,2528]{1,0:T(1,128)S(1)}, f32[1,2528]{1,0:T(1,128)S(1)}, u32[]{:S(2)}, u32[]{:S(2)}) collective-permute-start(f32[1,2528]{1,0:T(1,128)S(1)} %get-tuple-element.50), channel_id=1, source_target_pairs={{0,1},{1,2},{2,3},{3,4},{4,5},{5,6},{6,7},{7,0},{8,9},{9,10},{10,1... | collective-permute-start | bytes 30344 | tf_op jit(solution)/shard_map/ppermute | solution.py:400
  71.5 2.2 %copy-start.11 = (bf16[128,1024]{1,0:T(8,128)(2,1)S(1)}, bf16[128,1024]{1,0:T(8,128)(2,1)}, u32[]{:S(2)}) copy-start(bf16[128,1024]{1,0:T(8,128)(2,1)} %matrix.3) | copy-start | bytes 786436
